TPU v7x, 32 devices: a whole 2x2x4 slice. The times are simulated.
32 devices in a mesh: dp: 4 (over z), expert: 8 (over y, x, core).
Axes of the slice: x: 2, y: 2, z: 4, core: 2. Of those that a mesh axis runs over, the one named last changes fastest.
Arguments:
- tokens: bfloat16 [2048, 4096], P(('dp', 'expert')), may hold values from -6 to 6
- queries: bfloat16 [2048, 4096], P(('dp', 'expert')), may hold values from -64 to 64
- keys_values: bfloat16 [2048, 2048], P(('dp', 'expert')), may hold values from -4 to 4
- scan_input: bfloat16 [2048, 4096], P(('dp', 'expert')), may hold values from -6 to 6
- state_maps: float32 [2048, 32], P(('dp', 'expert')), may hold values from -1.5 to 1.5
- step_size: float32 [2048, 64], P(('dp', 'expert')), may hold values from 0.05 to 0.5
- step_decay: float32 [2048, 64], P(('dp', 'expert')), may hold values from -1.2 to 0
- block_pool: bfloat16 [256, 16, 2048], P(('dp', 'expert')), may hold values from -5 to 5
- state_pool: float32 [64, 65536], P(('dp', 'expert')), may hold values from -5 to 5
- block_holder: int32 [32, 16], P(('dp', 'expert')), may hold values from 0 to 3, as said below
- block_index: int32 [32, 16], P(('dp', 'expert')), may hold values from 0 to 7
- cached_blocks: int32 [32], P(('dp', 'expert')), may hold values from 1 to 16, as said below
- state_holder: int32 [32], P(('dp', 'expert')), may hold values from 0 to 3
- state_index: int32 [32], P(('dp', 'expert')), may hold values from 0 to 1
- norm_gain: float32 [4096], replicated, may hold values from 0.1 to 1.9
- router_weight: bfloat16 [4096, 8], replicated, may hold values from -0.09375 to 0.09375
- expert_ids: int32 [2048, 2], P(('dp', 'expert')), may hold values from 0 to 7, all different within a row; in each aligned block of 64 rows (0 to 63, 64 to 127, ...) at most 16 rows name the same one
- up_weight: bfloat16 [8, 4096, 7168], P('expert', None, 'dp'), may hold values from -0.09375 to 0.09375
- down_weight: bfloat16 [8, 7168, 4096], P('expert', 'dp'), may hold values from -0.0625 to 0.0625
Outputs:
- layer_out: bfloat16 [2048, 4096], P(('dp', 'expert'))
- final_state: float32 [32, 65536], P(('dp', 'expert'))
Inputs may be any that keep to these rules, and one draw needn't show every extreme that they name: `block_holder`: each row names every holder exactly 4 times over its 16 entries, so at most 4 of a request's cached blocks sit on one holder. `cached_blocks`: some request caches 16 blocks. `expert_ids`: the two experts of a token differ, and each expert is named by exactly 16 rows of one device.
All inputs are finite; a program needn't handle non-finite values.
Results may differ from a plain program's by a relative error of at most 0.0095.
Values may be sent and summed in bfloat16 or wider, within the bound.
No kernel may reach another device: no remote copies, remote signals or barrier semaphores. Data moves between devices by JAX's collectives and lax.ppermute only.
A program may use at most 128 MiB of HBM per device.

v0:
```python
import jax
import jax.numpy as jnp
from jax import lax
from jax.sharding import PartitionSpec as P

HEADS = 32
KV_HEADS = 8
HEAD = 128
SSM_HEADS = 64
SSM_DIM = 64
NSTATE = 16
BLOCK = 16


def attend(queries, keys_values, prefix, cached_count):
    length = queries.shape[0]
    groups = HEADS // KV_HEADS
    past_len = prefix.shape[0] * prefix.shape[1]
    joined = jnp.concatenate([prefix.reshape(past_len, -1), keys_values], 0)
    joined = joined.reshape(past_len + length, 2, KV_HEADS, HEAD)
    key_rows = joined[:, 0]
    values = joined[:, 1]
    grouped = queries.reshape(length, KV_HEADS, groups, HEAD)
    scores = jnp.einsum(
        "tgqd,kgd->gqtk", grouped, key_rows, preferred_element_type=jnp.float32
    ) * HEAD ** (-0.5)
    places = jnp.arange(past_len + length, dtype=jnp.int32)
    tokens_at = jnp.arange(length, dtype=jnp.int32)
    visible = jnp.where(
        places[None, :] < past_len,
        places[None, :] < cached_count * BLOCK,
        places[None, :] - past_len <= tokens_at[:, None],
    )
    scores = jnp.where(visible, scores, -jnp.inf)
    row_max = jnp.max(scores, axis=-1, keepdims=True)
    weights = jnp.exp(scores - row_max)
    weights = (weights / jnp.sum(weights, axis=-1, keepdims=True)).astype(jnp.bfloat16)
    output = jnp.einsum("gqtk,kgd->tgqd", weights, values, preferred_element_type=jnp.float32)
    return output.reshape(length, -1)


def state_block(inputs, state_maps, steps, decays, start_flat):
    length = inputs.shape[0]
    values = inputs.astype(jnp.float32).reshape(length, SSM_HEADS, SSM_DIM)
    entry_maps = state_maps[:, :NSTATE]
    readout = state_maps[:, NSTATE:]
    running = jnp.cumsum(decays, axis=0)
    places = jnp.arange(length, dtype=jnp.int32)
    causal = (places[:, None] >= places[None, :])[:, :, None]
    spread = running[:, None, :] - running[None, :, :]
    fading = jnp.where(causal, jnp.exp(jnp.where(causal, spread, 0.0)), 0.0)
    intersection = jnp.dot(readout, entry_maps.T, precision=lax.Precision.HIGHEST)
    mixing = fading * intersection[:, :, None] * steps[None, :, :]
    output = jnp.einsum("tsh,shp->thp", mixing, values, precision=lax.Precision.HIGHEST)
    start_state = start_flat.reshape(SSM_HEADS, SSM_DIM, NSTATE)
    output = output + jnp.exp(running)[:, :, None] * jnp.einsum(
        "tn,hpn->thp", readout, start_state, precision=lax.Precision.HIGHEST
    )
    last_sum = running[-1]
    weight = jnp.exp(last_sum[None, :] - running) * steps
    final_state = jnp.exp(last_sum)[:, None, None] * start_state + jnp.einsum(
        "sh,shp,sn->hpn", weight, values, entry_maps, precision=lax.Precision.HIGHEST
    )
    return (output.reshape(length, -1), final_state.reshape(-1))


def apply_expert(row_block, up_local, down_local):
    flattened = row_block.reshape(-1, row_block.shape[-1])
    hidden = jax.nn.silu(jnp.dot(flattened, up_local, preferred_element_type=jnp.float32)).astype(
        jnp.bfloat16
    )
    partial_value = jnp.dot(hidden, down_local, preferred_element_type=jnp.float32)
    return partial_value.reshape(row_block.shape)


def local(
    tokens,
    queries,
    keys_values,
    scan_input,
    state_maps,
    step_size,
    step_decay,
    block_pool,
    state_pool,
    block_holder,
    block_index,
    cached_blocks,
    state_holder,
    state_index,
    norm_gain,
    router_weight,
    expert_ids,
    up_weight,
    down_weight,
):
    dp_size = lax.axis_size("dp")
    holders = block_holder[0]
    indices = block_index[0]
    cached_count = cached_blocks[0]
    entries = holders.shape[0]
    places = jnp.arange(entries, dtype=jnp.int32)
    usable = places < cached_count
    peer_ids = jnp.arange(dp_size, dtype=jnp.int32)
    state_owner = state_holder[0]
    state_wanted = jnp.where(peer_ids == state_owner, state_index[0], 0)[:, None]
    pooled = lax.all_gather(block_pool, "dp", axis=0, tiled=True)
    row_ids = jnp.where(usable, holders * block_pool.shape[0] + indices, 0)
    prefix = pooled[row_ids]
    state_asked = lax.all_to_all(state_wanted, "dp", split_axis=0, concat_axis=0, tiled=True)
    sent_states = state_pool[state_asked.reshape(-1)][:, None, :]
    arrived_states = lax.all_to_all(
        sent_states.astype(jnp.bfloat16), "dp", split_axis=0, concat_axis=0, tiled=True
    ).astype(sent_states.dtype)
    start_flat = arrived_states[state_owner, 0]
    attended = attend(queries, keys_values, prefix, cached_count)
    ssm_out, final_state = state_block(scan_input, state_maps, step_size, step_decay, start_flat)
    mixed_rows = (tokens.astype(jnp.float32) + (attended + ssm_out)).astype(jnp.bfloat16)
    mixed_wide = lax.optimization_barrier(mixed_rows).astype(jnp.float32)
    normed = (
        mixed_wide
        * lax.rsqrt(jnp.mean(mixed_wide * mixed_wide, axis=-1, keepdims=True) + 1e-05)
        * norm_gain
    ).astype(jnp.bfloat16)
    logits = jnp.dot(normed, router_weight, preferred_element_type=jnp.float32)
    chosen = jnp.take_along_axis(logits, expert_ids, axis=1)
    lifted = jax.nn.sigmoid(chosen)
    gate_values = lifted / jnp.sum(lifted, axis=1, keepdims=True)
    experts = router_weight.shape[1]
    expert_list = expert_ids.reshape(-1)
    capacity = expert_list.shape[0] // experts
    onehot = (expert_list[:, None] == jnp.arange(experts, dtype=jnp.int32)[None, :]).astype(
        jnp.int32
    )
    before = jnp.cumsum(onehot, axis=0) - onehot
    expert_slot = jnp.sum(before * onehot, axis=1)
    target = expert_list * capacity + expert_slot
    owner_ids = jnp.arange(expert_list.shape[0], dtype=jnp.int32) // 2
    source = jnp.sum(
        jnp.where(
            target[:, None] == jnp.arange(experts * capacity, dtype=jnp.int32)[None, :],
            owner_ids[:, None],
            0,
        ),
        axis=0,
    )
    dispatch = normed[source].reshape(experts, capacity, -1)
    up_local = up_weight[0]
    down_local = down_weight[0]
    outgoing = jnp.broadcast_to(dispatch[None], (dp_size,) + dispatch.shape).reshape(
        (dp_size * experts,) + dispatch.shape[1:]
    )
    partial_value = apply_expert(
        lax.all_to_all(outgoing, ("dp", "expert"), split_axis=0, concat_axis=0, tiled=True),
        up_local,
        down_local,
    ).astype(jnp.bfloat16)
    returned = lax.all_to_all(
        partial_value, ("dp", "expert"), split_axis=0, concat_axis=0, tiled=True
    )
    summed = jnp.sum(
        returned.reshape((dp_size, experts) + returned.shape[1:]).astype(jnp.float32), axis=0
    )
    picked = summed.reshape(experts * capacity, -1)[target]
    combined = jnp.sum(picked.reshape(tokens.shape[0], 2, -1) * gate_values[:, :, None], axis=1)
    layer_out = (mixed_wide + combined).astype(jnp.bfloat16)
    return (layer_out, final_state[None, :])


def solution(mesh):
    placed = (
        P(("dp", "expert"), None),
        P(("dp", "expert"), None),
        P(("dp", "expert"), None),
        P(("dp", "expert"), None),
        P(("dp", "expert"), None),
        P(("dp", "expert"), None),
        P(("dp", "expert"), None),
        P(("dp", "expert"), None, None),
        P(("dp", "expert"), None),
        P(("dp", "expert"), None),
        P(("dp", "expert"), None),
        P(("dp", "expert")),
        P(("dp", "expert")),
        P(("dp", "expert")),
        P(),
        P(),
        P(("dp", "expert"), None),
        P("expert", None, "dp"),
        P("expert", "dp", None),
    )
    return jax.shard_map(
        local,
        mesh=mesh,
        in_specs=placed,
        out_specs=(P(("dp", "expert"), None), P(("dp", "expert"), None)),
        check_vma=False,
    )
```

profile of v0, /device:TPU:0, one launch (start us, length us, event | category | flops | bytes accessed | tf_op | source)
XLA Modules:
  0.0 320.1 jit_solution(16407792395237439972)
XLA Ops:
  7.2 0.7 all-gather.2.cloned.1.call-update
  9.2 0.6 compare_select_fusion
  9.8 6.3 %all-to-all-start = ((s32[4,1,1]{2,1,0:T(1,128)}), s32[4,1,1]{2,1,0:T(1,128)S(1)}, u32[]{:S(2)}, u32[]{:S(2)}) async-start(s32[4,1,1]{2,1,0:T(1,128)} %compare_select_fusion), calls=%async_computation | async-start | bytes 4096 | tf_op jit(solution)/shard_map/all_to_all | solution.py:110
  16.1 0.7 broadcast_multiply_fusion
  16.8 0.8 copy.155
  18.3 0.7 fusion.53
  19.0 0.1 mul.137
  19.2 0.1 reshape.272
  19.4 0.9 reduce_window_sum.22
  20.3 0.2 reduce_window_sum.23
  20.5 0.2 select_reduce_fusion.1
  20.8 0.8 exponential_multiply_fusion
  21.6 0.2 reduce
  21.8 1.1 gather_fusion.1
  22.9 0.5 broadcast.287
  23.4 1.3 reduce.7
  24.8 1.3 reshape.335
  26.1 5.2 %all-to-all-start.1 = ((bf16[4,2,32768]{2,1,0:T(2,128)(2,1)}), bf16[4,2,32768]{2,1,0:T(2,128)(2,1)S(1)}, u32[]{:S(2)}, u32[]{:S(2)}) async-start(bf16[4,2,32768]{2,1,0:T(2,128)(2,1)} %reshape.335), calls=%async_computation.1 | async-start | bytes 1048576 | tf_op jit(solution)/shard_map/all_to_all | solution.py:112
  31.6 0.4 reshape.268
  32.0 1.1 reshape.270
  33.2 0.2 fusion.47
  33.5 4.3 %fusion.12 = f32[64,64,64]{2,1,0:T(8,128)} fusion(f32[64,64]{0,1:T(8,128)S(1)} %copy.148, f32[64,64]{1,0:T(8,128)S(1)} %fusion.47, f32[64,64]{0,1:T(8,128)S(1)} %copy.146, pred[64,64]{1,0:T(8,128)(4,1)S(1)} %iota_compare_fusion.3, bf16[64,64,64]{2,1,0:T(8,128)(2,1)S(1)} %reshape.270), kind=kOutput, calls=%fused_computation.20 | convolution fusion | flops 202637312 | bytes 1626112 | tf_op jit(solution)/shard_map/tsh,shp->thp/dot_general | solution.py:54
  37.8 22.8 %all-to-all-done.1 = bf16[4,2,32768]{2,1,0:T(2,128)(2,1)S(1)} async-done(((bf16[4,2,32768]{2,1,0:T(2,128)(2,1)}), bf16[4,2,32768]{2,1,0:T(2,128)(2,1)S(1)}, u32[]{:S(2)}, u32[]{:S(2)}) %all-to-all-start.1) | async-done | bytes 524320 | tf_op jit(solution)/shard_map/all_to_all | solution.py:112
  60.5 0.5 reshape.336
  61.1 1.0 copy-done.4
  62.0 0.7 dynamic-slice_reduce_fusion
  62.8 0.7 reshape_squeeze.5
  63.5 4.5 %fusion.11 = f32[64,64,64]{2,0,1:T(8,128)S(1)} fusion(f32[64,64,64]{2,1,0:T(8,128)} %fusion.12, bf16[64,64,16]{2,1,0:T(8,128)(2,1)S(1)} %reshape_squeeze.5, f32[64,64]{0,1:T(8,128)S(1)} %copy.150, f32[64,32]{0,1:T(8,128)S(1)} %copy-done.10), kind=kOutput, calls=%fused_computation.18 | convolution fusion | flops 50855936 | bytes 3186688 | tf_op jit(solution)/shard_map/tn,hpn->thp/dot_general | solution.py:56
  68.0 1.2 copy.154
  69.2 1.6 reshape.271
  70.9 2.2 gather_fusion
  73.1 0.2 copy.168
  73.3 0.3 copy_dynamic-update-slice_fusion
  73.7 0.6 fusion.37
  74.3 1.4 fusion.59
  75.6 1.1 fusion.23
  76.8 1.7 copy.145
  78.4 1.6 reshape.269
  80.1 0.1 add_convert_fusion
  80.2 0.2 fusion.25
  80.5 0.4 copy-done.12
  80.8 0.2 fusion.27
  81.0 1.2 gather_fusion.2
  82.2 0.5 broadcast_in_dim.121
  82.7 98.4 %all_to_all.24 = bf16[32,16,4096]{2,1,0:T(8,128)(2,1)S(1)} all-to-all(bf16[32,16,4096]{2,1,0:T(8,128)(2,1)S(1)} %bitcast.113), channel_id=1, replica_groups=mesh['dp'=4,'expert'=8] {'dp','expert'}, dimensions={0} | all-to-all | bytes 8388608 | tf_op jit(solution)/shard_map/all_to_all | solution.py:154
  181.1 12.7 %multiply_convert_fusion = bf16[512,1792]{1,0:T(8,128)(2,1)S(1)} fusion(bf16[512,4096]{1,0:T(8,128)(2,1)S(1)} %bitcast.116, bf16[1,4096,1792]{2,1,0:T(8,128)(2,1)} %param.36), kind=kOutput, calls=%fused_computation.12 | convolution fusion | flops 7520780288 | bytes 20709376 | tf_op jit(solution)/shard_map/dot_general | solution.py:69
  193.8 9.4 %fusion.5 = bf16[32,16,4096]{2,1,0:T(8,128)(2,1)} fusion(bf16[32,16,1792]{2,1,0:T(8,128)(2,1)S(1)} %bitcast.123, bf16[1,1792,4096]{2,1,0:T(8,128)(2,1)S(1)} %bitcast.122), kind=kOutput, calls=%fused_computation.11 | convolution fusion | flops 7518289920 | bytes 20709376 | tf_op jit(solution)/shard_map/dot_general | solution.py:72
  203.2 4.1 %all-to-all-start.3 = ((bf16[32,16,4096]{2,1,0:T(8,128)(2,1)}), bf16[32,16,4096]{2,1,0:T(8,128)(2,1)}, u32[]{:S(2)}, u32[]{:S(2)}) async-start(bf16[32,16,4096]{2,1,0:T(8,128)(2,1)} %fusion.5), calls=%async_computation.3 | async-start | bytes 8388608 | tf_op jit(solution)/shard_map/all_to_all | solution.py:158
  207.4 0.1 reshape.311
  207.6 1.7 convert_reduce_fusion.1
  209.3 0.6 reshape_squeeze.6
  209.9 1.4 copy.160
  211.3 3.7 %fusion.24 = f32[64,64,16]{1,2,0:T(8,128)} fusion(bf16[64,64,64]{2,1,0:T(8,128)(2,1)} %copy-done.3, f32[64,64,16]{1,2,0:T(8,128)} %copy.160, f32[64,16]{0,1:T(8,128)S(1)} %slice-done, f32[64,64]{0,1:T(8,128)S(1)} %copy.161, f32[64]{0:T(128)S(1)} %fusion.57), kind=kOutput, calls=%fused_computation.36 | convolution fusion | flops 50528256 | bytes 1069312 | tf_op jit(solution)/shard_map/sh,shp,sn->hpn/dot_general | solution.py:61
  215.1 1.7 copy.163
  216.8 1.5 broadcast_in_dim_reshape.2
  218.2 0.2 fusion.60
  218.5 1.0 gather_fusion.4
  219.5 0.1 reshape.314
  219.9 81.1 %all-to-all-done.3 = bf16[32,16,4096]{2,1,0:T(8,128)(2,1)} async-done(((bf16[32,16,4096]{2,1,0:T(8,128)(2,1)}), bf16[32,16,4096]{2,1,0:T(8,128)(2,1)}, u32[]{:S(2)}, u32[]{:S(2)}) %all-to-all-start.3) | async-done | bytes 4194336 | tf_op jit(solution)/shard_map/all_to_all | solution.py:158
  300.9 3.1 convert_reduce_fusion
  304.1 2.6 gather_fusion.3
  306.6 2.5 reshape.276
  309.2 3.1 multiply_reduce_fusion
  312.3 0.9 fusion.28
  (70 shorter events, 1.3 us)
Async XLA Ops:
  7.2 14.7 %copy-start = (f32[2,65536]{1,0:T(2,128)S(1)}, f32[2,65536]{1,0:T(2,128)}, u32[]{:S(2)}) copy-start(f32[2,65536]{1,0:T(2,128)} %param.27) | copy-start | bytes 1572868
  7.2 63.7 %all-gather.2.cloned.1.call-start = ((), (), s32[]{:S(2)}) async-start(), calls=%async_computation.4 | async-start | bytes 2621440 | tf_op jit(solution)/shard_map/all_gather | solution.py:107
  9.8 11.8 %all-to-all-start = ((s32[4,1,1]{2,1,0:T(1,128)}), s32[4,1,1]{2,1,0:T(1,128)S(1)}, u32[]{:S(2)}, u32[]{:S(2)}) async-start(s32[4,1,1]{2,1,0:T(1,128)} %compare_select_fusion), calls=%async_computation | async-start | bytes 4096 | tf_op jit(solution)/shard_map/all_to_all | solution.py:110
  22.9 8.5 %copy-start.9 = (f32[64,64]{1,0:T(8,128)S(1)}, f32[64,64]{1,0:T(8,128)}, u32[]{:S(2)}) copy-start(f32[64,64]{1,0:T(8,128)} %param.24) | copy-start | bytes 49156
  22.9 8.7 %copy-start.8 = (bf16[64,2048]{1,0:T(8,128)(2,1)S(1)}, bf16[64,2048]{1,0:T(8,128)(2,1)}, u32[]{:S(2)}) copy-start(bf16[64,2048]{1,0:T(8,128)(2,1)} %param.21) | copy-start | bytes 786436
  22.9 8.7 %copy-start.6 = (bf16[64,4096]{1,0:T(8,128)(2,1)S(1)}, bf16[64,4096]{1,0:T(8,128)(2,1)}, u32[]{:S(2)}) copy-start(bf16[64,4096]{1,0:T(8,128)(2,1)} %param.20) | copy-start | bytes 1572868
  24.8 7.2 %copy-start.5 = (bf16[64,4096]{1,0:T(8,128)(2,1)S(1)}, bf16[64,4096]{1,0:T(8,128)(2,1)}, u32[]{:S(2)}) copy-start(bf16[64,4096]{1,0:T(8,128)(2,1)} %param.22) | copy-start | bytes 1572868
  26.1 7.1 %copy-start.10 = (f32[64,32]{0,1:T(8,128)S(1)}, f32[64,32]{0,1:T(8,128)}, u32[]{:S(2)}) copy-start(f32[64,32]{0,1:T(8,128)} %param.23) | copy-start | bytes 24580
  26.1 34.4 %all-to-all-start.1 = ((bf16[4,2,32768]{2,1,0:T(2,128)(2,1)}), bf16[4,2,32768]{2,1,0:T(2,128)(2,1)S(1)}, u32[]{:S(2)}, u32[]{:S(2)}) async-start(bf16[4,2,32768]{2,1,0:T(2,128)(2,1)} %reshape.335), calls=%async_computation.1 | async-start | bytes 1048576 | tf_op jit(solution)/shard_map/all_to_all | solution.py:112
  33.2 4.6 %copy-start.3 = (bf16[64,64,64]{2,1,0:T(8,128)(2,1)}, bf16[64,64,64]{2,1,0:T(8,128)(2,1)S(1)}, u32[]{:S(2)}) copy-start(bf16[64,64,64]{2,1,0:T(8,128)(2,1)S(1)} %reshape.270) | copy-start | bytes 1572868
  61.1 1.0 copy-start.4
  76.7 3.3 %copy-start.2 = (f32[64,4096]{1,0:T(8,128)S(1)}, f32[64,4096]{1,0:T(8,128)}, u32[]{:S(2)}) copy-start(f32[64,4096]{1,0:T(8,128)} %reshape.271) | copy-start | bytes 3145732
  76.7 3.3 %copy-start.7 = (bf16[64,4096]{1,0:T(8,128)(2,1)S(1)}, bf16[64,4096]{1,0:T(8,128)(2,1)}, u32[]{:S(2)}) copy-start(bf16[64,4096]{1,0:T(8,128)(2,1)} %param.19) | copy-start | bytes 1572868
  80.1 0.7 copy-start.12
  82.7 111.1 %slice-start.1 = ((s8[14680064]{0:T(1024)(128)(4,1)}), s8[4194304]{0:T(1024)(128)(4,1)S(1)}, s32[]{:S(2)}) async-start(s8[14680064]{0:T(1024)(128)(4,1)} %bitcast.121), calls=%async_computation.6 | async-start | bytes 8388608
  181.1 12.7 %slice-start.2 = ((s8[14680064]{0:T(1024)(128)(4,1)}), s8[4194304]{0:T(1024)(128)(4,1)S(1)}, s32[]{:S(2)}) async-start(s8[14680064]{0:T(1024)(128)(4,1)} %bitcast.121), calls=%async_computation.7 | async-start | bytes 8388608
  181.1 12.7 %slice-start.3 = ((s8[14680064]{0:T(1024)(128)(4,1)}), s8[4194304]{0:T(1024)(128)(4,1)S(1)}, s32[]{:S(2)}) async-start(s8[14680064]{0:T(1024)(128)(4,1)} %bitcast.121), calls=%async_computation.8 | async-start | bytes 8388608
  181.1 12.7 %slice-start.4 = ((s8[14680064]{0:T(1024)(128)(4,1)}), s8[2097152]{0:T(1024)(128)(4,1)S(1)}, s32[]{:S(2)}) async-start(s8[14680064]{0:T(1024)(128)(4,1)} %bitcast.121), calls=%async_computation.9 | async-start | bytes 4194304
  203.2 4.1 %copy-start.13 = (s32[64,2]{0,1:T(2,128)S(1)}, s32[64,2]{0,1:T(2,128)}, u32[]{:S(2)}) copy-start(s32[64,2]{0,1:T(2,128)} %param.35) | copy-start | bytes 1540
  203.2 97.7 %all-to-all-start.3 = ((bf16[32,16,4096]{2,1,0:T(8,128)(2,1)}), bf16[32,16,4096]{2,1,0:T(8,128)(2,1)}, u32[]{:S(2)}, u32[]{:S(2)}) async-start(bf16[32,16,4096]{2,1,0:T(8,128)(2,1)} %fusion.5), calls=%async_computation.3 | async-start | bytes 8388608 | tf_op jit(solution)/shard_map/all_to_all | solution.py:158
  209.3 2.0 slice-start
  215.1 3.2 copy-start.11
  306.6 6.6 %copy-start.1 = (f32[2,65536]{1,0:T(2,128)S(1)}, f32[2,65536]{1,0:T(2,128)}, u32[]{:S(2)}) copy-start(f32[2,65536]{1,0:T(2,128)} %param.27) | copy-start | bytes 1572868
Sparse Core Ops, SparseCore 0:
  9.6 59.6 all-gather.1
where the time goes:
time: 321 us; the launch traced here: 320 us
  waiting for transfers between devices  105 us (33%)
  blocking collectives  98.4 us (31%)
  matrix products  36.8 us (11%)
  local copies, waits for them, and re-layouts  31.7 us (10%)
  other arithmetic  16.6 us (5%)
  between operations  16.5 us (5%)
  starting transfers between devices  15.6 us (5%)
    all_to_all x1, blocking collectives, local(): lax.all_to_all(outgoing, ('dp', 'expert'), split_axis=0, concat_axis=0, t...  98.4 us
    all_to_all x1, waiting for transfers between devices, local(): lax.all_to_all(partial_value, ('dp', 'expert'), split_axis=0, concat_axis...  81.1 us
    all_to_all x1, waiting for transfers between devices, local(): lax.all_to_all(sent_states.astype(jnp.bfloat16), 'dp', split_axis=0, conc...  22.8 us
    dot_general x1, matrix products, apply_expert(): jnp.dot(flattened, up_local, preferred_element_type=jnp.float32)  12.7 us
    dot_general x1, matrix products, apply_expert(): jnp.dot(hidden, down_local, preferred_element_type=jnp.float32)  9.35 us
  transfers between devices with their start and end apart: 4, of which 2 were waited for; matrix products, arithmetic and copies ran while one was open for 12% of the time, Pallas kernels for 0%

commit v1 on v0

v1 whole, which is shorter than its diff:
```python
import functools

import jax
import jax.numpy as jnp
from jax import lax
from jax.experimental import pallas as pl
from jax.experimental.pallas import tpu as pltpu
from jax.sharding import PartitionSpec as P

HEADS = 32
KV_HEADS = 8
HEAD = 128
SSM_HEADS = 64
SSM_DIM = 64
NSTATE = 16
BLOCK = 16
LANES = 128
HIGH = lax.Precision.HIGHEST
F32 = jnp.float32
BF16 = jnp.bfloat16
VMEM = pl.BlockSpec(memory_space=pltpu.VMEM)
SMEM = pl.BlockSpec(memory_space=pltpu.SMEM)


def split_rows(value):
    high = value.astype(BF16)
    low = (value - high.astype(F32)).astype(BF16)
    return jnp.concatenate([high, low], 0)


def spread(column_pair, width):
    rows = column_pair.shape[0]
    lane = lax.broadcasted_iota(jnp.int32, (rows, LANES), 1)
    return jnp.where(
        lane < width,
        jnp.broadcast_to(column_pair[:, 0:1], (rows, LANES)),
        jnp.broadcast_to(column_pair[:, 1:2], (rows, LANES)),
    )


def pack_kernel(slot, *refs):
    asked_ref = refs[0]
    blocks = refs[1 : 1 + slot]
    state_ref = refs[1 + slot]
    out_ref = refs[2 + slot]
    for s in range(slot):
        out_ref[0, s * BLOCK : (s + 1) * BLOCK, :] = blocks[s][0]
    base = slot * BLOCK
    width = out_ref.shape[2]
    groups = width // LANES
    rows = state_ref.shape[1] // groups
    for b in range(groups):
        out_ref[0, base : base + rows, b * LANES : (b + 1) * LANES] = state_ref[
            0, b * rows : (b + 1) * rows, :
        ]


def pack(asked, block_pool, states):
    peers = asked.shape[0]
    slot = asked.shape[1] - 1
    width = block_pool.shape[2]
    state_rows = states.shape[1] * LANES // width
    rows = slot * BLOCK + state_rows

    def block_spec(s):
        return pl.BlockSpec((1, BLOCK, width), lambda j, asked_ref: (asked_ref[j, s], 0, 0))

    return pl.pallas_call(
        functools.partial(pack_kernel, slot),
        out_shape=jax.ShapeDtypeStruct((peers, rows, width), BF16),
        grid_spec=pltpu.PrefetchScalarGridSpec(
            num_scalar_prefetch=1,
            grid=(peers,),
            in_specs=[block_spec(s) for s in range(slot)]
            + [pl.BlockSpec((1,) + states.shape[1:], lambda j, asked_ref: (asked_ref[j, slot], 0, 0))],
            out_specs=pl.BlockSpec((1, rows, width), lambda j, asked_ref: (j, 0, 0)),
        ),
        name="pack",
    )(asked, *([block_pool] * slot), states)


def scan_kernel(x_ref, maps_ref, steps_ref, decays_ref, tokens_ref, sum_ref, local_ref, fade_ref, keep_ref):
    length = x_ref.shape[0]
    rows_i = lax.broadcasted_iota(jnp.int32, (length, length), 0)
    cols_i = lax.broadcasted_iota(jnp.int32, (length, length), 1)
    causal = rows_i >= cols_i
    running = jnp.dot(
        causal.astype(F32), decays_ref[...], precision=HIGH, preferred_element_type=F32
    )
    last = running[length - 1 : length, :]
    middle = 0.5 * last
    rise = jnp.exp(running - middle)
    fall = jnp.exp(middle - running) * steps_ref[...]
    half = jnp.exp(middle)
    fade_ref[...] = jnp.exp(running)
    keep_ref[...] = jnp.exp(last)
    entry = maps_ref[:, :NSTATE]
    readout = maps_ref[:, NSTATE:]
    meeting = lax.dot_general(
        readout, entry, (((1,), (1,)), ((), ())), precision=HIGH, preferred_element_type=F32
    )
    meeting = split_rows(jnp.where(causal, meeting, 0.0))
    per = LANES // NSTATE
    tiled = jnp.concatenate([entry] * per, 1)
    tiled_high = tiled.astype(BF16)
    tiled_low = (tiled - tiled_high.astype(F32)).astype(BF16)
    tiled = jnp.concatenate([tiled_high, tiled_low], 1)
    sub = lax.broadcasted_iota(jnp.int32, (LANES, LANES), 0)
    lane = lax.broadcasted_iota(jnp.int32, (LANES, LANES), 1)
    own = (sub % per) == (lane // NSTATE)
    heads_per = LANES // SSM_DIM
    state_rows = LANES // per
    for q in range(x_ref.shape[1] // LANES):
        cols = slice(q * LANES, (q + 1) * LANES)
        pair = slice(q * heads_per, (q + 1) * heads_per)
        drive = (x_ref[:, cols].astype(F32) * spread(fall[:, pair], SSM_DIM)).astype(BF16)
        both = jnp.dot(meeting, drive, preferred_element_type=F32)
        part = both[:length] + both[length:]
        sum_ref[:, cols] = tokens_ref[:, cols].astype(F32) + part * spread(rise[:, pair], SSM_DIM)
        outer = lax.dot_general(
            drive, tiled, (((0,), (0,)), ((), ())), preferred_element_type=F32
        )
        outer = jnp.where(own, outer[:, :LANES] + outer[:, LANES:], 0.0)
        folded = jnp.sum(outer.reshape(state_rows, per, LANES), axis=1)
        upper = lax.broadcasted_iota(jnp.int32, (state_rows, LANES), 0) < state_rows // 2
        scale = jnp.where(
            upper,
            jnp.broadcast_to(half[:, q * heads_per : q * heads_per + 1], (state_rows, LANES)),
            jnp.broadcast_to(half[:, q * heads_per + 1 : q * heads_per + 2], (state_rows, LANES)),
        )
        local_ref[q * state_rows : (q + 1) * state_rows, :] = folded * scale


def scan_local(x, maps, steps, decays, tokens):
    length, width = x.shape
    return pl.pallas_call(
        scan_kernel,
        out_shape=(
            jax.ShapeDtypeStruct((length, width), F32),
            jax.ShapeDtypeStruct((width * NSTATE // LANES, LANES), F32),
            jax.ShapeDtypeStruct(steps.shape, F32),
            jax.ShapeDtypeStruct((1, steps.shape[1]), F32),
        ),
        in_specs=[VMEM] * 5,
        out_specs=(VMEM,) * 4,
        name="scan_local",
    )(x, maps, steps, decays, tokens)


def mix_kernel(
    owner_ref,
    q_ref,
    kv_ref,
    got_ref,
    known_ref,
    sum_ref,
    local_ref,
    fade_ref,
    keep_ref,
    maps_ref,
    gain_ref,
    pick_ref,
    mixed_ref,
    normed_ref,
    send_ref,
    final_ref,
    total_ref,
):
    length, width = q_ref.shape
    peers = got_ref.shape[0]
    groups = HEADS // KV_HEADS
    state_rows = width * NSTATE // kv_ref.shape[1]
    block_rows = got_ref.shape[1] - state_rows
    past = peers * block_rows
    owner = owner_ref[0]
    per = LANES // NSTATE
    fold = LANES // per
    heads_per = LANES // SSM_DIM
    readout = maps_ref[:, NSTATE:]
    readout = split_rows(jnp.concatenate([readout] * per, 1))
    sub = lax.broadcasted_iota(jnp.int32, (fold, per, LANES), 1)
    lane = lax.broadcasted_iota(jnp.int32, (fold, per, LANES), 2)
    own = sub == lane // NSTATE
    fade = fade_ref[...]
    keep = keep_ref[...]
    token = lax.broadcasted_iota(jnp.int32, (length, length), 0)
    other = lax.broadcasted_iota(jnp.int32, (length, length), 1)
    seen = jnp.concatenate(
        [
            jnp.broadcast_to(known_ref[...], (length, past)),
            jnp.where(other <= token, 0.0, -1e30).astype(F32),
        ],
        1,
    )
    seen = jnp.concatenate([seen] * groups, 0)
    half = kv_ref.shape[1] // 2
    squares = jnp.zeros((length, LANES), F32)
    for g in range(KV_HEADS):
        key_cols = slice(g * HEAD, (g + 1) * HEAD)
        value_cols = slice(half + g * HEAD, half + (g + 1) * HEAD)
        keys = jnp.concatenate(
            [got_ref[j, 0:block_rows, key_cols] for j in range(peers)] + [kv_ref[:, key_cols]], 0
        )
        values = jnp.concatenate(
            [got_ref[j, 0:block_rows, value_cols] for j in range(peers)] + [kv_ref[:, value_cols]], 0
        )
        asks = jnp.concatenate(
            [
                q_ref[:, (g * groups + i) * HEAD : (g * groups + i + 1) * HEAD]
                for i in range(groups)
            ],
            0,
        )
        scores = (
            lax.dot_general(asks, keys, (((1,), (1,)), ((), ())), preferred_element_type=F32)
            * HEAD ** (-0.5)
            + seen
        )
        top = jnp.max(scores, axis=1, keepdims=True)
        weights = jnp.exp(scores - top)
        weights = (weights * (1.0 / jnp.sum(weights, axis=1, keepdims=True))).astype(BF16)
        attended = jnp.dot(weights, values, preferred_element_type=F32)
        for i in range(groups):
            q = g * groups + i
            cols = slice(q * LANES, (q + 1) * LANES)
            per_side = state_rows // fold
            rows_at = block_rows + (q % per_side) * fold
            start = got_ref[
                owner, rows_at : rows_at + fold, (q // per_side) * LANES : (q // per_side + 1) * LANES
            ].astype(F32)
            wide = jnp.where(own, jnp.broadcast_to(start[:, None, :], (fold, per, LANES)), 0.0)
            wide = wide.reshape(LANES, LANES).astype(BF16)
            both = lax.dot_general(
                readout, wide, (((1,), (1,)), ((), ())), preferred_element_type=F32
            )
            pair = slice(q * heads_per, (q + 1) * heads_per)
            carried = (both[:length] + both[length:]) * spread(fade[:, pair], SSM_DIM)
            upper = lax.broadcasted_iota(jnp.int32, (fold, LANES), 0) < fold // 2
            scale = jnp.where(
                upper,
                jnp.broadcast_to(keep[:, q * heads_per : q * heads_per + 1], (fold, LANES)),
                jnp.broadcast_to(keep[:, q * heads_per + 1 : q * heads_per + 2], (fold, LANES)),
            )
            final_ref[q * fold : (q + 1) * fold, :] = (
                scale * start + local_ref[q * fold : (q + 1) * fold, :]
            )
            mixed = (sum_ref[:, cols] + attended[i * length : (i + 1) * length] + carried).astype(BF16)
            mixed_ref[:, cols] = mixed
            mixed = mixed.astype(F32)
            total_ref[:, cols] = mixed
            squares = squares + mixed * mixed
    mean = jnp.sum(squares, axis=1, keepdims=True) * (1.0 / width)
    scale = lax.rsqrt(mean + 1e-05)
    step = 4 * LANES
    for q in range(width // step):
        cols = slice(q * step, (q + 1) * step)
        normed = (total_ref[:, cols] * scale * gain_ref[:, cols]).astype(BF16)
        normed_ref[:, cols] = normed
        rows = jnp.dot(pick_ref[...], normed, preferred_element_type=F32).astype(BF16)
        for i in range(send_ref.shape[0]):
            send_ref[i, :, cols] = rows


def mix(owner, queries, keys_values, got, known, sums, local, fade, keep, maps, gain, pick, copies):
    length, width = queries.shape
    return pl.pallas_call(
        mix_kernel,
        out_shape=(
            jax.ShapeDtypeStruct((length, width), BF16),
            jax.ShapeDtypeStruct((length, width), BF16),
            jax.ShapeDtypeStruct((copies, pick.shape[0], width), BF16),
            jax.ShapeDtypeStruct(local.shape, F32),
        ),
        in_specs=[SMEM] + [VMEM] * 11,
        out_specs=(VMEM,) * 4,
        scratch_shapes=[pltpu.VMEM((length, width), F32)],
        name="mix",
    )(owner, queries, keys_values, got, known, sums, local, fade, keep, maps, gain, pick)


def choose_kernel(rows_ref, pick_ref, send_ref):
    step = 4 * LANES
    for q in range(rows_ref.shape[1] // step):
        cols = slice(q * step, (q + 1) * step)
        rows = jnp.dot(pick_ref[...], rows_ref[:, cols], preferred_element_type=F32).astype(BF16)
        for i in range(send_ref.shape[0]):
            send_ref[i, :, cols] = rows


def choose(rows, pick, copies):
    return pl.pallas_call(
        choose_kernel,
        out_shape=jax.ShapeDtypeStruct((copies, pick.shape[0], rows.shape[1]), BF16),
        in_specs=[VMEM] * 2,
        out_specs=VMEM,
        name="choose",
    )(rows, pick)


def combine_kernel(parts_ref, weights_ref, out_ref):
    length = out_ref.shape[0]
    both = jnp.dot(weights_ref[...], parts_ref[...], preferred_element_type=F32)
    out_ref[...] = (both[:length] + both[length:]).astype(out_ref.dtype)


def combine(parts, weights, dtype):
    rows, width = parts.shape
    length = weights.shape[0] // 2
    step = 8 * LANES
    return pl.pallas_call(
        combine_kernel,
        out_shape=jax.ShapeDtypeStruct((length, width), dtype),
        grid=(width // step,),
        in_specs=[
            pl.BlockSpec((rows, step), lambda i: (0, i)),
            pl.BlockSpec(weights.shape, lambda i: (0, 0)),
        ],
        out_specs=pl.BlockSpec((length, step), lambda i: (0, i)),
        name="combine",
    )(parts, weights)


def finish_kernel(parts_ref, weights_ref, mixed_ref, far_ref, out_ref):
    length = out_ref.shape[0]
    both = jnp.dot(weights_ref[...], parts_ref[...], preferred_element_type=F32)
    summed = both[:length] + both[length:] + far_ref[...].astype(F32)
    out_ref[...] = (mixed_ref[...].astype(F32) + summed).astype(out_ref.dtype)


def finish(parts, weights, mixed, far):
    rows, width = parts.shape
    length = weights.shape[0] // 2
    step = 8 * LANES
    narrow = pl.BlockSpec((length, step), lambda i: (0, i))
    return pl.pallas_call(
        finish_kernel,
        out_shape=jax.ShapeDtypeStruct((length, width), BF16),
        grid=(width // step,),
        in_specs=[
            pl.BlockSpec((rows, step), lambda i: (0, i)),
            pl.BlockSpec(weights.shape, lambda i: (0, 0)),
            narrow,
            narrow,
        ],
        out_specs=narrow,
        name="finish",
    )(parts, weights, mixed, far)


def targets(expert_list, experts):
    capacity = expert_list.shape[0] // experts
    onehot = (expert_list[:, None] == jnp.arange(experts, dtype=jnp.int32)[None, :]).astype(F32)
    number = expert_list.shape[0]
    places = jnp.arange(number, dtype=jnp.int32)
    earlier = (places[:, None] > places[None, :]).astype(F32)
    before = jnp.dot(earlier, onehot, preferred_element_type=F32)
    slot = jnp.sum(before * onehot, axis=1).astype(jnp.int32)
    return expert_list * capacity + slot


def one_hots(expert_list, experts):
    target = targets(expert_list, experts).reshape(-1, 2)
    places = jnp.arange(expert_list.shape[0], dtype=jnp.int32)
    return target[:, :, None] == places[None, None, :]


def picker(hot):
    return jnp.any(hot, axis=1).T.astype(BF16)


def gate_weights(rows, router_weight, expert_ids, hot, copies):
    logits = jnp.dot(rows, router_weight, preferred_element_type=F32)
    named = expert_ids[:, :, None] == jnp.arange(router_weight.shape[1], dtype=jnp.int32)
    chosen = jnp.sum(jnp.where(named, logits[:, None, :], 0.0), axis=2)
    lifted = jax.nn.sigmoid(chosen)
    gates = lifted / jnp.sum(lifted, axis=1, keepdims=True)
    weights = jnp.sum(jnp.where(hot, gates[:, :, None], 0.0), axis=1)
    weights = jnp.concatenate([weights] * copies, 1)
    return split_rows(weights)


def apply_expert(rows, up_local, down_local):
    hidden = jax.nn.silu(jnp.dot(rows, up_local, preferred_element_type=F32)).astype(BF16)
    return jnp.dot(hidden, down_local, preferred_element_type=F32).astype(BF16)


def local(
    tokens,
    queries,
    keys_values,
    scan_input,
    state_maps,
    step_size,
    step_decay,
    block_pool,
    state_pool,
    block_holder,
    block_index,
    cached_blocks,
    state_holder,
    state_index,
    norm_gain,
    router_weight,
    expert_ids,
    up_weight,
    down_weight,
):
    peers = lax.axis_size("dp")
    columns = lax.axis_size("expert")
    near = peers // 2
    ring = [(k, (k + near) % peers) for k in range(peers)]
    groups = [
        [(h * near + i) * columns + c for i in range(near) for c in range(columns)]
        for h in range(2)
    ]
    experts = router_weight.shape[1]
    holders = block_holder[0]
    indices = block_index[0]
    entries = holders.shape[0]
    slot = entries // peers

    def swap(rows):
        return lax.all_to_all(
            rows,
            ("dp", "expert"),
            split_axis=0,
            concat_axis=0,
            tiled=True,
            axis_index_groups=groups,
        )

    places = jnp.arange(entries, dtype=jnp.int32)
    same = holders[:, None] == holders[None, :]
    rank = jnp.sum((same & (places[None, :] < places[:, None])).astype(jnp.int32), axis=1)
    seat = holders * slot + rank
    at_seat = seat[None, :] == places[:, None]
    wanted = jnp.sum(jnp.where(at_seat, indices[None, :], 0), axis=1)
    entry = jnp.sum(jnp.where(at_seat, places[None, :], 0), axis=1)
    known = jnp.where(entry < cached_blocks[0], 0.0, -1e30).astype(F32)
    known = jnp.repeat(known, BLOCK)[None, :]
    state_wanted = jnp.broadcast_to(state_index[0], (peers, 1))
    mine = expert_ids.reshape(-1)
    ask = jnp.concatenate(
        [
            wanted.reshape(peers, slot),
            state_wanted,
            jnp.broadcast_to(mine[None], (peers, mine.shape[0])),
        ],
        1,
    )
    asked = lax.all_to_all(ask, "dp", split_axis=0, concat_axis=0, tiled=True)
    partner = (lax.axis_index("dp") + near) % peers
    theirs = lax.dynamic_index_in_dim(asked[:, slot + 1 :], partner, 0, keepdims=False)

    states = state_pool.reshape(state_pool.shape[0], -1, LANES).astype(BF16)
    packed = pack(asked[:, : slot + 1], block_pool, states)
    got = lax.all_to_all(packed, "dp", split_axis=0, concat_axis=0, tiled=True)

    hot = one_hots(mine, experts)
    pick = picker(hot)
    sums, from_inputs, fade, keep = scan_local(
        scan_input, state_maps, step_size, step_decay, tokens
    )
    mixed, normed, send, final_state = mix(
        state_holder,
        queries,
        keys_values,
        got,
        known,
        sums,
        from_inputs,
        fade,
        keep,
        state_maps,
        norm_gain[None, :],
        pick,
        near,
    )
    capacity = mine.shape[0] // experts
    width = tokens.shape[1]
    up_local = up_weight[0]
    down_local = down_weight[0]

    far_rows = lax.ppermute(normed, "dp", ring)
    near_in = swap(send.reshape(near * experts, capacity, width))
    far_hot = one_hots(theirs, experts)
    far_send = choose(far_rows, picker(far_hot), near)
    far_in = swap(far_send.reshape(near * experts, capacity, width))

    near_out = apply_expert(near_in.reshape(-1, width), up_local, down_local)
    far_out = apply_expert(far_in.reshape(-1, width), up_local, down_local)
    near_weights = gate_weights(normed, router_weight, expert_ids, hot, near)
    far_weights = gate_weights(
        far_rows, router_weight, theirs.reshape(expert_ids.shape), far_hot, near
    )
    far_back = swap(far_out.reshape(near_in.shape)).reshape(-1, width)
    far_sum = lax.ppermute(combine(far_back, far_weights, BF16), "dp", ring)
    near_back = swap(near_out.reshape(near_in.shape)).reshape(-1, width)
    layer_out = finish(near_back, near_weights, mixed, far_sum)
    return (layer_out, final_state.reshape(1, -1))


def solution(mesh):
    placed = (
        P(("dp", "expert"), None),
        P(("dp", "expert"), None),
        P(("dp", "expert"), None),
        P(("dp", "expert"), None),
        P(("dp", "expert"), None),
        P(("dp", "expert"), None),
        P(("dp", "expert"), None),
        P(("dp", "expert"), None, None),
        P(("dp", "expert"), None),
        P(("dp", "expert"), None),
        P(("dp", "expert"), None),
        P(("dp", "expert")),
        P(("dp", "expert")),
        P(("dp", "expert")),
        P(),
        P(),
        P(("dp", "expert"), None),
        P("expert", None, "dp"),
        P("expert", "dp", None),
    )
    return jax.shard_map(
        local,
        mesh=mesh,
        in_specs=placed,
        out_specs=(P(("dp", "expert"), None), P(("dp", "expert"), None)),
        check_vma=False,
    )
```

time: 321 us -> 250 us (0.78)
  blocking collectives: 98.4 us -> 31.8 us
  Pallas kernels: 0 us -> 28.3 us
  local copies, waits for them, and re-layouts: 31.7 us -> 12.7 us
  between operations: 16.5 us -> 2.86 us
  other arithmetic: 16.6 us -> 5.45 us
  starting transfers between devices: 15.6 us -> 25.6 us
    all_to_all x1, blocking collectives: 98.4 us -> 31.8 us  [swap(): lax.all_to_all(rows, ('dp', 'expert'), split_axis=0, concat_axis=0, tiled...]
    pallas_call x0 -> x6, Pallas kernels: none -> 28.3 us  [the longest x1 8.43 us: mix(): pl.pallas_call(mix_kernel, out_shape=(jax.ShapeDtypeStruct((length, width...]
    all_to_all x3 -> x5, waiting for transfers between devices: 104 us -> 80.9 us  [the longest x3 50.2 us: swap(): lax.all_to_all(rows, ('dp', 'expert'), split_axis=0, concat_axis=0, tiled...]
    ppermute x0 -> x2, waiting for transfers between devices: none -> 21 us  [the longest x1 21 us: local(): far_rows = lax.ppermute(normed, 'dp', ring)]
    gather x9 -> x0, local copies, waits for them, and re-layouts: 8.48 us -> none  [the longest x1 2.57 us: local(): picked = summed.reshape(experts * capacity, -1)[target]]
    all_to_all x3 -> x5, starting transfers between devices: 15.6 us -> 23.3 us  [the longest x3 13.2 us: swap(): lax.all_to_all(rows, ('dp', 'expert'), split_axis=0, concat_axis=0, tiled...]
    reshape x6 -> x1, local copies, waits for them, and re-layouts: 7.46 us -> 0.08 us  [local(): wanted.reshape(peers, slot)]
    reduce_sum x6 -> x8, other arithmetic: 6.81 us -> 2.01 us  [the longest x1 0.91 us: local(): jnp.sum((same & (places[None, :] < places[:, None])).astype(jnp.int32), a...]
  transfers between devices with their start and end apart: 4 -> 7, of which waited for: 2 -> 6; matrix products, arithmetic and copies ran while one was open for 12% -> 19% of each run, Pallas kernels for 0% -> 3%
where the time goes in v1:
time: 250 us; the launch traced here: 249 us
  waiting for transfers between devices  102 us (41%)
  matrix products  40 us (16%)
  blocking collectives  31.8 us (13%)
  Pallas kernels  28.3 us (11%)
  starting transfers between devices  25.6 us (10%)
  local copies, waits for them, and re-layouts  12.7 us (5%)
  other arithmetic  5.45 us (2%)
  between operations  2.86 us (1%)
    all_to_all x3, waiting for transfers between devices, swap(): lax.all_to_all(rows, ('dp', 'expert'), split_axis=0, concat_axis=0, tiled...  50.2 us
    dot_general x2, matrix products, apply_expert(): return jnp.dot(hidden, down_local, preferred_element_type=F32).astype(BF16)  39.3 us
    all_to_all x1, blocking collectives, swap(): lax.all_to_all(rows, ('dp', 'expert'), split_axis=0, concat_axis=0, tiled...  31.8 us
    all_to_all x1, waiting for transfers between devices, local(): got = lax.all_to_all(packed, 'dp', split_axis=0, concat_axis=0, tiled=True)  27.1 us
    ppermute x1, waiting for transfers between devices, local(): far_rows = lax.ppermute(normed, 'dp', ring)  21 us
    all_to_all x3, starting transfers between devices, swap(): lax.all_to_all(rows, ('dp', 'expert'), split_axis=0, concat_axis=0, tiled...  13.2 us
    pallas_call x1, Pallas kernels, mix(): pl.pallas_call(mix_kernel, out_shape=(jax.ShapeDtypeStruct((length, width...  8.43 us
    unnamed x26, local copies, waits for them, and re-layouts  8.31 us
  transfers between devices with their start and end apart: 7, of which 6 were waited for; matrix products, arithmetic and copies ran while one was open for 19% of the time, Pallas kernels for 3%

profile of v1, /device:TPU:0, one launch (start us, length us, event | category | flops | bytes accessed | tf_op | source)
XLA Modules:
  0.0 248.6 jit_solution(6295886113205128396)
XLA Ops:
  0.6 0.0 copy-start
  1.3 0.9 convert_reduce_fusion
  2.2 0.7 fusion.35
  2.9 0.8 select_reduce_fusion.4
  3.7 0.1 reshape.114
  3.8 0.8 copy.55
  4.5 0.1 reshape.131
  4.7 0.1 pad.9.clone
  4.7 0.1 pad.10.clone
  4.8 0.6 all_to_all.23
  5.4 6.3 %all-to-all-start = ((s32[4,1,133]{2,1,0:T(1,128)}), s32[4,1,133]{2,1,0:T(1,128)S(1)}, u32[]{:S(2)}, u32[]{:S(2)}) async-start(s32[4,1,133]{2,1,0:T(1,128)} %all_to_all.23), calls=%async_computation | async-start | bytes 8192 | tf_op jit(solution)/shard_map/all_to_all | solution.py:451
  11.8 1.2 convert_bitcast_fusion
  13.0 0.7 copy.68
  13.7 3.6 %all-to-all-done = s32[4,1,133]{2,1,0:T(1,128)S(1)} async-done(((s32[4,1,133]{2,1,0:T(1,128)}), s32[4,1,133]{2,1,0:T(1,128)S(1)}, u32[]{:S(2)}, u32[]{:S(2)}) %all-to-all-start) | async-done | bytes 2160 | tf_op jit(solution)/shard_map/all_to_all | solution.py:451
  17.4 0.6 slice.8.refs_0_
  17.9 4.3 %pack.1 = bf16[4,96,2048]{2,1,0:T(8,128)(2,1)} custom-call(s32[4,5]{1,0:T(4,128)} %slice.8.refs_0_, bf16[8,16,2048]{2,1,0:T(8,128)(2,1)} %refs_4_.1, bf16[8,16,2048]{2,1,0:T(8,128)(2,1)} %refs_4_.1, bf16[8,16,2048]{2,1,0:T(8,128)(2,1)} %refs_4_.1, bf16[8,16,2048]{2,1,0:T(8,128)(2,1)} %refs_4_.1, bf16[2,512,128]{2,1,0:T(8,128)(2,1)} %bitcast.68), custom_call_target="tpu_custom_call" | custom-call | tf_op jit(solution)/shard_map/pack/pallas_call | solution.py:68
  22.3 3.7 %all-to-all-start.1 = ((bf16[4,96,2048]{2,1,0:T(8,128)(2,1)}), bf16[4,96,2048]{2,1,0:T(8,128)(2,1)S(1)}, u32[]{:S(2)}, u32[]{:S(2)}) async-start(bf16[4,96,2048]{2,1,0:T(8,128)(2,1)} %pack.1), calls=%async_computation.1 | async-start | bytes 3145728 | tf_op jit(solution)/shard_map/all_to_all | solution.py:457
  27.3 0.1 broadcast_in_dim.109
  27.3 0.6 broadcast_in_dim_reshape.2.known_ref
  28.0 0.7 copy.56.maps_ref
  28.7 0.1 fusion.18
  28.8 0.1 convert_element_type.74
  29.0 0.1 copy.57
  29.1 0.1 fusion.31
  29.2 0.7 copy.58
  29.9 4.8 %scan_local.1 = (f32[64,4096]{1,0:T(8,128)}, f32[512,128]{1,0:T(8,128)}, f32[64,64]{1,0:T(8,128)}, f32[1,64]{1,0:T(1,128)}) custom-call(bf16[64,4096]{1,0:T(8,128)(2,1)} %x_ref.1, f32[64,32]{1,0:T(8,128)} %copy.56.maps_ref, f32[64,64]{1,0:T(8,128)} %steps_ref.1, f32[64,64]{1,0:T(8,128)} %decays_ref.1, bf16[64,4096]{1,0:T(8,128)(2,1)} %tokens_ref.1), custom_call_target="tpu_custom_call" | custom-call | tf_op jit(solution)/shard_map/scan_local/pallas_call | solution.py:136
  34.7 27.1 %all-to-all-done.1.got_ref = bf16[4,96,2048]{2,1,0:T(8,128)(2,1)S(1)} async-done(((bf16[4,96,2048]{2,1,0:T(8,128)(2,1)}), bf16[4,96,2048]{2,1,0:T(8,128)(2,1)S(1)}, u32[]{:S(2)}, u32[]{:S(2)}) %all-to-all-start.1) | async-done | bytes 1572896 | tf_op jit(solution)/shard_map/all_to_all | solution.py:457
  61.7 1.1 copy-done.3
  62.9 8.4 %mix.1 = (bf16[64,4096]{1,0:T(8,128)(2,1)}, bf16[64,4096]{1,0:T(8,128)(2,1)}, bf16[2,128,4096]{2,1,0:T(8,128)(2,1)}, f32[512,128]{1,0:T(8,128)}) custom-call(s32[1]{0:T(128)S(6)} %copy.71.owner_ref, bf16[64,4096]{1,0:T(8,128)(2,1)} %q_ref.1, bf16[64,2048]{1,0:T(8,128)(2,1)} %kv_ref.1, bf16[4,96,2048]{2,1,0:T(8,128)(2,1)} %copy-done.3, ...), custom_call_target="tpu_custom_call" | custom-call | tf_op jit(solution)/shard_map/mix/pallas_call | solution.py:266
  71.3 0.0 collective-permute-start
  71.3 0.1 slice.9
  71.4 0.1 fusion.19
  71.6 0.1 convert_element_type.83
  71.7 0.1 copy.61
  71.8 0.1 squeeze.21
  72.0 0.1 copy.60
  72.0 0.1 fusion.30
  72.2 0.7 copy.62
  72.9 21.0 %collective-permute-done.rows_ref = bf16[64,4096]{1,0:T(8,128)(2,1)S(1)} collective-permute-done((bf16[64,4096]{1,0:T(8,128)(2,1)}, bf16[64,4096]{1,0:T(8,128)(2,1)S(1)}, u32[]{:S(2)}, u32[]{:S(2)}) %collective-permute-start) | collective-permute-done | bytes 524320 | tf_op jit(solution)/shard_map/ppermute | solution.py:484
  93.8 0.8 copy-done.5
  94.7 2.8 %choose.1 = bf16[2,128,4096]{2,1,0:T(8,128)(2,1)} custom-call(bf16[64,4096]{1,0:T(8,128)(2,1)} %copy-done.5, bf16[128,64]{1,0:T(8,128)(2,1)} %bitcast.70), custom_call_target="tpu_custom_call" | custom-call | tf_op jit(solution)/shard_map/choose/pallas_call | solution.py:291
  97.4 31.8 %all_to_all.37 = bf16[16,16,4096]{2,1,0:T(8,128)(2,1)} all-to-all(bf16[16,16,4096]{2,1,0:T(8,128)(2,1)} %bitcast.63), channel_id=1, replica_groups={{0,1,2,3,4,5,6,7,8,9,10,11,12,13,14,15},{16,17,18,19,20,21,22,23,24,25,..., dimensions={0} | all-to-all | bytes 4194304 | tf_op jit(solution)/shard_map/all_to_all | solution.py:423
  129.2 3.9 %all-to-all-start.2 = ((bf16[16,16,4096]{2,1,0:T(8,128)(2,1)}), bf16[16,16,4096]{2,1,0:T(8,128)(2,1)S(1)}, u32[]{:S(2)}, u32[]{:S(2)}) async-start(bf16[16,16,4096]{2,1,0:T(8,128)(2,1)} %bitcast.8), calls=%async_computation.2 | async-start | bytes 4194304 | tf_op jit(solution)/shard_map/all_to_all | solution.py:423
  133.1 19.6 %fusion.11 = bf16[256,4096]{1,0:T(8,128)(2,1)} fusion(bf16[1,1792,4096]{2,1,0:T(8,128)(2,1)} %param.37, bf16[256,4096]{1,0:T(8,128)(2,1)} %bitcast.67, bf16[1,4096,1792]{2,1,0:T(8,128)(2,1)} %param.36), kind=kOutput, calls=%fused_computation.9 | convolution fusion | flops 7519535104 | bytes 33554432 | tf_op jit(solution)/shard_map/dot_general | solution.py:384
  152.7 9.3 %all-to-all-done.2 = bf16[16,16,4096]{2,1,0:T(8,128)(2,1)S(1)} async-done(((bf16[16,16,4096]{2,1,0:T(8,128)(2,1)}), bf16[16,16,4096]{2,1,0:T(8,128)(2,1)S(1)}, u32[]{:S(2)}, u32[]{:S(2)}) %all-to-all-start.2) | async-done | bytes 2097184 | tf_op jit(solution)/shard_map/all_to_all | solution.py:423
  162.0 1.3 copy-done.4
  163.3 4.4 %all-to-all-start.5 = ((bf16[16,16,4096]{2,1,0:T(8,128)(2,1)}), bf16[16,16,4096]{2,1,0:T(8,128)(2,1)S(1)}, u32[]{:S(2)}, u32[]{:S(2)}) async-start(bf16[16,16,4096]{2,1,0:T(8,128)(2,1)} %bitcast.66), calls=%async_computation.5 | async-start | bytes 4194304 | tf_op jit(solution)/shard_map/all_to_all | solution.py:423
  167.7 19.7 %fusion.8 = bf16[256,4096]{1,0:T(8,128)(2,1)} fusion(bf16[1,1792,4096]{2,1,0:T(8,128)(2,1)} %param.37, bf16[256,4096]{1,0:T(8,128)(2,1)} %bitcast.65, bf16[1,4096,1792]{2,1,0:T(8,128)(2,1)} %param.36), kind=kOutput, calls=%fused_computation.8 | convolution fusion | flops 7519535104 | bytes 33554432 | tf_op jit(solution)/shard_map/dot_general | solution.py:384
  187.4 9.4 %all-to-all-done.5 = bf16[16,16,4096]{2,1,0:T(8,128)(2,1)S(1)} async-done(((bf16[16,16,4096]{2,1,0:T(8,128)(2,1)}), bf16[16,16,4096]{2,1,0:T(8,128)(2,1)S(1)}, u32[]{:S(2)}, u32[]{:S(2)}) %all-to-all-start.5) | async-done | bytes 2097184 | tf_op jit(solution)/shard_map/all_to_all | solution.py:423
  196.8 1.3 copy-done.2
  198.1 4.9 %all-to-all-start.3 = ((bf16[16,16,4096]{2,1,0:T(8,128)(2,1)}), bf16[16,16,4096]{2,1,0:T(8,128)(2,1)S(1)}, u32[]{:S(2)}, u32[]{:S(2)}) async-start(bf16[16,16,4096]{2,1,0:T(8,128)(2,1)} %bitcast.64), calls=%async_computation.3 | async-start | bytes 4194304 | tf_op jit(solution)/shard_map/all_to_all | solution.py:423
  203.0 0.2 fusion.40
  203.3 0.2 fusion.41
  203.6 0.1 select_reduce_fusion
  203.8 0.6 pad_maximum_fusion.3.weights_ref
  204.4 3.9 %combine.1 = bf16[64,4096]{1,0:T(8,128)(2,1)} custom-call(bf16[256,4096]{1,0:T(8,128)(2,1)} %bitcast.62, bf16[128,256]{1,0:T(8,128)(2,1)} %pad_maximum_fusion.3.weights_ref), custom_call_target="tpu_custom_call" | custom-call | tf_op jit(solution)/shard_map/combine/pallas_call | solution.py:310
  208.3 2.3 collective-permute-start.1
  210.7 0.1 select_reduce_fusion.1
  210.8 0.6 pad_maximum_fusion.1.weights_ref
  211.4 31.5 %all-to-all-done.3 = bf16[16,16,4096]{2,1,0:T(8,128)(2,1)S(1)} async-done(((bf16[16,16,4096]{2,1,0:T(8,128)(2,1)}), bf16[16,16,4096]{2,1,0:T(8,128)(2,1)S(1)}, u32[]{:S(2)}, u32[]{:S(2)}) %all-to-all-start.3) | async-done | bytes 2097184 | tf_op jit(solution)/shard_map/all_to_all | solution.py:423
  243.0 0.0 collective-permute-done.1.far_ref
  243.0 1.3 copy-done.1
  244.3 0.2 copy-done.7
  244.5 4.1 %finish.1 = bf16[64,4096]{1,0:T(8,128)(2,1)} custom-call(bf16[256,4096]{1,0:T(8,128)(2,1)} %bitcast.61, bf16[128,256]{1,0:T(8,128)(2,1)} %pad_maximum_fusion.1.weights_ref, bf16[64,4096]{1,0:T(8,128)(2,1)} %get-tuple-element.16.mixed_ref, bf16[64,4096]{1,0:T(8,128)(2,1)} %copy-done.7), custom_call_target="tpu_custom_call" | custom-call | tf_op jit(solution)/shard_map/finish/pallas_call | solution.py:335
  (35 shorter events, 0.2 us)
Async XLA Ops:
  0.6 202.4 %copy-start = (bf16[4096,8]{0,1:T(8,128)(2,1)S(1)}, bf16[4096,8]{0,1:T(8,128)(2,1)}, u32[]{:S(2)}) copy-start(bf16[4096,8]{0,1:T(8,128)(2,1)} %param.34) | copy-start | bytes 196612
  5.4 11.9 %all-to-all-start = ((s32[4,1,133]{2,1,0:T(1,128)}), s32[4,1,133]{2,1,0:T(1,128)S(1)}, u32[]{:S(2)}, u32[]{:S(2)}) async-start(s32[4,1,133]{2,1,0:T(1,128)} %all_to_all.23), calls=%async_computation | async-start | bytes 8192 | tf_op jit(solution)/shard_map/all_to_all | solution.py:451
  22.3 5.7 %copy-start.9 = (f32[64,32]{0,1:T(8,128)S(1)}, f32[64,32]{0,1:T(8,128)}, u32[]{:S(2)}) copy-start(f32[64,32]{0,1:T(8,128)} %param.23) | copy-start | bytes 24580
  22.3 6.8 %copy-start.10 = (s32[64,2]{0,1:T(2,128)S(1)}, s32[64,2]{0,1:T(2,128)}, u32[]{:S(2)}) copy-start(s32[64,2]{0,1:T(2,128)} %param.35) | copy-start | bytes 1540
  22.3 39.5 %all-to-all-start.1 = ((bf16[4,96,2048]{2,1,0:T(8,128)(2,1)}), bf16[4,96,2048]{2,1,0:T(8,128)(2,1)S(1)}, u32[]{:S(2)}, u32[]{:S(2)}) async-start(bf16[4,96,2048]{2,1,0:T(8,128)(2,1)} %pack.1), calls=%async_computation.1 | async-start | bytes 3145728 | tf_op jit(solution)/shard_map/all_to_all | solution.py:457
  61.7 1.1 copy-start.3
  71.3 22.5 %collective-permute-start = (bf16[64,4096]{1,0:T(8,128)(2,1)}, bf16[64,4096]{1,0:T(8,128)(2,1)S(1)}, u32[]{:S(2)}, u32[]{:S(2)}) collective-permute-start(bf16[64,4096]{1,0:T(8,128)(2,1)} %get-tuple-element.15), channel_id=1, source_target_pairs={{0,16},{8,24},{16,0},{24,8},{1,17},{9,25},{17,1},{25,9},{2,18},{10... | collective-permute-start | bytes 1572872 | tf_op jit(solution)/shard_map/ppermute | solution.py:484
  93.8 0.8 copy-start.5
  129.2 32.8 %all-to-all-start.2 = ((bf16[16,16,4096]{2,1,0:T(8,128)(2,1)}), bf16[16,16,4096]{2,1,0:T(8,128)(2,1)S(1)}, u32[]{:S(2)}, u32[]{:S(2)}) async-start(bf16[16,16,4096]{2,1,0:T(8,128)(2,1)} %bitcast.8), calls=%async_computation.2 | async-start | bytes 4194304 | tf_op jit(solution)/shard_map/all_to_all | solution.py:423
  162.0 1.3 copy-start.4
  163.3 33.5 %all-to-all-start.5 = ((bf16[16,16,4096]{2,1,0:T(8,128)(2,1)}), bf16[16,16,4096]{2,1,0:T(8,128)(2,1)S(1)}, u32[]{:S(2)}, u32[]{:S(2)}) async-start(bf16[16,16,4096]{2,1,0:T(8,128)(2,1)} %bitcast.66), calls=%async_computation.5 | async-start | bytes 4194304 | tf_op jit(solution)/shard_map/all_to_all | solution.py:423
  196.8 1.3 copy-start.2
  196.8 6.2 %copy-start.8 = (bf16[64,4096]{1,0:T(8,128)(2,1)S(1)}, bf16[64,4096]{1,0:T(8,128)(2,1)}, u32[]{:S(2)}) copy-start(bf16[64,4096]{1,0:T(8,128)(2,1)} %get-tuple-element.15) | copy-start | bytes 1572868
  196.8 6.5 %copy-start.6 = (bf16[64,4096]{1,0:T(8,128)(2,1)S(1)}, bf16[64,4096]{1,0:T(8,128)(2,1)}, u32[]{:S(2)}) copy-start(bf16[64,4096]{1,0:T(8,128)(2,1)} %copy-done.5) | copy-start | bytes 1572868
  198.1 44.9 %all-to-all-start.3 = ((bf16[16,16,4096]{2,1,0:T(8,128)(2,1)}), bf16[16,16,4096]{2,1,0:T(8,128)(2,1)S(1)}, u32[]{:S(2)}, u32[]{:S(2)}) async-start(bf16[16,16,4096]{2,1,0:T(8,128)(2,1)} %bitcast.64), calls=%async_computation.3 | async-start | bytes 4194304 | tf_op jit(solution)/shard_map/all_to_all | solution.py:423
  208.3 34.6 %collective-permute-start.1 = (bf16[64,4096]{1,0:T(8,128)(2,1)}, bf16[64,4096]{1,0:T(8,128)(2,1)S(1)}, u32[]{:S(2)}, u32[]{:S(2)}) collective-permute-start(bf16[64,4096]{1,0:T(8,128)(2,1)} %combine.1), channel_id=1, source_target_pairs={{0,16},{8,24},{16,0},{24,8},{1,17},{9,25},{17,1},{25,9},{2,18},{10... | collective-permute-start | bytes 1572872 | tf_op jit(solution)/shard_map/ppermute | solution.py:497
  243.0 1.4 copy-start.1
  243.0 1.5 copy-start.7

commit v2 on v1

--- a/solution.py
+++ b/solution.py
@@ -7,10 +7,10 @@
 from jax.experimental.pallas import tpu as pltpu
 from jax.sharding import PartitionSpec as P
 
+
 HEADS = 32
 KV_HEADS = 8
 HEAD = 128
-SSM_HEADS = 64
 SSM_DIM = 64
 NSTATE = 16
 BLOCK = 16
@@ -39,7 +39,6 @@
 
 
 def pack_kernel(slot, *refs):
-    asked_ref = refs[0]
     blocks = refs[1 : 1 + slot]
     state_ref = refs[1 + slot]
     out_ref = refs[2 + slot]
@@ -256,19 +255,19 @@
         cols = slice(q * step, (q + 1) * step)
         normed = (total_ref[:, cols] * scale * gain_ref[:, cols]).astype(BF16)
         normed_ref[:, cols] = normed
-        rows = jnp.dot(pick_ref[...], normed, preferred_element_type=F32).astype(BF16)
-        for i in range(send_ref.shape[0]):
-            send_ref[i, :, cols] = rows
-
-
-def mix(owner, queries, keys_values, got, known, sums, local, fade, keep, maps, gain, pick, copies):
+        send_ref[:, cols] = jnp.dot(
+            pick_ref[...], normed, preferred_element_type=F32
+        ).astype(BF16)
+
+
+def mix(owner, queries, keys_values, got, known, sums, local, fade, keep, maps, gain, pick):
     length, width = queries.shape
     return pl.pallas_call(
         mix_kernel,
         out_shape=(
             jax.ShapeDtypeStruct((length, width), BF16),
             jax.ShapeDtypeStruct((length, width), BF16),
-            jax.ShapeDtypeStruct((copies, pick.shape[0], width), BF16),
+            jax.ShapeDtypeStruct((pick.shape[0], width), BF16),
             jax.ShapeDtypeStruct(local.shape, F32),
         ),
         in_specs=[SMEM] + [VMEM] * 11,
@@ -278,73 +277,98 @@
     )(owner, queries, keys_values, got, known, sums, local, fade, keep, maps, gain, pick)
 
 
-def choose_kernel(rows_ref, pick_ref, send_ref):
-    step = 4 * LANES
-    for q in range(rows_ref.shape[1] // step):
-        cols = slice(q * step, (q + 1) * step)
-        rows = jnp.dot(pick_ref[...], rows_ref[:, cols], preferred_element_type=F32).astype(BF16)
-        for i in range(send_ref.shape[0]):
-            send_ref[i, :, cols] = rows
-
-
-def choose(rows, pick, copies):
+def stream_kernel(body, arrays, chunks, *refs):
+    consts = len(refs) - 2 * arrays - 4
+    sources = refs[:arrays]
+    fixed = refs[arrays : arrays + consts]
+    out_ref = refs[arrays + consts]
+    held = refs[arrays + consts + 1 : 2 * arrays + consts + 1]
+    made, in_sems, out_sems = refs[2 * arrays + consts + 1 :]
+    step = out_ref.shape[1] // chunks
+
+    def inward(k, c):
+        cols = pl.ds(c * step, step)
+        return pltpu.make_async_copy(
+            sources[k].at[:, cols], held[k].at[:, cols], in_sems.at[k, c]
+        )
+
+    def outward(c):
+        cols = pl.ds(c * step, step)
+        return pltpu.make_async_copy(made.at[:, cols], out_ref.at[:, cols], out_sems.at[c])
+
+    for c in range(chunks):
+        for k in range(arrays):
+            inward(k, c).start()
+    constants = [ref[...] for ref in fixed]
+    for c in range(chunks):
+        cols = slice(c * step, (c + 1) * step)
+        for k in range(arrays):
+            inward(k, c).wait()
+        made[:, cols] = body([ref[:, cols] for ref in held], *constants)
+        outward(c).start()
+    for c in range(chunks):
+        outward(c).wait()
+
+
+def stream(body, arrays, consts, rows, chunks=4):
+    width = arrays[0].shape[1]
+    anywhere = pl.BlockSpec(memory_space=pl.ANY)
+    moved = sum(array.shape[0] for array in arrays) + rows
     return pl.pallas_call(
-        choose_kernel,
-        out_shape=jax.ShapeDtypeStruct((copies, pick.shape[0], rows.shape[1]), BF16),
-        in_specs=[VMEM] * 2,
-        out_specs=VMEM,
-        name="choose",
-    )(rows, pick)
-
-
-def combine_kernel(parts_ref, weights_ref, out_ref):
-    length = out_ref.shape[0]
-    both = jnp.dot(weights_ref[...], parts_ref[...], preferred_element_type=F32)
-    out_ref[...] = (both[:length] + both[length:]).astype(out_ref.dtype)
-
-
-def combine(parts, weights, dtype):
-    rows, width = parts.shape
+        functools.partial(stream_kernel, body, len(arrays), chunks),
+        out_shape=jax.ShapeDtypeStruct((rows, width), BF16),
+        in_specs=[anywhere] * len(arrays) + [VMEM] * len(consts),
+        out_specs=anywhere,
+        scratch_shapes=[pltpu.VMEM(array.shape, array.dtype) for array in arrays]
+        + [
+            pltpu.VMEM((rows, width), BF16),
+            pltpu.SemaphoreType.DMA((len(arrays), chunks)),
+            pltpu.SemaphoreType.DMA((chunks,)),
+        ],
+        cost_estimate=pl.CostEstimate(
+            flops=2 * moved * width, bytes_accessed=2 * moved * width, transcendentals=0
+        ),
+    )(*arrays, *consts)
+
+
+def choose(rows, pick):
+    def body(parts, pick):
+        return jnp.dot(pick, parts[0], preferred_element_type=F32).astype(BF16)
+
+    return stream(body, [rows], [pick], pick.shape[0])
+
+
+def weighed(parts, weights):
+    both = jnp.dot(weights, parts, preferred_element_type=F32)
     length = weights.shape[0] // 2
-    step = 8 * LANES
-    return pl.pallas_call(
-        combine_kernel,
-        out_shape=jax.ShapeDtypeStruct((length, width), dtype),
-        grid=(width // step,),
-        in_specs=[
-            pl.BlockSpec((rows, step), lambda i: (0, i)),
-            pl.BlockSpec(weights.shape, lambda i: (0, 0)),
-        ],
-        out_specs=pl.BlockSpec((length, step), lambda i: (0, i)),
-        name="combine",
-    )(parts, weights)
-
-
-def finish_kernel(parts_ref, weights_ref, mixed_ref, far_ref, out_ref):
-    length = out_ref.shape[0]
-    both = jnp.dot(weights_ref[...], parts_ref[...], preferred_element_type=F32)
-    summed = both[:length] + both[length:] + far_ref[...].astype(F32)
-    out_ref[...] = (mixed_ref[...].astype(F32) + summed).astype(out_ref.dtype)
-
-
-def finish(parts, weights, mixed, far):
-    rows, width = parts.shape
-    length = weights.shape[0] // 2
-    step = 8 * LANES
-    narrow = pl.BlockSpec((length, step), lambda i: (0, i))
-    return pl.pallas_call(
-        finish_kernel,
-        out_shape=jax.ShapeDtypeStruct((length, width), BF16),
-        grid=(width // step,),
-        in_specs=[
-            pl.BlockSpec((rows, step), lambda i: (0, i)),
-            pl.BlockSpec(weights.shape, lambda i: (0, 0)),
-            narrow,
-            narrow,
-        ],
-        out_specs=narrow,
-        name="finish",
-    )(parts, weights, mixed, far)
+    return both[:length] + both[length:]
+
+
+def combine(parts, weights):
+    def body(held, weights):
+        return weighed(held[0], weights).astype(BF16)
+
+    return stream(body, [parts], [weights], weights.shape[0] // 2)
+
+
+def finish(parts, weights, mixed, sums):
+    def body(held, weights):
+        total = weighed(held[0], weights)
+        for far in held[2:]:
+            total = total + far.astype(F32)
+        return (held[1].astype(F32) + total).astype(BF16)
+
+    return stream(body, [parts, mixed] + sums, [weights], mixed.shape[0])
+
+
+def join(first, others):
+    if not others:
+        return first
+
+    def body(held):
+        return sum(part.astype(F32) for part in held).astype(BF16)
+
+    return stream(body, [first] + others, [], first.shape[0])
 
 
 def targets(expert_list, experts):
@@ -368,20 +392,71 @@
     return jnp.any(hot, axis=1).T.astype(BF16)
 
 
-def gate_weights(rows, router_weight, expert_ids, hot, copies):
+def gate_weights(rows, router_weight, expert_ids, hot):
     logits = jnp.dot(rows, router_weight, preferred_element_type=F32)
     named = expert_ids[:, :, None] == jnp.arange(router_weight.shape[1], dtype=jnp.int32)
     chosen = jnp.sum(jnp.where(named, logits[:, None, :], 0.0), axis=2)
     lifted = jax.nn.sigmoid(chosen)
     gates = lifted / jnp.sum(lifted, axis=1, keepdims=True)
     weights = jnp.sum(jnp.where(hot, gates[:, :, None], 0.0), axis=1)
-    weights = jnp.concatenate([weights] * copies, 1)
     return split_rows(weights)
 
 
-def apply_expert(rows, up_local, down_local):
-    hidden = jax.nn.silu(jnp.dot(rows, up_local, preferred_element_type=F32)).astype(BF16)
-    return jnp.dot(hidden, down_local, preferred_element_type=F32).astype(BF16)
+def expert_kernel(count, first, *refs):
+    sources = refs[:count]
+    up_ref, down_ref = refs[count : count + 2]
+    outs = refs[count + 2 : 2 * count + 2]
+    rows_ref, hidden_ref = refs[2 * count + 2 :]
+    step = pl.program_id(0)
+    tile = up_ref.shape[1]
+    each = sources[0].shape[0]
+
+    @pl.when(step == 0)
+    def _():
+        for k in range(count):
+            rows_ref[k * each : (k + 1) * each, :] = sources[k][...]
+
+    @pl.when(step < first)
+    def _():
+        lifted = jnp.dot(rows_ref[...], up_ref[...], preferred_element_type=F32)
+        cols = pl.ds(pl.multiple_of(jnp.minimum(step, first - 1) * tile, tile), tile)
+        hidden_ref[:, cols] = (lifted / (1.0 + jnp.exp(-lifted))).astype(BF16)
+
+    @pl.when(step >= first)
+    def _():
+        part = jnp.dot(hidden_ref[...], down_ref[...], preferred_element_type=F32).astype(BF16)
+        for k in range(count):
+            outs[k][...] = part[k * each : (k + 1) * each]
+
+
+def apply_expert(chunks, up_local, down_local):
+    count = len(chunks)
+    each, width = chunks[0].shape
+    hidden = up_local.shape[1]
+    tile = next(t for t in (896, 512, 256, 128) if hidden % t == 0)
+    wide = 8 * LANES
+    first = hidden // tile
+    return pl.pallas_call(
+        functools.partial(expert_kernel, count, first),
+        out_shape=[jax.ShapeDtypeStruct((each, width), BF16)] * count,
+        grid=(first + width // wide,),
+        in_specs=[pl.BlockSpec((each, width), lambda i: (0, 0))] * count
+        + [
+            pl.BlockSpec((width, tile), lambda i: (0, jnp.minimum(i, first - 1))),
+            pl.BlockSpec((hidden, wide), lambda i: (0, jnp.maximum(i - first, 0))),
+        ],
+        out_specs=[pl.BlockSpec((each, wide), lambda i: (0, jnp.maximum(i - first, 0)))] * count,
+        scratch_shapes=[
+            pltpu.VMEM((count * each, width), BF16),
+            pltpu.VMEM((count * each, hidden), BF16),
+        ],
+        cost_estimate=pl.CostEstimate(
+            flops=4 * count * each * width * hidden,
+            bytes_accessed=4 * width * hidden + 4 * count * each * width,
+            transcendentals=count * each * hidden,
+        ),
+        name="expert",
+    )(*chunks, up_local, down_local)
 
 
 def local(
@@ -408,26 +483,27 @@
     peers = lax.axis_size("dp")
     columns = lax.axis_size("expert")
     near = peers // 2
-    ring = [(k, (k + near) % peers) for k in range(peers)]
-    groups = [
-        [(h * near + i) * columns + c for i in range(near) for c in range(columns)]
-        for h in range(2)
-    ]
+
+    def route(turn, side):
+        return [
+            (h * near + i, (h + side) % 2 * near + (i + turn) % near)
+            for h in range(2)
+            for i in range(near)
+        ]
+
     experts = router_weight.shape[1]
     holders = block_holder[0]
     indices = block_index[0]
     entries = holders.shape[0]
     slot = entries // peers
 
-    def swap(rows):
-        return lax.all_to_all(
-            rows,
-            ("dp", "expert"),
-            split_axis=0,
-            concat_axis=0,
-            tiled=True,
-            axis_index_groups=groups,
-        )
+    def move(rows, turn, side):
+        return lax.ppermute(rows, "dp", route(turn, side))
+
+    def swap_rows(rows):
+        blocks = rows.reshape(columns, -1, rows.shape[-1])
+        moved = lax.all_to_all(blocks, "expert", split_axis=0, concat_axis=0, tiled=True)
+        return moved.reshape(rows.shape)
 
     places = jnp.arange(entries, dtype=jnp.int32)
     same = holders[:, None] == holders[None, :]
@@ -449,8 +525,11 @@
         1,
     )
     asked = lax.all_to_all(ask, "dp", split_axis=0, concat_axis=0, tiled=True)
-    partner = (lax.axis_index("dp") + near) % peers
-    theirs = lax.dynamic_index_in_dim(asked[:, slot + 1 :], partner, 0, keepdims=False)
+    place = lax.axis_index("dp")
+
+    def names_of(turn):
+        source = (place // near + 1) % 2 * near + (place % near + near - turn) % near
+        return lax.dynamic_index_in_dim(asked[:, slot + 1 :], source, 0, keepdims=False)
 
     states = state_pool.reshape(state_pool.shape[0], -1, LANES).astype(BF16)
     packed = pack(asked[:, : slot + 1], block_pool, states)
@@ -474,29 +553,40 @@
         state_maps,
         norm_gain[None, :],
         pick,
-        near,
-    )
-    capacity = mine.shape[0] // experts
-    width = tokens.shape[1]
+    )
     up_local = up_weight[0]
     down_local = down_weight[0]
 
-    far_rows = lax.ppermute(normed, "dp", ring)
-    near_in = swap(send.reshape(near * experts, capacity, width))
-    far_hot = one_hots(theirs, experts)
-    far_send = choose(far_rows, picker(far_hot), near)
-    far_in = swap(far_send.reshape(near * experts, capacity, width))
-
-    near_out = apply_expert(near_in.reshape(-1, width), up_local, down_local)
-    far_out = apply_expert(far_in.reshape(-1, width), up_local, down_local)
-    near_weights = gate_weights(normed, router_weight, expert_ids, hot, near)
-    far_weights = gate_weights(
-        far_rows, router_weight, theirs.reshape(expert_ids.shape), far_hot, near
-    )
-    far_back = swap(far_out.reshape(near_in.shape)).reshape(-1, width)
-    far_sum = lax.ppermute(combine(far_back, far_weights, BF16), "dp", ring)
-    near_back = swap(near_out.reshape(near_in.shape)).reshape(-1, width)
-    layer_out = finish(near_back, near_weights, mixed, far_sum)
+    def gates(rows, names, hots):
+        return gate_weights(rows, router_weight, names.reshape(expert_ids.shape), hots)
+
+    far_rows = [move(normed, 0, 1)]
+    near_in = swap_rows(send)
+    near_moved = [move(near_in, turn, 0) for turn in range(1, near)]
+    far_rows += [move(far_rows[0], turn, 0) for turn in range(1, near)]
+    far_names = [names_of(turn) for turn in range(near)]
+    far_hots = [one_hots(names, experts) for names in far_names]
+    far_in = []
+    for turn in range(near):
+        chosen = choose(far_rows[turn], picker(far_hots[turn]))
+        far_in.append(swap_rows(chosen))
+
+    near_out, first_out = apply_expert([near_in, far_in[0]], up_local, down_local)
+    moved_out, far_out = [], [first_out]
+    if near > 1:
+        moved_out += apply_expert(near_moved, up_local, down_local)
+        far_out += apply_expert(far_in[1:], up_local, down_local)
+
+    far_sums = []
+    for turn in range(near):
+        weights = gates(far_rows[turn], far_names[turn], far_hots[turn])
+        back = swap_rows(far_out[turn])
+        part = combine(back, weights)
+        far_sums.append(move(part, near - turn, 1))
+    moved_back = [move(rows, near - turn, 0) for turn, rows in enumerate(moved_out, 1)]
+    joined = join(near_out, moved_back)
+    near_back = swap_rows(joined)
+    layer_out = finish(near_back, gates(normed, mine, hot), mixed, far_sums)
     return (layer_out, final_state.reshape(1, -1))
 
 

time: 250 us -> 266 us (1.064)
  the two profiles are of different devices: /device:TPU:0 before, /device:TPU:10 now
where the time goes in v2:
time: 266 us; the launch traced here: 265 us
  waiting for transfers between devices  109 us (41%)
  Pallas kernels  82.3 us (31%)
  starting transfers between devices  47.6 us (18%)
  local copies, waits for them, and re-layouts  12.4 us (5%)
  other arithmetic  6.94 us (3%)
  matrix products  3.26 us (1%)
  between operations  3.08 us (1%)
    ppermute x6, waiting for transfers between devices, move(): return lax.ppermute(rows, 'dp', route(turn, side))  77.3 us
    pallas_call x3, Pallas kernels, apply_expert(): pl.pallas_call(functools.partial(expert_kernel, count, first), out_shape=...  46 us
    all_to_all x6, starting transfers between devices, swap_rows(): lax.all_to_all(blocks, 'expert', split_axis=0, concat_axis=0, tiled=True)  26.2 us
    all_to_all x1, waiting for transfers between devices, local(): got = lax.all_to_all(packed, 'dp', split_axis=0, concat_axis=0, tiled=True)  22.3 us
    pallas_call x6, Pallas kernels, stream(): pl.pallas_call(functools.partial(stream_kernel, body, len(arrays), chunks...  19.1 us
    ppermute x6, starting transfers between devices, move(): return lax.ppermute(rows, 'dp', route(turn, side))  11.2 us
    pallas_call x1, Pallas kernels, mix(): pl.pallas_call(mix_kernel, out_shape=(jax.ShapeDtypeStruct((length, width...  8.03 us
    all_to_all x6, waiting for transfers between devices, swap_rows(): lax.all_to_all(blocks, 'expert', split_axis=0, concat_axis=0, tiled=True)  7.17 us
  transfers between devices with their start and end apart: 14, of which 9 were waited for; matrix products, arithmetic and copies ran while one was open for 5% of the time, Pallas kernels for 25%

profile of v2, /device:TPU:10, one launch (start us, length us, event | category | flops | bytes accessed | tf_op | source)
XLA Modules:
  0.0 264.6 jit_solution(1705936365899572233)
XLA Ops:
  1.3 0.9 convert_reduce_fusion
  2.2 0.7 fusion.10
  2.9 0.8 select_reduce_fusion.6
  3.8 0.8 copy.61
  4.8 0.6 all_to_all.29
  5.4 5.3 %all-to-all-start = ((s32[4,1,133]{2,1,0:T(1,128)}), s32[4,1,133]{2,1,0:T(1,128)S(1)}, u32[]{:S(2)}, u32[]{:S(2)}) async-start(s32[4,1,133]{2,1,0:T(1,128)} %all_to_all.29), calls=%async_computation | async-start | bytes 8192 | tf_op jit(solution)/shard_map/all_to_all | solution.py:527
  10.8 1.2 convert_bitcast_fusion
  12.0 0.7 copy.78
  12.7 2.2 all-to-all-done
  14.9 0.6 slice.9.refs_0_
  15.5 4.4 %pack.1 = bf16[4,96,2048]{2,1,0:T(8,128)(2,1)} custom-call(s32[4,5]{1,0:T(4,128)} %slice.9.refs_0_, bf16[8,16,2048]{2,1,0:T(8,128)(2,1)} %refs_4_.1, bf16[8,16,2048]{2,1,0:T(8,128)(2,1)} %refs_4_.1, bf16[8,16,2048]{2,1,0:T(8,128)(2,1)} %refs_4_.1, bf16[8,16,2048]{2,1,0:T(8,128)(2,1)} %refs_4_.1, bf16[2,512,128]{2,1,0:T(8,128)(2,1)} %bitcast.65), custom_call_target="tpu_custom_call" | custom-call | tf_op jit(solution)/shard_map/pack/pallas_call | solution.py:67
  19.9 5.0 %all-to-all-start.1 = ((bf16[4,96,2048]{2,1,0:T(8,128)(2,1)}), bf16[4,96,2048]{2,1,0:T(8,128)(2,1)S(1)}, u32[]{:S(2)}, u32[]{:S(2)}) async-start(bf16[4,96,2048]{2,1,0:T(8,128)(2,1)} %pack.1), calls=%async_computation.1 | async-start | bytes 3145728 | tf_op jit(solution)/shard_map/all_to_all | solution.py:536
  26.2 0.7 broadcast_in_dim_reshape.2.known_ref
  26.9 1.4 copy.62.maps_ref
  28.5 0.1 convert_element_type.88
  28.7 0.7 multiply_add_fusion.2
  29.5 0.7 copy.64
  30.2 4.8 %scan_local.1 = (f32[64,4096]{1,0:T(8,128)}, f32[512,128]{1,0:T(8,128)}, f32[64,64]{1,0:T(8,128)}, f32[1,64]{1,0:T(1,128)}) custom-call(bf16[64,4096]{1,0:T(8,128)(2,1)} %x_ref.1, f32[64,32]{1,0:T(8,128)} %copy.62.maps_ref, f32[64,64]{1,0:T(8,128)} %steps_ref.1, f32[64,64]{1,0:T(8,128)} %decays_ref.1, bf16[64,4096]{1,0:T(8,128)(2,1)} %tokens_ref.1), custom_call_target="tpu_custom_call" | custom-call | tf_op jit(solution)/shard_map/scan_local/pallas_call | solution.py:135
  35.0 22.3 %all-to-all-done.1.got_ref = bf16[4,96,2048]{2,1,0:T(8,128)(2,1)S(1)} async-done(((bf16[4,96,2048]{2,1,0:T(8,128)(2,1)}), bf16[4,96,2048]{2,1,0:T(8,128)(2,1)S(1)}, u32[]{:S(2)}, u32[]{:S(2)}) %all-to-all-start.1) | async-done | bytes 1572896 | tf_op jit(solution)/shard_map/all_to_all | solution.py:536
  57.3 1.2 copy-done.1
  58.4 8.0 %mix.1 = (bf16[64,4096]{1,0:T(8,128)(2,1)}, bf16[64,4096]{1,0:T(8,128)(2,1)}, bf16[128,4096]{1,0:T(8,128)(2,1)}, f32[512,128]{1,0:T(8,128)}) custom-call(s32[1]{0:T(128)S(6)} %copy.81.owner_ref, bf16[64,4096]{1,0:T(8,128)(2,1)} %q_ref.1, bf16[64,2048]{1,0:T(8,128)(2,1)} %kv_ref.1, bf16[4,96,2048]{2,1,0:T(8,128)(2,1)} %copy-done.1, ...), custom_call_target="tpu_custom_call" | custom-call | tf_op jit(solution)/shard_map/mix/pallas_call | solution.py:265
  66.4 4.4 %all-to-all-start.2 = ((bf16[8,16,4096]{2,1,0:T(8,128)(2,1)}), bf16[8,16,4096]{2,1,0:T(8,128)(2,1)S(1)}, u32[]{:S(2)}, u32[]{:S(2)}) async-start(bf16[8,16,4096]{2,1,0:T(8,128)(2,1)} %bitcast.66), calls=%async_computation.2 | async-start | bytes 2097152 | tf_op jit(solution)/shard_map/all_to_all | solution.py:505
  70.9 3.3 %collective-permute-start = (bf16[64,4096]{1,0:T(8,128)(2,1)}, bf16[64,4096]{1,0:T(8,128)(2,1)S(1)}, u32[]{:S(2)}, u32[]{:S(2)}) collective-permute-start(bf16[64,4096]{1,0:T(8,128)(2,1)} %get-tuple-element.17), channel_id=1, source_target_pairs={{0,16},{8,24},{16,0},{24,8},{1,17},{9,25},{17,1},{25,9},{2,18},{10... | collective-permute-start | bytes 1572872 | tf_op jit(solution)/shard_map/ppermute | solution.py:501
  74.3 0.1 fusion.2
  74.4 0.2 fusion.1
  74.6 0.1 convert_element_type.92
  75.4 0.7 copy.68
  76.3 20.7 %collective-permute-done.refs_0_ = bf16[64,4096]{1,0:T(8,128)(2,1)S(1)} collective-permute-done((bf16[64,4096]{1,0:T(8,128)(2,1)}, bf16[64,4096]{1,0:T(8,128)(2,1)S(1)}, u32[]{:S(2)}, u32[]{:S(2)}) %collective-permute-start) | collective-permute-done | bytes 524320 | tf_op jit(solution)/shard_map/ppermute | solution.py:501
  97.0 0.8 copy-done.10
  97.8 3.2 %shard_map.194 = bf16[128,4096]{1,0:T(8,128)(2,1)} custom-call(bf16[64,4096]{1,0:T(8,128)(2,1)} %copy-done.10, bf16[128,64]{1,0:T(8,128)(2,1)} %bitcast.70), custom_call_target="tpu_custom_call" | custom-call | flops 1572864 | bytes 1572864 | tf_op jit(solution)/shard_map/pallas_call | solution.py:317
  101.1 4.2 %all-to-all-start.3 = ((bf16[8,16,4096]{2,1,0:T(8,128)(2,1)}), bf16[8,16,4096]{2,1,0:T(8,128)(2,1)S(1)}, u32[]{:S(2)}, u32[]{:S(2)}) async-start(bf16[8,16,4096]{2,1,0:T(8,128)(2,1)} %bitcast.63), calls=%async_computation.3 | async-start | bytes 2097152 | tf_op jit(solution)/shard_map/all_to_all | solution.py:505
  105.4 0.7 copy.72
  106.1 2.4 collective-permute-start.4
  108.5 1.3 fusion.17
  109.9 1.3 fusion.15
  111.2 9.8 %collective-permute-done.4.refs_0_ = bf16[64,4096]{1,0:T(8,128)(2,1)S(1)} collective-permute-done((bf16[64,4096]{1,0:T(8,128)(2,1)}, bf16[64,4096]{1,0:T(8,128)(2,1)S(1)}, u32[]{:S(2)}, u32[]{:S(2)}) %collective-permute-start.4) | collective-permute-done | bytes 524320 | tf_op jit(solution)/shard_map/ppermute | solution.py:501
  120.9 0.8 copy-done.8
  121.7 3.3 %shard_map.197 = bf16[128,4096]{1,0:T(8,128)(2,1)} custom-call(bf16[64,4096]{1,0:T(8,128)(2,1)} %copy-done.8, bf16[128,64]{1,0:T(8,128)(2,1)} %bitcast.69), custom_call_target="tpu_custom_call" | custom-call | flops 1572864 | bytes 1572864 | tf_op jit(solution)/shard_map/pallas_call | solution.py:317
  125.0 4.2 %all-to-all-start.6 = ((bf16[8,16,4096]{2,1,0:T(8,128)(2,1)}), bf16[8,16,4096]{2,1,0:T(8,128)(2,1)S(1)}, u32[]{:S(2)}, u32[]{:S(2)}) async-start(bf16[8,16,4096]{2,1,0:T(8,128)(2,1)} %bitcast.64), calls=%async_computation.6 | async-start | bytes 2097152 | tf_op jit(solution)/shard_map/all_to_all | solution.py:505
  129.2 1.8 collective-permute-start.1
  131.1 17.3 %expert.3 = (bf16[128,4096]{1,0:T(8,128)(2,1)}, bf16[128,4096]{1,0:T(8,128)(2,1)}) custom-call(bf16[128,4096]{1,0:T(8,128)(2,1)} %bitcast.55, bf16[128,4096]{1,0:T(8,128)(2,1)} %bitcast.58, bf16[4096,1792]{1,0:T(8,128)(2,1)} %bitcast.48, bf16[1792,4096]{1,0:T(8,128)(2,1)} %bitcast.51), custom_call_target="tpu_custom_call" | custom-call | flops 7516192768 | bytes 33554432 | tf_op jit(solution)/shard_map/expert/pallas_call | solution.py:439
  148.4 4.2 %all-to-all-start.5 = ((bf16[8,16,4096]{2,1,0:T(8,128)(2,1)}), bf16[8,16,4096]{2,1,0:T(8,128)(2,1)S(1)}, u32[]{:S(2)}, u32[]{:S(2)}) async-start(bf16[8,16,4096]{2,1,0:T(8,128)(2,1)} %bitcast.67), calls=%async_computation.5 | async-start | bytes 2097152 | tf_op jit(solution)/shard_map/all_to_all | solution.py:505
  152.7 1.9 collective-permute-done.1.refs_0_
  154.6 14.3 %expert.4 = bf16[128,4096]{1,0:T(8,128)(2,1)} custom-call(bf16[128,4096]{1,0:T(8,128)(2,1)} %collective-permute-done.1.refs_0_, bf16[4096,1792]{1,0:T(8,128)(2,1)} %bitcast.49, bf16[1792,4096]{1,0:T(8,128)(2,1)} %bitcast.52), custom_call_target="tpu_custom_call" | custom-call | flops 3758096384 | bytes 31457280 | tf_op jit(solution)/shard_map/expert/pallas_call | solution.py:439
  168.9 1.7 collective-permute-start.2
  170.7 14.4 %expert.5 = bf16[128,4096]{1,0:T(8,128)(2,1)} custom-call(bf16[128,4096]{1,0:T(8,128)(2,1)} %bitcast.59, bf16[4096,1792]{1,0:T(8,128)(2,1)} %bitcast.50, bf16[1792,4096]{1,0:T(8,128)(2,1)} %bitcast.53), custom_call_target="tpu_custom_call" | custom-call | flops 3758096384 | bytes 31457280 | tf_op jit(solution)/shard_map/expert/pallas_call | solution.py:439
  185.1 4.2 %all-to-all-start.7 = ((bf16[8,16,4096]{2,1,0:T(8,128)(2,1)}), bf16[8,16,4096]{2,1,0:T(8,128)(2,1)S(1)}, u32[]{:S(2)}, u32[]{:S(2)}) async-start(bf16[8,16,4096]{2,1,0:T(8,128)(2,1)} %bitcast.60), calls=%async_computation.7 | async-start | bytes 2097152 | tf_op jit(solution)/shard_map/all_to_all | solution.py:505
  189.3 0.6 pad_maximum_fusion.refs_1_
  189.9 0.2 fusion.16
  190.3 3.3 %collective-permute-done.2.refs_1_ = bf16[128,4096]{1,0:T(8,128)(2,1)} collective-permute-done((bf16[128,4096]{1,0:T(8,128)(2,1)}, bf16[128,4096]{1,0:T(8,128)(2,1)}, u32[]{:S(2)}, u32[]{:S(2)}) %collective-permute-start.2) | collective-permute-done | bytes 1048608 | tf_op jit(solution)/shard_map/ppermute | solution.py:501
  193.6 2.4 shard_map.195
  196.0 7.2 %all-to-all-done.7 = bf16[8,16,4096]{2,1,0:T(8,128)(2,1)S(1)} async-done(((bf16[8,16,4096]{2,1,0:T(8,128)(2,1)}), bf16[8,16,4096]{2,1,0:T(8,128)(2,1)S(1)}, u32[]{:S(2)}, u32[]{:S(2)}) %all-to-all-start.7) | async-done | bytes 1048608 | tf_op jit(solution)/shard_map/all_to_all | solution.py:505
  203.1 5.0 %all-to-all-start.4 = ((bf16[8,16,4096]{2,1,0:T(8,128)(2,1)}), bf16[8,16,4096]{2,1,0:T(8,128)(2,1)S(1)}, u32[]{:S(2)}, u32[]{:S(2)}) async-start(bf16[8,16,4096]{2,1,0:T(8,128)(2,1)} %bitcast.56), calls=%async_computation.4 | async-start | bytes 2097152 | tf_op jit(solution)/shard_map/all_to_all | solution.py:505
  208.1 0.6 pad_maximum_fusion.1.refs_1_
  208.7 3.3 %shard_map.196 = bf16[64,4096]{1,0:T(8,128)(2,1)} custom-call(bf16[128,4096]{1,0:T(8,128)(2,1)} %bitcast.61, bf16[128,128]{1,0:T(8,128)(2,1)} %pad_maximum_fusion.refs_1_), custom_call_target="tpu_custom_call" | custom-call | flops 1572864 | bytes 1572864 | tf_op jit(solution)/shard_map/pallas_call | solution.py:317
  212.0 1.3 collective-permute-start.3
  213.3 3.3 %shard_map.198 = bf16[64,4096]{1,0:T(8,128)(2,1)} custom-call(bf16[128,4096]{1,0:T(8,128)(2,1)} %bitcast.62, bf16[128,128]{1,0:T(8,128)(2,1)} %pad_maximum_fusion.1.refs_1_), custom_call_target="tpu_custom_call" | custom-call | flops 1572864 | bytes 1572864 | tf_op jit(solution)/shard_map/pallas_call | solution.py:317
  216.6 0.6 collective-permute-start.5
  217.4 0.6 pad_maximum_fusion.2.refs_4_
  218.0 30.4 %collective-permute-done.3.refs_2_ = bf16[64,4096]{1,0:T(8,128)(2,1)S(1)} collective-permute-done((bf16[64,4096]{1,0:T(8,128)(2,1)}, bf16[64,4096]{1,0:T(8,128)(2,1)S(1)}, u32[]{:S(2)}, u32[]{:S(2)}) %collective-permute-start.3) | collective-permute-done | bytes 524320 | tf_op jit(solution)/shard_map/ppermute | solution.py:501
  248.4 11.3 %collective-permute-done.5.refs_3_ = bf16[64,4096]{1,0:T(8,128)(2,1)S(1)} collective-permute-done((bf16[64,4096]{1,0:T(8,128)(2,1)}, bf16[64,4096]{1,0:T(8,128)(2,1)S(1)}, u32[]{:S(2)}, u32[]{:S(2)}) %collective-permute-start.5) | collective-permute-done | bytes 524320 | tf_op jit(solution)/shard_map/ppermute | solution.py:501
  259.7 0.8 copy-done.12
  260.5 0.4 copy-done.3
  260.9 3.6 %shard_map.199 = bf16[64,4096]{1,0:T(8,128)(2,1)} custom-call(bf16[128,4096]{1,0:T(8,128)(2,1)} %bitcast.57, bf16[64,4096]{1,0:T(8,128)(2,1)} %get-tuple-element.19.refs_1_, bf16[64,4096]{1,0:T(8,128)(2,1)} %copy-done.11, bf16[64,4096]{1,0:T(8,128)(2,1)} %copy-done.12, bf16[128,128]{1,0:T(8,128)(2,1)} %pad_maximum_fusion.2.refs_4_), custom_call_target="tpu_custom_call" | custom-call | flops 3145728 | bytes 3145728 | tf_op jit(solution)/shard_map/pallas_call | solution.py:317
  (73 shorter events, 2.4 us)
Async XLA Ops:
  0.6 107.9 %copy-start = (bf16[4096,8]{0,1:T(8,128)(2,1)S(1)}, bf16[4096,8]{0,1:T(8,128)(2,1)}, u32[]{:S(2)}) copy-start(bf16[4096,8]{0,1:T(8,128)(2,1)} %param.34) | copy-start | bytes 196612
  0.6 109.2 %copy-start.13 = (s32[64,2]{0,1:T(2,128)S(1)}, s32[64,2]{0,1:T(2,128)}, u32[]{:S(2)}) copy-start(s32[64,2]{0,1:T(2,128)} %param.35) | copy-start | bytes 1540
  5.4 9.5 %all-to-all-start = ((s32[4,1,133]{2,1,0:T(1,128)}), s32[4,1,133]{2,1,0:T(1,128)S(1)}, u32[]{:S(2)}, u32[]{:S(2)}) async-start(s32[4,1,133]{2,1,0:T(1,128)} %all_to_all.29), calls=%async_computation | async-start | bytes 8192 | tf_op jit(solution)/shard_map/all_to_all | solution.py:527
  19.9 37.4 %all-to-all-start.1 = ((bf16[4,96,2048]{2,1,0:T(8,128)(2,1)}), bf16[4,96,2048]{2,1,0:T(8,128)(2,1)S(1)}, u32[]{:S(2)}, u32[]{:S(2)}) async-start(bf16[4,96,2048]{2,1,0:T(8,128)(2,1)} %pack.1), calls=%async_computation.1 | async-start | bytes 3145728 | tf_op jit(solution)/shard_map/all_to_all | solution.py:536
  57.3 1.2 copy-start.1
  66.4 34.6 %all-to-all-start.2 = ((bf16[8,16,4096]{2,1,0:T(8,128)(2,1)}), bf16[8,16,4096]{2,1,0:T(8,128)(2,1)S(1)}, u32[]{:S(2)}, u32[]{:S(2)}) async-start(bf16[8,16,4096]{2,1,0:T(8,128)(2,1)} %bitcast.66), calls=%async_computation.2 | async-start | bytes 2097152 | tf_op jit(solution)/shard_map/all_to_all | solution.py:505
  70.9 26.1 %collective-permute-start = (bf16[64,4096]{1,0:T(8,128)(2,1)}, bf16[64,4096]{1,0:T(8,128)(2,1)S(1)}, u32[]{:S(2)}, u32[]{:S(2)}) collective-permute-start(bf16[64,4096]{1,0:T(8,128)(2,1)} %get-tuple-element.17), channel_id=1, source_target_pairs={{0,16},{8,24},{16,0},{24,8},{1,17},{9,25},{17,1},{25,9},{2,18},{10... | collective-permute-start | bytes 1572872 | tf_op jit(solution)/shard_map/ppermute | solution.py:501
  97.0 0.8 copy-start.10
  101.1 30.0 %copy-start.2 = (bf16[8,16,4096]{2,1,0:T(8,128)(2,1)}, bf16[8,16,4096]{2,1,0:T(8,128)(2,1)S(1)}, u32[]{:S(2)}) copy-start(bf16[8,16,4096]{2,1,0:T(8,128)(2,1)S(1)} %all-to-all-done.2) | copy-start | bytes 3145732
  101.1 23.9 %all-to-all-start.3 = ((bf16[8,16,4096]{2,1,0:T(8,128)(2,1)}), bf16[8,16,4096]{2,1,0:T(8,128)(2,1)S(1)}, u32[]{:S(2)}, u32[]{:S(2)}) async-start(bf16[8,16,4096]{2,1,0:T(8,128)(2,1)} %bitcast.63), calls=%async_computation.3 | async-start | bytes 2097152 | tf_op jit(solution)/shard_map/all_to_all | solution.py:505
  106.1 14.8 %collective-permute-start.4 = (bf16[64,4096]{1,0:T(8,128)(2,1)}, bf16[64,4096]{1,0:T(8,128)(2,1)S(1)}, u32[]{:S(2)}, u32[]{:S(2)}) collective-permute-start(bf16[64,4096]{1,0:T(8,128)(2,1)} %copy-done.10), channel_id=1, source_target_pairs={{0,8},{8,0},{16,24},{24,16},{1,9},{9,1},{17,25},{25,17},{2,10},{10... | collective-permute-start | bytes 1572872 | tf_op jit(solution)/shard_map/ppermute | solution.py:501
  120.9 0.8 copy-start.8
  125.0 6.0 %copy-start.4 = (bf16[8,16,4096]{2,1,0:T(8,128)(2,1)}, bf16[8,16,4096]{2,1,0:T(8,128)(2,1)S(1)}, u32[]{:S(2)}) copy-start(bf16[8,16,4096]{2,1,0:T(8,128)(2,1)S(1)} %all-to-all-done.3) | copy-start | bytes 3145732
  125.0 23.3 %all-to-all-start.6 = ((bf16[8,16,4096]{2,1,0:T(8,128)(2,1)}), bf16[8,16,4096]{2,1,0:T(8,128)(2,1)S(1)}, u32[]{:S(2)}, u32[]{:S(2)}) async-start(bf16[8,16,4096]{2,1,0:T(8,128)(2,1)} %bitcast.64), calls=%async_computation.6 | async-start | bytes 2097152 | tf_op jit(solution)/shard_map/all_to_all | solution.py:505
  129.2 25.3 %collective-permute-start.1 = (bf16[128,4096]{1,0:T(8,128)(2,1)S(1)}, bf16[128,4096]{1,0:T(8,128)(2,1)}, u32[]{:S(2)}, u32[]{:S(2)}) collective-permute-start(bf16[128,4096]{1,0:T(8,128)(2,1)S(1)} %bitcast.54), channel_id=1, source_target_pairs={{0,8},{8,0},{16,24},{24,16},{1,9},{9,1},{17,25},{25,17},{2,10},{10... | collective-permute-start | bytes 3145736 | tf_op jit(solution)/shard_map/ppermute | solution.py:501
  148.3 20.6 %copy-start.5 = (bf16[8,16,4096]{2,1,0:T(8,128)(2,1)}, bf16[8,16,4096]{2,1,0:T(8,128)(2,1)S(1)}, u32[]{:S(2)}) copy-start(bf16[8,16,4096]{2,1,0:T(8,128)(2,1)S(1)} %all-to-all-done.6) | copy-start | bytes 3145732
  148.4 36.7 %all-to-all-start.5 = ((bf16[8,16,4096]{2,1,0:T(8,128)(2,1)}), bf16[8,16,4096]{2,1,0:T(8,128)(2,1)S(1)}, u32[]{:S(2)}, u32[]{:S(2)}) async-start(bf16[8,16,4096]{2,1,0:T(8,128)(2,1)} %bitcast.67), calls=%async_computation.5 | async-start | bytes 2097152 | tf_op jit(solution)/shard_map/all_to_all | solution.py:505
  168.9 24.6 %collective-permute-start.2 = (bf16[128,4096]{1,0:T(8,128)(2,1)}, bf16[128,4096]{1,0:T(8,128)(2,1)}, u32[]{:S(2)}, u32[]{:S(2)}) collective-permute-start(bf16[128,4096]{1,0:T(8,128)(2,1)} %expert.4), channel_id=1, source_target_pairs={{0,8},{8,0},{16,24},{24,16},{1,9},{9,1},{17,25},{25,17},{2,10},{10... | collective-permute-start | bytes 3145736 | tf_op jit(solution)/shard_map/ppermute | solution.py:501
  170.7 19.2 %copy-start.9 = (bf16[64,4096]{1,0:T(8,128)(2,1)S(1)}, bf16[64,4096]{1,0:T(8,128)(2,1)}, u32[]{:S(2)}) copy-start(bf16[64,4096]{1,0:T(8,128)(2,1)} %copy-done.8) | copy-start | bytes 1572868
  185.0 23.7 %copy-start.6 = (bf16[8,16,4096]{2,1,0:T(8,128)(2,1)}, bf16[8,16,4096]{2,1,0:T(8,128)(2,1)S(1)}, u32[]{:S(2)}) copy-start(bf16[8,16,4096]{2,1,0:T(8,128)(2,1)S(1)} %all-to-all-done.5) | copy-start | bytes 3145732
  185.1 18.1 %all-to-all-start.7 = ((bf16[8,16,4096]{2,1,0:T(8,128)(2,1)}), bf16[8,16,4096]{2,1,0:T(8,128)(2,1)S(1)}, u32[]{:S(2)}, u32[]{:S(2)}) async-start(bf16[8,16,4096]{2,1,0:T(8,128)(2,1)} %bitcast.60), calls=%async_computation.7 | async-start | bytes 2097152 | tf_op jit(solution)/shard_map/all_to_all | solution.py:505
  203.1 10.2 %copy-start.7 = (bf16[8,16,4096]{2,1,0:T(8,128)(2,1)}, bf16[8,16,4096]{2,1,0:T(8,128)(2,1)S(1)}, u32[]{:S(2)}) copy-start(bf16[8,16,4096]{2,1,0:T(8,128)(2,1)S(1)} %all-to-all-done.7) | copy-start | bytes 3145732
  203.1 56.6 %all-to-all-start.4 = ((bf16[8,16,4096]{2,1,0:T(8,128)(2,1)}), bf16[8,16,4096]{2,1,0:T(8,128)(2,1)S(1)}, u32[]{:S(2)}, u32[]{:S(2)}) async-start(bf16[8,16,4096]{2,1,0:T(8,128)(2,1)} %bitcast.56), calls=%async_computation.4 | async-start | bytes 2097152 | tf_op jit(solution)/shard_map/all_to_all | solution.py:505
  212.0 36.4 %collective-permute-start.3 = (bf16[64,4096]{1,0:T(8,128)(2,1)}, bf16[64,4096]{1,0:T(8,128)(2,1)S(1)}, u32[]{:S(2)}, u32[]{:S(2)}) collective-permute-start(bf16[64,4096]{1,0:T(8,128)(2,1)} %shard_map.196), channel_id=1, source_target_pairs={{0,16},{8,24},{16,0},{24,8},{1,17},{9,25},{17,1},{25,9},{2,18},{10... | collective-permute-start | bytes 1572872 | tf_op jit(solution)/shard_map/ppermute | solution.py:501
  216.6 43.1 %collective-permute-start.5 = (bf16[64,4096]{1,0:T(8,128)(2,1)}, bf16[64,4096]{1,0:T(8,128)(2,1)S(1)}, u32[]{:S(2)}, u32[]{:S(2)}) collective-permute-start(bf16[64,4096]{1,0:T(8,128)(2,1)} %shard_map.198), channel_id=1, source_target_pairs={{0,24},{8,16},{16,8},{24,0},{1,25},{9,17},{17,9},{25,1},{2,26},{10... | collective-permute-start | bytes 1572872 | tf_op jit(solution)/shard_map/ppermute | solution.py:501
  248.4 11.3 %copy-start.11 = (bf16[64,4096]{1,0:T(8,128)(2,1)}, bf16[64,4096]{1,0:T(8,128)(2,1)S(1)}, u32[]{:S(2)}) copy-start(bf16[64,4096]{1,0:T(8,128)(2,1)S(1)} %collective-permute-done.3.refs_2_) | copy-start | bytes 1572868
  259.7 0.8 copy-start.12
  259.7 1.2 copy-start.3

commit v3 on v2

--- a/solution.py
+++ b/solution.py
@@ -36,6 +36,49 @@
         jnp.broadcast_to(column_pair[:, 0:1], (rows, LANES)),
         jnp.broadcast_to(column_pair[:, 1:2], (rows, LANES)),
     )
+
+
+def places_of(names):
+    count = names.shape[1]
+    length = count // 2
+    token = lax.broadcasted_iota(jnp.int32, (length, count), 0)
+    lane = lax.broadcasted_iota(jnp.int32, (length, count), 1)
+    wide = jnp.broadcast_to(names.astype(F32), (length, count))
+    return [
+        jnp.sum(jnp.where(lane == 2 * token + j, wide, 0.0), axis=1, keepdims=True)
+        for j in range(2)
+    ]
+
+
+def hots_of(names, capacity):
+    columns = places_of(names)
+    count = names.shape[1]
+    length = count // 2
+    lane = lax.broadcasted_iota(jnp.int32, (length, count), 1)
+    expert = (lane // capacity).astype(F32)
+    place = (lane % capacity).astype(F32)
+    ones = [jnp.where(expert == column, 1.0, 0.0) for column in columns]
+    rows = lax.broadcasted_iota(jnp.int32, (length, length), 0)
+    cols = lax.broadcasted_iota(jnp.int32, (length, length), 1)
+    earlier = jnp.where(rows > cols, 1.0, 0.0).astype(BF16)
+    before = jnp.dot(earlier, (ones[0] + ones[1]).astype(BF16), preferred_element_type=F32)
+    here = jnp.where(before == place, 1.0, 0.0)
+    return [one * here for one in ones]
+
+
+def weights_of(logits, hots):
+    experts = logits.shape[1]
+    count = hots[0].shape[1]
+    sub = lax.broadcasted_iota(jnp.int32, (experts, count), 0)
+    lane = lax.broadcasted_iota(jnp.int32, (experts, count), 1)
+    wider = jnp.where(lane // (count // experts) == sub, 1.0, 0.0)
+    wide = jnp.dot(logits, wider, precision=HIGH, preferred_element_type=F32)
+    lifted = [
+        lax.logistic(jnp.sum(wide * hot, axis=1, keepdims=True)) for hot in hots
+    ]
+    total = lifted[0] + lifted[1]
+    weights = sum(hot * (lift / total) for hot, lift in zip(hots, lifted))
+    return split_rows(weights)
 
 
 def pack_kernel(slot, *refs):
@@ -74,6 +117,7 @@
             + [pl.BlockSpec((1,) + states.shape[1:], lambda j, asked_ref: (asked_ref[j, slot], 0, 0))],
             out_specs=pl.BlockSpec((1, rows, width), lambda j, asked_ref: (j, 0, 0)),
         ),
+        compiler_params=pltpu.CompilerParams(vmem_limit_bytes=8 << 20),
         name="pack",
     )(asked, *([block_pool] * slot), states)
 
@@ -142,6 +186,7 @@
         ),
         in_specs=[VMEM] * 5,
         out_specs=(VMEM,) * 4,
+        compiler_params=pltpu.CompilerParams(vmem_limit_bytes=56 << 20),
         name="scan_local",
     )(x, maps, steps, decays, tokens)
 
@@ -158,12 +203,18 @@
     keep_ref,
     maps_ref,
     gain_ref,
-    pick_ref,
+    names_ref,
+    router_ref,
+    mixed_out,
+    normed_ref,
+    send_out,
+    final_ref,
+    weights_ref,
+    total_ref,
     mixed_ref,
-    normed_ref,
     send_ref,
-    final_ref,
-    total_ref,
+    mixed_sem,
+    send_sems,
 ):
     length, width = q_ref.shape
     peers = got_ref.shape[0]
@@ -248,94 +299,126 @@
             mixed = mixed.astype(F32)
             total_ref[:, cols] = mixed
             squares = squares + mixed * mixed
+    mixed_copy = pltpu.make_async_copy(mixed_ref, mixed_out, mixed_sem)
+    mixed_copy.start()
+    send_copies = []
     mean = jnp.sum(squares, axis=1, keepdims=True) * (1.0 / width)
     scale = lax.rsqrt(mean + 1e-05)
+    experts = router_ref.shape[0]
+    hots = hots_of(names_ref[...], names_ref.shape[1] // experts)
+    pick = (hots[0] + hots[1]).astype(BF16)
+    logits = jnp.zeros((length, experts), F32)
     step = 4 * LANES
     for q in range(width // step):
         cols = slice(q * step, (q + 1) * step)
         normed = (total_ref[:, cols] * scale * gain_ref[:, cols]).astype(BF16)
         normed_ref[:, cols] = normed
-        send_ref[:, cols] = jnp.dot(
-            pick_ref[...], normed, preferred_element_type=F32
+        send_ref[:, cols] = lax.dot_general(
+            pick, normed, (((0,), (0,)), ((), ())), preferred_element_type=F32
         ).astype(BF16)
-
-
-def mix(owner, queries, keys_values, got, known, sums, local, fade, keep, maps, gain, pick):
+        send_copies.append(
+            pltpu.make_async_copy(send_ref.at[:, cols], send_out.at[:, cols], send_sems.at[q])
+        )
+        send_copies[-1].start()
+        logits = logits + lax.dot_general(
+            normed, router_ref[:, cols], (((1,), (1,)), ((), ())), preferred_element_type=F32
+        )
+    weights_ref[...] = weights_of(logits, hots)
+    mixed_copy.wait()
+    for copy in send_copies:
+        copy.wait()
+
+
+def mix(owner, *arrays):
+    queries, local, names = arrays[0], arrays[5], arrays[10]
     length, width = queries.shape
+    count = names.shape[1]
+    anywhere = pl.BlockSpec(memory_space=pl.ANY)
     return pl.pallas_call(
         mix_kernel,
         out_shape=(
+            pltpu.HBM((length, width), BF16),
             jax.ShapeDtypeStruct((length, width), BF16),
-            jax.ShapeDtypeStruct((length, width), BF16),
-            jax.ShapeDtypeStruct((pick.shape[0], width), BF16),
+            pltpu.HBM((count, width), BF16),
             jax.ShapeDtypeStruct(local.shape, F32),
+            jax.ShapeDtypeStruct((2 * length, count), BF16),
         ),
-        in_specs=[SMEM] + [VMEM] * 11,
-        out_specs=(VMEM,) * 4,
-        scratch_shapes=[pltpu.VMEM((length, width), F32)],
+        in_specs=[SMEM] + [VMEM] * len(arrays),
+        out_specs=(anywhere, VMEM, anywhere, VMEM, VMEM),
+        scratch_shapes=[
+            pltpu.VMEM((length, width), F32),
+            pltpu.VMEM((length, width), BF16),
+            pltpu.VMEM((count, width), BF16),
+            pltpu.SemaphoreType.DMA,
+            pltpu.SemaphoreType.DMA((width // (4 * LANES),)),
+        ],
+        compiler_params=pltpu.CompilerParams(vmem_limit_bytes=56 << 20),
         name="mix",
-    )(owner, queries, keys_values, got, known, sums, local, fade, keep, maps, gain, pick)
+    )(owner, *arrays[:2], resident(arrays[2]), *arrays[3:])
+
+
+def resident(array):
+    return pltpu.with_memory_space_constraint(array, pltpu.VMEM)
 
 
 def stream_kernel(body, arrays, chunks, *refs):
-    consts = len(refs) - 2 * arrays - 4
-    sources = refs[:arrays]
-    fixed = refs[arrays : arrays + consts]
-    out_ref = refs[arrays + consts]
-    held = refs[arrays + consts + 1 : 2 * arrays + consts + 1]
-    made, in_sems, out_sems = refs[2 * arrays + consts + 1 :]
+    held, fixed, out_ref = refs[:arrays], refs[arrays:-1], refs[-1]
     step = out_ref.shape[1] // chunks
-
-    def inward(k, c):
-        cols = pl.ds(c * step, step)
-        return pltpu.make_async_copy(
-            sources[k].at[:, cols], held[k].at[:, cols], in_sems.at[k, c]
-        )
-
-    def outward(c):
-        cols = pl.ds(c * step, step)
-        return pltpu.make_async_copy(made.at[:, cols], out_ref.at[:, cols], out_sems.at[c])
-
-    for c in range(chunks):
-        for k in range(arrays):
-            inward(k, c).start()
     constants = [ref[...] for ref in fixed]
     for c in range(chunks):
         cols = slice(c * step, (c + 1) * step)
-        for k in range(arrays):
-            inward(k, c).wait()
-        made[:, cols] = body([ref[:, cols] for ref in held], *constants)
-        outward(c).start()
-    for c in range(chunks):
-        outward(c).wait()
-
-
-def stream(body, arrays, consts, rows, chunks=4):
+        out_ref[:, cols] = body([ref[:, cols] for ref in held], *constants)
+
+
+def stream(body, arrays, consts, rows, chunks=4, keep=True, dtype=BF16):
     width = arrays[0].shape[1]
-    anywhere = pl.BlockSpec(memory_space=pl.ANY)
     moved = sum(array.shape[0] for array in arrays) + rows
+    shape = (rows, width)
     return pl.pallas_call(
         functools.partial(stream_kernel, body, len(arrays), chunks),
-        out_shape=jax.ShapeDtypeStruct((rows, width), BF16),
-        in_specs=[anywhere] * len(arrays) + [VMEM] * len(consts),
-        out_specs=anywhere,
-        scratch_shapes=[pltpu.VMEM(array.shape, array.dtype) for array in arrays]
-        + [
-            pltpu.VMEM((rows, width), BF16),
-            pltpu.SemaphoreType.DMA((len(arrays), chunks)),
-            pltpu.SemaphoreType.DMA((chunks,)),
-        ],
+        out_shape=pltpu.VMEM(shape, dtype) if keep else jax.ShapeDtypeStruct(shape, dtype),
+        in_specs=[VMEM] * (len(arrays) + len(consts)),
+        out_specs=VMEM,
         cost_estimate=pl.CostEstimate(
             flops=2 * moved * width, bytes_accessed=2 * moved * width, transcendentals=0
         ),
-    )(*arrays, *consts)
-
-
-def choose(rows, pick):
-    def body(parts, pick):
-        return jnp.dot(pick, parts[0], preferred_element_type=F32).astype(BF16)
-
-    return stream(body, [rows], [pick], pick.shape[0])
+        compiler_params=pltpu.CompilerParams(vmem_limit_bytes=8 << 20),
+    )(*[resident(array) for array in arrays], *consts)
+
+
+def choose_kernel(source_ref, rows_ref, names_ref, router_ref, send_ref, weights_ref):
+    experts = router_ref.shape[0]
+    length, width = rows_ref.shape
+    names = names_ref[pl.ds(source_ref[0], 1), :][:, : 2 * length]
+    hots = hots_of(names, 2 * length // experts)
+    pick = (hots[0] + hots[1]).astype(BF16)
+    logits = jnp.zeros((length, experts), F32)
+    step = 8 * LANES
+    for q in range(width // step):
+        cols = slice(q * step, (q + 1) * step)
+        rows = rows_ref[:, cols]
+        send_ref[:, cols] = lax.dot_general(
+            pick, rows, (((0,), (0,)), ((), ())), preferred_element_type=F32
+        ).astype(BF16)
+        logits = logits + lax.dot_general(
+            rows, router_ref[:, cols], (((1,), (1,)), ((), ())), preferred_element_type=F32
+        )
+    weights_ref[...] = weights_of(logits, hots)
+
+
+def choose(source, rows, names, router):
+    length, width = rows.shape
+    return pl.pallas_call(
+        choose_kernel,
+        out_shape=(
+            pltpu.HBM((2 * length, width), BF16),
+            jax.ShapeDtypeStruct((2 * length, 2 * length), BF16),
+        ),
+        in_specs=[SMEM] + [VMEM] * 3,
+        out_specs=(VMEM, VMEM),
+        compiler_params=pltpu.CompilerParams(vmem_limit_bytes=8 << 20),
+        name="choose",
+    )(source, resident(rows), names, router)
 
 
 def weighed(parts, weights):
@@ -351,14 +434,21 @@
     return stream(body, [parts], [weights], weights.shape[0] // 2)
 
 
-def finish(parts, weights, mixed, sums):
+def settle(parts, weights, mixed):
     def body(held, weights):
-        total = weighed(held[0], weights)
+        return weighed(held[0], weights)
+
+    return stream(body, [parts], [weights], mixed.shape[0], dtype=F32)
+
+
+def finish(base, mixed, sums):
+    def body(held):
+        total = held[0]
         for far in held[2:]:
             total = total + far.astype(F32)
         return (held[1].astype(F32) + total).astype(BF16)
 
-    return stream(body, [parts, mixed] + sums, [weights], mixed.shape[0])
+    return stream(body, [base, mixed] + sums, [], mixed.shape[0], keep=False)
 
 
 def join(first, others):
@@ -371,92 +461,89 @@
     return stream(body, [first] + others, [], first.shape[0])
 
 
-def targets(expert_list, experts):
-    capacity = expert_list.shape[0] // experts
-    onehot = (expert_list[:, None] == jnp.arange(experts, dtype=jnp.int32)[None, :]).astype(F32)
-    number = expert_list.shape[0]
-    places = jnp.arange(number, dtype=jnp.int32)
-    earlier = (places[:, None] > places[None, :]).astype(F32)
-    before = jnp.dot(earlier, onehot, preferred_element_type=F32)
-    slot = jnp.sum(before * onehot, axis=1).astype(jnp.int32)
-    return expert_list * capacity + slot
-
-
-def one_hots(expert_list, experts):
-    target = targets(expert_list, experts).reshape(-1, 2)
-    places = jnp.arange(expert_list.shape[0], dtype=jnp.int32)
-    return target[:, :, None] == places[None, None, :]
-
-
-def picker(hot):
-    return jnp.any(hot, axis=1).T.astype(BF16)
-
-
-def gate_weights(rows, router_weight, expert_ids, hot):
-    logits = jnp.dot(rows, router_weight, preferred_element_type=F32)
-    named = expert_ids[:, :, None] == jnp.arange(router_weight.shape[1], dtype=jnp.int32)
-    chosen = jnp.sum(jnp.where(named, logits[:, None, :], 0.0), axis=2)
-    lifted = jax.nn.sigmoid(chosen)
-    gates = lifted / jnp.sum(lifted, axis=1, keepdims=True)
-    weights = jnp.sum(jnp.where(hot, gates[:, :, None], 0.0), axis=1)
-    return split_rows(weights)
-
-
-def expert_kernel(count, first, *refs):
+def expert_kernel(count, ahead, *refs):
     sources = refs[:count]
-    up_ref, down_ref = refs[count : count + 2]
+    up_hbm, down_hbm = refs[count : count + 2]
     outs = refs[count + 2 : 2 * count + 2]
-    rows_ref, hidden_ref = refs[2 * count + 2 :]
-    step = pl.program_id(0)
-    tile = up_ref.shape[1]
-    each = sources[0].shape[0]
-
-    @pl.when(step == 0)
-    def _():
+    up_ref, down_ref, hidden_ref, made_ref, sems, out_sems = refs[2 * count + 2 :]
+    each, width = sources[0].shape
+    tile = 2 * LANES if up_ref.shape[1] % (2 * LANES) == 0 else LANES
+    wide = 4 * LANES
+    first, second = up_ref.shape[1] // tile, width // wide
+
+    def inward(n):
+        if n < first:
+            cols = pl.ds(n * tile, tile)
+            pair = up_hbm.at[:, cols], up_ref.at[:, cols]
+        else:
+            cols = pl.ds((n - first) * wide, wide)
+            pair = down_hbm.at[:, cols], down_ref.at[:, cols]
+        return pltpu.make_async_copy(*pair, sems.at[n])
+
+    def outward(k, n):
+        cols = pl.ds(n * wide, wide)
+        return pltpu.make_async_copy(
+            made_ref.at[pl.ds(k * each, each), cols], outs[k].at[:, cols], out_sems.at[k, n]
+        )
+
+    for n in range(min(ahead, first + second)):
+        inward(n).start()
+    if count == 1:
+        rows = sources[0][...]
+    else:
+        rows = jnp.concatenate([source[...] for source in sources], 0)
+    for n in range(first + second):
+        inward(n).wait()
+        if n + ahead < first + second:
+            inward(n + ahead).start()
+        if n < first:
+            cols = slice(n * tile, (n + 1) * tile)
+            lifted = jnp.dot(rows, up_ref[:, cols], preferred_element_type=F32)
+            hidden_ref[:, cols] = (lifted / (1.0 + jnp.exp(-lifted))).astype(BF16)
+        else:
+            cols = slice((n - first) * wide, (n - first + 1) * wide)
+            made_ref[:, cols] = jnp.dot(
+                hidden_ref[...], down_ref[:, cols], preferred_element_type=F32
+            ).astype(BF16)
+            for k in range(count):
+                outward(k, n - first).start()
+    for n in range(second):
         for k in range(count):
-            rows_ref[k * each : (k + 1) * each, :] = sources[k][...]
-
-    @pl.when(step < first)
-    def _():
-        lifted = jnp.dot(rows_ref[...], up_ref[...], preferred_element_type=F32)
-        cols = pl.ds(pl.multiple_of(jnp.minimum(step, first - 1) * tile, tile), tile)
-        hidden_ref[:, cols] = (lifted / (1.0 + jnp.exp(-lifted))).astype(BF16)
-
-    @pl.when(step >= first)
-    def _():
-        part = jnp.dot(hidden_ref[...], down_ref[...], preferred_element_type=F32).astype(BF16)
-        for k in range(count):
-            outs[k][...] = part[k * each : (k + 1) * each]
+            outward(k, n).wait()
 
 
 def apply_expert(chunks, up_local, down_local):
     count = len(chunks)
     each, width = chunks[0].shape
     hidden = up_local.shape[1]
-    tile = next(t for t in (896, 512, 256, 128) if hidden % t == 0)
-    wide = 8 * LANES
-    first = hidden // tile
+    anywhere = pl.BlockSpec(memory_space=pl.ANY)
+    tiles = hidden // (2 * LANES if hidden % (2 * LANES) == 0 else LANES)
+    outs = width // (4 * LANES)
     return pl.pallas_call(
-        functools.partial(expert_kernel, count, first),
-        out_shape=[jax.ShapeDtypeStruct((each, width), BF16)] * count,
-        grid=(first + width // wide,),
-        in_specs=[pl.BlockSpec((each, width), lambda i: (0, 0))] * count
-        + [
-            pl.BlockSpec((width, tile), lambda i: (0, jnp.minimum(i, first - 1))),
-            pl.BlockSpec((hidden, wide), lambda i: (0, jnp.maximum(i - first, 0))),
-        ],
-        out_specs=[pl.BlockSpec((each, wide), lambda i: (0, jnp.maximum(i - first, 0)))] * count,
+        functools.partial(expert_kernel, count, 6),
+        out_shape=[pltpu.HBM((each, width), BF16)] * count,
+        in_specs=[VMEM] * count + [anywhere] * 2,
+        out_specs=[anywhere] * count,
         scratch_shapes=[
+            pltpu.VMEM(up_local.shape, BF16),
+            pltpu.VMEM(down_local.shape, BF16),
+            pltpu.VMEM((count * each, hidden), BF16),
             pltpu.VMEM((count * each, width), BF16),
-            pltpu.VMEM((count * each, hidden), BF16),
+            pltpu.SemaphoreType.DMA((tiles + outs,)),
+            pltpu.SemaphoreType.DMA((count, outs)),
         ],
         cost_estimate=pl.CostEstimate(
             flops=4 * count * each * width * hidden,
             bytes_accessed=4 * width * hidden + 4 * count * each * width,
             transcendentals=count * each * hidden,
         ),
+        compiler_params=pltpu.CompilerParams(vmem_limit_bytes=48 << 20),
         name="expert",
-    )(*chunks, up_local, down_local)
+    )(
+        *[resident(chunk) for chunk in chunks],
+        pltpu.with_memory_space_constraint(up_local, pltpu.HBM),
+        pltpu.with_memory_space_constraint(down_local, pltpu.HBM),
+    )
 
 
 def local(
@@ -491,7 +578,6 @@
             for i in range(near)
         ]
 
-    experts = router_weight.shape[1]
     holders = block_holder[0]
     indices = block_index[0]
     entries = holders.shape[0]
@@ -515,78 +601,65 @@
     known = jnp.where(entry < cached_blocks[0], 0.0, -1e30).astype(F32)
     known = jnp.repeat(known, BLOCK)[None, :]
     state_wanted = jnp.broadcast_to(state_index[0], (peers, 1))
-    mine = expert_ids.reshape(-1)
+    mine = expert_ids.reshape(1, -1)
+    count = mine.shape[1]
     ask = jnp.concatenate(
         [
+            jnp.broadcast_to(mine, (peers, count)),
             wanted.reshape(peers, slot),
             state_wanted,
-            jnp.broadcast_to(mine[None], (peers, mine.shape[0])),
         ],
         1,
     )
     asked = lax.all_to_all(ask, "dp", split_axis=0, concat_axis=0, tiled=True)
     place = lax.axis_index("dp")
 
-    def names_of(turn):
-        source = (place // near + 1) % 2 * near + (place % near + near - turn) % near
-        return lax.dynamic_index_in_dim(asked[:, slot + 1 :], source, 0, keepdims=False)
+    def source_of(turn):
+        return (place // near + 1) % 2 * near + (place % near + near - turn) % near
 
     states = state_pool.reshape(state_pool.shape[0], -1, LANES).astype(BF16)
-    packed = pack(asked[:, : slot + 1], block_pool, states)
+    packed = pack(asked[:, count:], block_pool, states)
     got = lax.all_to_all(packed, "dp", split_axis=0, concat_axis=0, tiled=True)
 
-    hot = one_hots(mine, experts)
-    pick = picker(hot)
+    router = router_weight.T
     sums, from_inputs, fade, keep = scan_local(
         scan_input, state_maps, step_size, step_decay, tokens
     )
-    mixed, normed, send, final_state = mix(
-        state_holder,
-        queries,
-        keys_values,
-        got,
-        known,
-        sums,
-        from_inputs,
-        fade,
-        keep,
-        state_maps,
-        norm_gain[None, :],
-        pick,
-    )
-    up_local = up_weight[0]
-    down_local = down_weight[0]
-
-    def gates(rows, names, hots):
-        return gate_weights(rows, router_weight, names.reshape(expert_ids.shape), hots)
+    mixed, normed, send, final_state, weights = mix(
+        state_holder, queries, keys_values, got, known, sums, from_inputs, fade, keep, state_maps,
+        norm_gain[None, :], mine, router,
+    )
+    up_local, down_local = up_weight[0], down_weight[0]
 
     far_rows = [move(normed, 0, 1)]
     near_in = swap_rows(send)
     near_moved = [move(near_in, turn, 0) for turn in range(1, near)]
     far_rows += [move(far_rows[0], turn, 0) for turn in range(1, near)]
-    far_names = [names_of(turn) for turn in range(near)]
-    far_hots = [one_hots(names, experts) for names in far_names]
-    far_in = []
+    far_in, far_weights = [], []
     for turn in range(near):
-        chosen = choose(far_rows[turn], picker(far_hots[turn]))
+        chosen, gates = choose(source_of(turn)[None], far_rows[turn], asked, router)
         far_in.append(swap_rows(chosen))
-
-    near_out, first_out = apply_expert([near_in, far_in[0]], up_local, down_local)
+        far_weights.append(gates)
+
+    def experts_on(rows):
+        return list(apply_expert(rows, up_local, down_local))
+
+    near_out, first_out = experts_on([near_in, far_in[0]])
     moved_out, far_out = [], [first_out]
     if near > 1:
-        moved_out += apply_expert(near_moved, up_local, down_local)
-        far_out += apply_expert(far_in[1:], up_local, down_local)
+        late = experts_on(near_moved + far_in[1:])
+        moved_out, far_out = late[: near - 1], far_out + late[near - 1 :]
 
     far_sums = []
     for turn in range(near):
-        weights = gates(far_rows[turn], far_names[turn], far_hots[turn])
         back = swap_rows(far_out[turn])
-        part = combine(back, weights)
+        part = combine(back, far_weights[turn])
         far_sums.append(move(part, near - turn, 1))
     moved_back = [move(rows, near - turn, 0) for turn, rows in enumerate(moved_out, 1)]
     joined = join(near_out, moved_back)
     near_back = swap_rows(joined)
-    layer_out = finish(near_back, gates(normed, mine, hot), mixed, far_sums)
+    base = settle(near_back, weights, mixed)
+    layer_out = finish(base, mixed, far_sums)
     return (layer_out, final_state.reshape(1, -1))
 
 

time: 266 us -> 247 us (0.929)
  the two profiles are of different devices: /device:TPU:10 before, /device:TPU:11 now
where the time goes in v3:
time: 247 us; the launch traced here: 246 us
  waiting for transfers between devices  124 us (50%)
  Pallas kernels  58.5 us (24%)
  starting transfers between devices  49 us (20%)
  local copies, waits for them, and re-layouts  7.78 us (3%)
  other arithmetic  3.58 us (1%)
  between operations  2.71 us (1%)
    ppermute x6, waiting for transfers between devices, move(): return lax.ppermute(rows, 'dp', route(turn, side))  89.4 us
    pallas_call x2, Pallas kernels, apply_expert(): pl.pallas_call(functools.partial(expert_kernel, count, 6), out_shape=[plt...  35 us
    all_to_all x6, starting transfers between devices, swap_rows(): lax.all_to_all(blocks, 'expert', split_axis=0, concat_axis=0, tiled=True)  29.9 us
    all_to_all x1, waiting for transfers between devices, local(): got = lax.all_to_all(packed, 'dp', split_axis=0, concat_axis=0, tiled=True)  23.1 us
    ppermute x6, starting transfers between devices, move(): return lax.ppermute(rows, 'dp', route(turn, side))  9.62 us
    all_to_all x6, waiting for transfers between devices, swap_rows(): lax.all_to_all(blocks, 'expert', split_axis=0, concat_axis=0, tiled=True)  9.47 us
    pallas_call x1, Pallas kernels, mix(): pl.pallas_call(mix_kernel, out_shape=(pltpu.HBM((length, width), BF16), j...  8.56 us
    unnamed x14, local copies, waits for them, and re-layouts  5.53 us
  transfers between devices with their start and end apart: 14, of which 8 were waited for; matrix products, arithmetic and copies ran while one was open for 2% of the time, Pallas kernels for 19%

profile of v3, /device:TPU:11, one launch (start us, length us, event | category | flops | bytes accessed | tf_op | source)
XLA Modules:
  0.0 245.5 jit_solution(14425459912403564163)
XLA Ops:
  0.6 0.0 copy-start.2
  1.3 0.9 convert_reduce_fusion
  2.2 0.7 fusion.1
  2.9 0.8 select_reduce_fusion
  3.7 0.1 reshape.56
  3.7 0.8 copy.33
  4.5 0.1 reshape.71
  4.7 0.1 pad.2.clone
  4.8 0.6 all_to_all.28
  5.4 4.8 %all-to-all-start = ((s32[4,1,133]{2,1,0:T(1,128)}), s32[4,1,133]{2,1,0:T(1,128)S(1)}, u32[]{:S(2)}, u32[]{:S(2)}) async-start(s32[4,1,133]{2,1,0:T(1,128)} %all_to_all.28), calls=%async_computation | async-start | bytes 8192 | tf_op jit(solution)/shard_map/all_to_all | solution.py:614
  10.1 1.2 convert_bitcast_fusion
  11.4 2.0 all-to-all-done
  13.4 0.0 copy-start
  13.4 1.0 copy-done
  14.4 2.3 pack.1
  16.8 4.7 %all-to-all-start.1 = ((bf16[4,96,2048]{2,1,0:T(8,128)(2,1)}), bf16[4,96,2048]{2,1,0:T(8,128)(2,1)S(1)}, u32[]{:S(2)}, u32[]{:S(2)}) async-start(bf16[4,96,2048]{2,1,0:T(8,128)(2,1)} %pack.1), calls=%async_computation.1 | async-start | bytes 3145728 | tf_op jit(solution)/shard_map/all_to_all | solution.py:622
  21.5 0.6 reshape.57.names_ref
  23.4 0.1 broadcast_in_dim.61
  23.5 0.6 broadcast_in_dim_reshape.3.known_ref
  24.1 1.4 copy.34.maps_ref
  25.5 4.8 %scan_local.1 = (f32[64,4096]{1,0:T(8,128)}, f32[512,128]{1,0:T(8,128)}, f32[64,64]{1,0:T(8,128)}, f32[1,64]{1,0:T(1,128)}) custom-call(bf16[64,4096]{1,0:T(8,128)(2,1)} %x_ref.1, f32[64,32]{1,0:T(8,128)} %copy.34.maps_ref, f32[64,64]{1,0:T(8,128)} %steps_ref.1, f32[64,64]{1,0:T(8,128)} %decays_ref.1, bf16[64,4096]{1,0:T(8,128)(2,1)} %tokens_ref.1), custom_call_target="tpu_custom_call" | custom-call | tf_op jit(solution)/shard_map/scan_local/pallas_call | solution.py:179
  30.3 23.1 %all-to-all-done.1.got_ref = bf16[4,96,2048]{2,1,0:T(8,128)(2,1)S(1)} async-done(((bf16[4,96,2048]{2,1,0:T(8,128)(2,1)}), bf16[4,96,2048]{2,1,0:T(8,128)(2,1)S(1)}, u32[]{:S(2)}, u32[]{:S(2)}) %all-to-all-start.1) | async-done | bytes 1572896 | tf_op jit(solution)/shard_map/all_to_all | solution.py:622
  53.4 8.6 %mix.1 = (bf16[64,4096]{1,0:T(8,128)(2,1)}, bf16[64,4096]{1,0:T(8,128)(2,1)}, bf16[128,4096]{1,0:T(8,128)(2,1)}, f32[512,128]{1,0:T(8,128)}, bf16[128,128]{1,0:T(8,128)(2,1)}) custom-call(s32[1]{0:T(128)S(6)} %copy.44.owner_ref, bf16[64,4096]{1,0:T(8,128)(2,1)} %q_ref.1, bf16[64,2048]{1,0:T(8,128)(2,1)} %kv_ref.1, ...), custom_call_target="tpu_custom_call" | custom-call | tf_op jit(solution)/shard_map/mix/pallas_call | solution.py:337
  62.0 6.8 %all-to-all-start.2 = ((bf16[8,16,4096]{2,1,0:T(8,128)(2,1)}), bf16[8,16,4096]{2,1,0:T(8,128)(2,1)S(1)}, u32[]{:S(2)}, u32[]{:S(2)}) async-start(bf16[8,16,4096]{2,1,0:T(8,128)(2,1)} %bitcast.56), calls=%async_computation.2 | async-start | bytes 2097152 | tf_op jit(solution)/shard_map/all_to_all | solution.py:591
  68.8 3.0 %collective-permute-start = (bf16[64,4096]{1,0:T(8,128)(2,1)}, bf16[64,4096]{1,0:T(8,128)(2,1)S(1)}, u32[]{:S(2)}, u32[]{:S(2)}) collective-permute-start(bf16[64,4096]{1,0:T(8,128)(2,1)} %get-tuple-element.24), channel_id=1, source_target_pairs={{0,16},{8,24},{16,0},{24,8},{1,17},{9,25},{17,1},{25,9},{2,18},{10... | collective-permute-start | bytes 1572872 | tf_op jit(solution)/shard_map/ppermute | solution.py:587
  71.8 22.9 %collective-permute-done.rows_ref = bf16[64,4096]{1,0:T(8,128)(2,1)S(1)} collective-permute-done((bf16[64,4096]{1,0:T(8,128)(2,1)}, bf16[64,4096]{1,0:T(8,128)(2,1)S(1)}, u32[]{:S(2)}, u32[]{:S(2)}) %collective-permute-start) | collective-permute-done | bytes 524320 | tf_op jit(solution)/shard_map/ppermute | solution.py:587
  94.8 0.0 copy-done.2
  94.8 1.7 choose.2
  96.5 0.0 all-to-all-done.2
  96.5 4.3 %all-to-all-start.3 = ((bf16[8,16,4096]{2,1,0:T(8,128)(2,1)}), bf16[8,16,4096]{2,1,0:T(8,128)(2,1)S(1)}, u32[]{:S(2)}, u32[]{:S(2)}) async-start(bf16[8,16,4096]{2,1,0:T(8,128)(2,1)} %bitcast.57), calls=%async_computation.3 | async-start | bytes 2097152 | tf_op jit(solution)/shard_map/all_to_all | solution.py:591
  100.8 2.1 collective-permute-start.2
  102.9 0.0 collective-permute-start.1
  102.9 11.9 %collective-permute-done.2.rows_ref = bf16[64,4096]{1,0:T(8,128)(2,1)S(1)} collective-permute-done((bf16[64,4096]{1,0:T(8,128)(2,1)S(1)}, bf16[64,4096]{1,0:T(8,128)(2,1)S(1)}, u32[]{:S(2)}, u32[]{:S(2)}) %collective-permute-start.2) | collective-permute-done | bytes 524320 | tf_op jit(solution)/shard_map/ppermute | solution.py:587
  114.8 1.7 choose.3
  116.5 0.0 all-to-all-done.3
  116.5 5.3 %all-to-all-start.4 = ((bf16[8,16,4096]{2,1,0:T(8,128)(2,1)}), bf16[8,16,4096]{2,1,0:T(8,128)(2,1)S(1)}, u32[]{:S(2)}, u32[]{:S(2)}) async-start(bf16[8,16,4096]{2,1,0:T(8,128)(2,1)} %bitcast.60), calls=%async_computation.4 | async-start | bytes 2097152 | tf_op jit(solution)/shard_map/all_to_all | solution.py:591
  121.9 16.9 %expert.2 = (bf16[128,4096]{1,0:T(8,128)(2,1)}, bf16[128,4096]{1,0:T(8,128)(2,1)}) custom-call(bf16[128,4096]{1,0:T(8,128)(2,1)S(1)} %bitcast.39, bf16[128,4096]{1,0:T(8,128)(2,1)S(1)} %bitcast.40, bf16[4096,1792]{1,0:T(8,128)(2,1)} %bitcast.52, bf16[1792,4096]{1,0:T(8,128)(2,1)} %bitcast.54), custom_call_target="tpu_custom_call" | custom-call | flops 7516192768 | bytes 33554432 | tf_op jit(solution)/shard_map/expert/pallas_call | solution.py:522
  138.8 0.0 all-to-all-done.4
  138.8 4.2 %all-to-all-start.6 = ((bf16[8,16,4096]{2,1,0:T(8,128)(2,1)}), bf16[8,16,4096]{2,1,0:T(8,128)(2,1)S(1)}, u32[]{:S(2)}, u32[]{:S(2)}) async-start(bf16[8,16,4096]{2,1,0:T(8,128)(2,1)} %bitcast.58), calls=%async_computation.6 | async-start | bytes 2097152 | tf_op jit(solution)/shard_map/all_to_all | solution.py:591
  143.0 0.0 collective-permute-done.1.refs_0_
  143.0 0.0 copy-start.4
  143.0 18.1 %expert.3 = (bf16[128,4096]{1,0:T(8,128)(2,1)}, bf16[128,4096]{1,0:T(8,128)(2,1)}) custom-call(bf16[128,4096]{1,0:T(8,128)(2,1)} %collective-permute-done.1.refs_0_, bf16[128,4096]{1,0:T(8,128)(2,1)S(1)} %bitcast.41, bf16[4096,1792]{1,0:T(8,128)(2,1)} %bitcast.53, bf16[1792,4096]{1,0:T(8,128)(2,1)} %bitcast.55), custom_call_target="tpu_custom_call" | custom-call | flops 7516192768 | bytes 33554432 | tf_op jit(solution)/shard_map/expert/pallas_call | solution.py:522
  161.2 1.8 collective-permute-start.3
  163.0 0.0 all-to-all-done.6
  163.0 4.5 %all-to-all-start.7 = ((bf16[8,16,4096]{2,1,0:T(8,128)(2,1)}), bf16[8,16,4096]{2,1,0:T(8,128)(2,1)S(1)}, u32[]{:S(2)}, u32[]{:S(2)}) async-start(bf16[8,16,4096]{2,1,0:T(8,128)(2,1)} %bitcast.59), calls=%async_computation.7 | async-start | bytes 2097152 | tf_op jit(solution)/shard_map/all_to_all | solution.py:591
  167.5 18.9 %collective-permute-done.3.refs_1_ = bf16[128,4096]{1,0:T(8,128)(2,1)S(1)} collective-permute-done((bf16[128,4096]{1,0:T(8,128)(2,1)}, bf16[128,4096]{1,0:T(8,128)(2,1)S(1)}, u32[]{:S(2)}, u32[]{:S(2)}) %collective-permute-start.3) | collective-permute-done | bytes 1048608 | tf_op jit(solution)/shard_map/ppermute | solution.py:587
  186.3 0.0 copy-start.1
  186.3 1.2 copy-done.1
  187.6 1.2 shard_map.194
  188.8 0.0 all-to-all-done.7
  188.8 4.8 %all-to-all-start.5 = ((bf16[8,16,4096]{2,1,0:T(8,128)(2,1)}), bf16[8,16,4096]{2,1,0:T(8,128)(2,1)S(1)}, u32[]{:S(2)}, u32[]{:S(2)}) async-start(bf16[8,16,4096]{2,1,0:T(8,128)(2,1)} %bitcast.18), calls=%async_computation.5 | async-start | bytes 2097152 | tf_op jit(solution)/shard_map/all_to_all | solution.py:591
  193.6 1.2 shard_map.196
  194.8 2.4 collective-permute-start.4
  197.2 0.4 shard_map.197
  197.6 0.3 collective-permute-start.5
  197.9 9.5 %all-to-all-done.5 = bf16[8,16,4096]{2,1,0:T(8,128)(2,1)S(1)} async-done(((bf16[8,16,4096]{2,1,0:T(8,128)(2,1)}), bf16[8,16,4096]{2,1,0:T(8,128)(2,1)S(1)}, u32[]{:S(2)}, u32[]{:S(2)}) %all-to-all-start.5) | async-done | bytes 1048608 | tf_op jit(solution)/shard_map/all_to_all | solution.py:591
  207.4 0.0 copy-done.4
  207.4 0.4 shard_map.195.refs_0_
  207.8 23.5 %collective-permute-done.4.refs_2_ = bf16[64,4096]{1,0:T(8,128)(2,1)S(1)} collective-permute-done((bf16[64,4096]{1,0:T(8,128)(2,1)}, bf16[64,4096]{1,0:T(8,128)(2,1)S(1)}, u32[]{:S(2)}, u32[]{:S(2)}) %collective-permute-start.4) | collective-permute-done | bytes 524320 | tf_op jit(solution)/shard_map/ppermute | solution.py:587
  231.3 12.1 %collective-permute-done.5.refs_3_ = bf16[64,4096]{1,0:T(8,128)(2,1)S(1)} collective-permute-done((bf16[64,4096]{1,0:T(8,128)(2,1)S(1)}, bf16[64,4096]{1,0:T(8,128)(2,1)S(1)}, u32[]{:S(2)}, u32[]{:S(2)}) %collective-permute-start.5) | collective-permute-done | bytes 524320 | tf_op jit(solution)/shard_map/ppermute | solution.py:587
  243.5 0.0 copy-start.3
  243.5 1.0 copy-done.3
  244.5 1.0 shard_map.198
  (6 shorter events, 0.1 us)
Async XLA Ops:
  0.6 94.1 %copy-start.2 = (bf16[4096,8]{0,1:T(8,128)(2,1)S(1)}, bf16[4096,8]{0,1:T(8,128)(2,1)}, u32[]{:S(2)}) copy-start(bf16[4096,8]{0,1:T(8,128)(2,1)} %param.34) | copy-start | bytes 196612
  5.4 8.0 %all-to-all-start = ((s32[4,1,133]{2,1,0:T(1,128)}), s32[4,1,133]{2,1,0:T(1,128)S(1)}, u32[]{:S(2)}, u32[]{:S(2)}) async-start(s32[4,1,133]{2,1,0:T(1,128)} %all_to_all.28), calls=%async_computation | async-start | bytes 8192 | tf_op jit(solution)/shard_map/all_to_all | solution.py:614
  13.4 1.0 copy-start
  16.8 36.7 %all-to-all-start.1 = ((bf16[4,96,2048]{2,1,0:T(8,128)(2,1)}), bf16[4,96,2048]{2,1,0:T(8,128)(2,1)S(1)}, u32[]{:S(2)}, u32[]{:S(2)}) async-start(bf16[4,96,2048]{2,1,0:T(8,128)(2,1)} %pack.1), calls=%async_computation.1 | async-start | bytes 3145728 | tf_op jit(solution)/shard_map/all_to_all | solution.py:622
  62.0 34.5 %all-to-all-start.2 = ((bf16[8,16,4096]{2,1,0:T(8,128)(2,1)}), bf16[8,16,4096]{2,1,0:T(8,128)(2,1)S(1)}, u32[]{:S(2)}, u32[]{:S(2)}) async-start(bf16[8,16,4096]{2,1,0:T(8,128)(2,1)} %bitcast.56), calls=%async_computation.2 | async-start | bytes 2097152 | tf_op jit(solution)/shard_map/all_to_all | solution.py:591
  68.8 25.9 %collective-permute-start = (bf16[64,4096]{1,0:T(8,128)(2,1)}, bf16[64,4096]{1,0:T(8,128)(2,1)S(1)}, u32[]{:S(2)}, u32[]{:S(2)}) collective-permute-start(bf16[64,4096]{1,0:T(8,128)(2,1)} %get-tuple-element.24), channel_id=1, source_target_pairs={{0,16},{8,24},{16,0},{24,8},{1,17},{9,25},{17,1},{25,9},{2,18},{10... | collective-permute-start | bytes 1572872 | tf_op jit(solution)/shard_map/ppermute | solution.py:587
  96.5 20.0 %all-to-all-start.3 = ((bf16[8,16,4096]{2,1,0:T(8,128)(2,1)}), bf16[8,16,4096]{2,1,0:T(8,128)(2,1)S(1)}, u32[]{:S(2)}, u32[]{:S(2)}) async-start(bf16[8,16,4096]{2,1,0:T(8,128)(2,1)} %bitcast.57), calls=%async_computation.3 | async-start | bytes 2097152 | tf_op jit(solution)/shard_map/all_to_all | solution.py:591
  100.8 14.0 %collective-permute-start.2 = (bf16[64,4096]{1,0:T(8,128)(2,1)S(1)}, bf16[64,4096]{1,0:T(8,128)(2,1)S(1)}, u32[]{:S(2)}, u32[]{:S(2)}) collective-permute-start(bf16[64,4096]{1,0:T(8,128)(2,1)S(1)} %collective-permute-done.rows_ref), channel_id=1, source_target_pairs={{0,8},{8,0},{16,24},{24,16},{1,9},{9,1},{17,25},{25,17},{2,10},{10... | collective-permute-start | bytes 1572872 | tf_op jit(solution)/shard_map/ppermute | solution.py:587
  102.9 40.1 %collective-permute-start.1 = (bf16[128,4096]{1,0:T(8,128)(2,1)S(1)}, bf16[128,4096]{1,0:T(8,128)(2,1)}, u32[]{:S(2)}, u32[]{:S(2)}) collective-permute-start(bf16[128,4096]{1,0:T(8,128)(2,1)S(1)} %bitcast.38), channel_id=1, source_target_pairs={{0,8},{8,0},{16,24},{24,16},{1,9},{9,1},{17,25},{25,17},{2,10},{10... | collective-permute-start | bytes 3145736 | tf_op jit(solution)/shard_map/ppermute | solution.py:587
  116.5 22.3 %all-to-all-start.4 = ((bf16[8,16,4096]{2,1,0:T(8,128)(2,1)}), bf16[8,16,4096]{2,1,0:T(8,128)(2,1)S(1)}, u32[]{:S(2)}, u32[]{:S(2)}) async-start(bf16[8,16,4096]{2,1,0:T(8,128)(2,1)} %bitcast.60), calls=%async_computation.4 | async-start | bytes 2097152 | tf_op jit(solution)/shard_map/all_to_all | solution.py:591
  138.8 24.2 %all-to-all-start.6 = ((bf16[8,16,4096]{2,1,0:T(8,128)(2,1)}), bf16[8,16,4096]{2,1,0:T(8,128)(2,1)S(1)}, u32[]{:S(2)}, u32[]{:S(2)}) async-start(bf16[8,16,4096]{2,1,0:T(8,128)(2,1)} %bitcast.58), calls=%async_computation.6 | async-start | bytes 2097152 | tf_op jit(solution)/shard_map/all_to_all | solution.py:591
  143.0 64.4 %copy-start.4 = (bf16[128,128]{1,0:T(8,128)(2,1)S(1)}, bf16[128,128]{1,0:T(8,128)(2,1)}, u32[]{:S(2)}) copy-start(bf16[128,128]{1,0:T(8,128)(2,1)} %get-tuple-element.29.refs_1_) | copy-start | bytes 98308
  161.2 25.2 %collective-permute-start.3 = (bf16[128,4096]{1,0:T(8,128)(2,1)}, bf16[128,4096]{1,0:T(8,128)(2,1)S(1)}, u32[]{:S(2)}, u32[]{:S(2)}) collective-permute-start(bf16[128,4096]{1,0:T(8,128)(2,1)} %get-tuple-element.28), channel_id=1, source_target_pairs={{0,8},{8,0},{16,24},{24,16},{1,9},{9,1},{17,25},{25,17},{2,10},{10... | collective-permute-start | bytes 3145736 | tf_op jit(solution)/shard_map/ppermute | solution.py:587
  163.0 25.8 %all-to-all-start.7 = ((bf16[8,16,4096]{2,1,0:T(8,128)(2,1)}), bf16[8,16,4096]{2,1,0:T(8,128)(2,1)S(1)}, u32[]{:S(2)}, u32[]{:S(2)}) async-start(bf16[8,16,4096]{2,1,0:T(8,128)(2,1)} %bitcast.59), calls=%async_computation.7 | async-start | bytes 2097152 | tf_op jit(solution)/shard_map/all_to_all | solution.py:591
  186.3 1.2 copy-start.1
  188.8 18.6 %all-to-all-start.5 = ((bf16[8,16,4096]{2,1,0:T(8,128)(2,1)}), bf16[8,16,4096]{2,1,0:T(8,128)(2,1)S(1)}, u32[]{:S(2)}, u32[]{:S(2)}) async-start(bf16[8,16,4096]{2,1,0:T(8,128)(2,1)} %bitcast.18), calls=%async_computation.5 | async-start | bytes 2097152 | tf_op jit(solution)/shard_map/all_to_all | solution.py:591
  194.8 36.5 %collective-permute-start.4 = (bf16[64,4096]{1,0:T(8,128)(2,1)}, bf16[64,4096]{1,0:T(8,128)(2,1)S(1)}, u32[]{:S(2)}, u32[]{:S(2)}) collective-permute-start(bf16[64,4096]{1,0:T(8,128)(2,1)} %shard_map.196), channel_id=1, source_target_pairs={{0,16},{8,24},{16,0},{24,8},{1,17},{9,25},{17,1},{25,9},{2,18},{10... | collective-permute-start | bytes 1572872 | tf_op jit(solution)/shard_map/ppermute | solution.py:587
  197.6 45.9 %collective-permute-start.5 = (bf16[64,4096]{1,0:T(8,128)(2,1)S(1)}, bf16[64,4096]{1,0:T(8,128)(2,1)S(1)}, u32[]{:S(2)}, u32[]{:S(2)}) collective-permute-start(bf16[64,4096]{1,0:T(8,128)(2,1)S(1)} %shard_map.197), channel_id=1, source_target_pairs={{0,24},{8,16},{16,8},{24,0},{1,25},{9,17},{17,9},{25,1},{2,26},{10... | collective-permute-start | bytes 1572872 | tf_op jit(solution)/shard_map/ppermute | solution.py:587
  243.5 1.0 copy-start.3

commit v4 on v3

--- a/solution.py
+++ b/solution.py
@@ -15,6 +15,8 @@
 NSTATE = 16
 BLOCK = 16
 LANES = 128
+UP_SHARES = (1, 2, 2, 2)
+DOWN_SHARES = (4, 2, 1, 1)
 HIGH = lax.Precision.HIGHEST
 F32 = jnp.float32
 BF16 = jnp.bfloat16
@@ -79,6 +81,67 @@
     total = lifted[0] + lifted[1]
     weights = sum(hot * (lift / total) for hot, lift in zip(hots, lifted))
     return split_rows(weights)
+
+
+def turned(row):
+    count = row.shape[1]
+    sub = lax.broadcasted_iota(jnp.int32, (count, count), 0)
+    lane = lax.broadcasted_iota(jnp.int32, (count, count), 1)
+    return jnp.sum(
+        jnp.where(sub == lane, jnp.broadcast_to(row, (count, count)), 0.0), axis=1, keepdims=True
+    )
+
+
+def plan_kernel(slot, holders_ref, indices_ref, cached_ref, state_ref, names_ref, ask_ref, known_ref):
+    peers = ask_ref.shape[0]
+    entries = holders_ref.shape[1]
+    holders = holders_ref[...].astype(F32)
+    square = (entries, entries)
+    sub = lax.broadcasted_iota(jnp.int32, square, 0)
+    lane = lax.broadcasted_iota(jnp.int32, square, 1)
+    same = jnp.where(
+        (turned(holders) == jnp.broadcast_to(holders, square)) & (sub < lane), 1.0, 0.0
+    )
+    seats = turned(holders * slot + jnp.sum(same, axis=0, keepdims=True))
+    indices = turned(indices_ref[...].astype(F32))
+    length = names_ref.shape[1]
+    count = 2 * length
+    names = [turned(names_ref[j : j + 1, :].astype(F32)) for j in range(2)]
+    token = lax.broadcasted_iota(jnp.int32, (length, count), 0)
+    at = lax.broadcasted_iota(jnp.int32, (length, count), 1)
+    laid = sum(
+        jnp.where(at == 2 * token + j, jnp.broadcast_to(names[j], (length, count)), 0.0)
+        for j in range(2)
+    )
+    laid = jnp.sum(laid, axis=0, keepdims=True)
+    spots = lax.broadcasted_iota(jnp.int32, (entries, LANES), 1)
+    wide = jnp.broadcast_to(indices, (entries, LANES))
+    for j in range(peers):
+        here = (seats == (spots + j * slot).astype(F32)) & (spots < slot)
+        asks = jnp.sum(jnp.where(here, wide, 0.0), axis=0, keepdims=True)
+        asks = jnp.where(spots[:1] == slot, state_ref[0].astype(F32), asks)
+        ask_ref[j, 0:1, :] = jnp.concatenate([laid, asks], 1).astype(jnp.int32)
+    past = known_ref.shape[1]
+    spots = lax.broadcasted_iota(jnp.int32, (entries, past), 1) // BLOCK
+    order = lax.broadcasted_iota(jnp.int32, (entries, past), 0).astype(F32)
+    entry = jnp.sum(
+        jnp.where(seats == spots.astype(F32), order, 0.0), axis=0, keepdims=True
+    )
+    known_ref[...] = jnp.where(entry < cached_ref[0].astype(F32), 0.0, -1e30)
+
+
+def plan(peers, holders, indices, cached, state, names):
+    entries = holders.shape[1]
+    return pl.pallas_call(
+        functools.partial(plan_kernel, entries // peers),
+        out_shape=(
+            jax.ShapeDtypeStruct((peers, 1, 2 * names.shape[1] + LANES), jnp.int32),
+            jax.ShapeDtypeStruct((1, entries * BLOCK), F32),
+        ),
+        in_specs=[VMEM, VMEM, SMEM, SMEM, VMEM],
+        out_specs=(VMEM, VMEM),
+        name="plan",
+    )(holders, indices, cached, state, names)
 
 
 def pack_kernel(slot, *refs):
@@ -305,7 +368,7 @@
     mean = jnp.sum(squares, axis=1, keepdims=True) * (1.0 / width)
     scale = lax.rsqrt(mean + 1e-05)
     experts = router_ref.shape[0]
-    hots = hots_of(names_ref[...], names_ref.shape[1] // experts)
+    hots = hots_of(names_ref[:, : 2 * length], 2 * length // experts)
     pick = (hots[0] + hots[1]).astype(BF16)
     logits = jnp.zeros((length, experts), F32)
     step = 4 * LANES
@@ -330,9 +393,9 @@
 
 
 def mix(owner, *arrays):
-    queries, local, names = arrays[0], arrays[5], arrays[10]
+    queries, local = arrays[0], arrays[5]
     length, width = queries.shape
-    count = names.shape[1]
+    count = 2 * length
     anywhere = pl.BlockSpec(memory_space=pl.ANY)
     return pl.pallas_call(
         mix_kernel,
@@ -434,82 +497,124 @@
     return stream(body, [parts], [weights], weights.shape[0] // 2)
 
 
-def settle(parts, weights, mixed):
-    def body(held, weights):
-        return weighed(held[0], weights)
-
-    return stream(body, [parts], [weights], mixed.shape[0], dtype=F32)
-
-
-def finish(base, mixed, sums):
-    def body(held):
-        total = held[0]
-        for far in held[2:]:
-            total = total + far.astype(F32)
-        return (held[1].astype(F32) + total).astype(BF16)
-
-    return stream(body, [base, mixed] + sums, [], mixed.shape[0], keep=False)
+def held_kernel(body, arrays, *refs):
+    held, far_ref, out_ref = refs[:arrays], refs[arrays], refs[arrays + 1]
+    near_ref, made_ref, sem, out_sems = refs[arrays + 2 :]
+    chunks = out_sems.shape[0]
+    step = out_ref.shape[1] // chunks
+    copy = pltpu.make_async_copy(far_ref, near_ref, sem)
+    copy.start()
+    outs = []
+    for c in range(chunks):
+        cols = slice(c * step, (c + 1) * step)
+        made = body(cols, *held)
+        if c == 0:
+            copy.wait()
+        made_ref[:, cols] = (made + near_ref[:, cols].astype(F32)).astype(BF16)
+        outs.append(
+            pltpu.make_async_copy(made_ref.at[:, cols], out_ref.at[:, cols], out_sems.at[c])
+        )
+        outs[-1].start()
+    for out in outs:
+        out.wait()
+
+
+def held_call(body, arrays, far, chunks=4):
+    anywhere = pl.BlockSpec(memory_space=pl.ANY)
+    return pl.pallas_call(
+        functools.partial(held_kernel, body, len(arrays)),
+        out_shape=pltpu.HBM(far.shape, BF16),
+        in_specs=[VMEM] * len(arrays) + [anywhere],
+        out_specs=anywhere,
+        scratch_shapes=[
+            pltpu.VMEM(far.shape, BF16),
+            pltpu.VMEM(far.shape, BF16),
+            pltpu.SemaphoreType.DMA,
+            pltpu.SemaphoreType.DMA((chunks,)),
+        ],
+        compiler_params=pltpu.CompilerParams(vmem_limit_bytes=16 << 20),
+    )(*[resident(array) for array in arrays], pltpu.with_memory_space_constraint(far, pltpu.HBM))
+
+
+def finish(parts, weights, sums, mixed):
+    def body(cols, parts_ref, weights_ref, *sums_refs):
+        total = weighed(parts_ref[:, cols], weights_ref[...])
+        for ref in sums_refs:
+            total = total + ref[:, cols].astype(F32)
+        return total
+
+    return held_call(body, [parts, weights] + sums, mixed)
 
 
 def join(first, others):
     if not others:
         return first
 
-    def body(held):
-        return sum(part.astype(F32) for part in held).astype(BF16)
-
-    return stream(body, [first] + others, [], first.shape[0])
-
-
-def expert_kernel(count, ahead, *refs):
+    def body(cols, *refs):
+        return sum(ref[:, cols].astype(F32) for ref in refs)
+
+    return held_call(body, others, first)
+
+
+def expert_kernel(count, ups, downs, *refs):
     sources = refs[:count]
     up_hbm, down_hbm = refs[count : count + 2]
     outs = refs[count + 2 : 2 * count + 2]
     up_ref, down_ref, hidden_ref, made_ref, sems, out_sems = refs[2 * count + 2 :]
-    each, width = sources[0].shape
-    tile = 2 * LANES if up_ref.shape[1] % (2 * LANES) == 0 else LANES
-    wide = 4 * LANES
-    first, second = up_ref.shape[1] // tile, width // wide
-
-    def inward(n):
-        if n < first:
-            cols = pl.ds(n * tile, tile)
-            pair = up_hbm.at[:, cols], up_ref.at[:, cols]
-        else:
-            cols = pl.ds((n - first) * wide, wide)
-            pair = down_hbm.at[:, cols], down_ref.at[:, cols]
-        return pltpu.make_async_copy(*pair, sems.at[n])
-
-    def outward(k, n):
-        cols = pl.ds(n * wide, wide)
-        return pltpu.make_async_copy(
-            made_ref.at[pl.ds(k * each, each), cols], outs[k].at[:, cols], out_sems.at[k, n]
-        )
-
-    for n in range(min(ahead, first + second)):
-        inward(n).start()
+    each, _ = sources[0].shape
+    copies = [
+        pltpu.make_async_copy(
+            hbm.at[:, pl.ds(start, size)], ref.at[:, pl.ds(start, size)], sems.at[base + n]
+        )
+        for hbm, ref, blocks, base in (
+            (up_hbm, up_ref, ups, 0),
+            (down_hbm, down_ref, downs, len(ups)),
+        )
+        for n, (start, size) in enumerate(blocks)
+    ]
+    for copy in copies:
+        copy.start()
     if count == 1:
         rows = sources[0][...]
     else:
         rows = jnp.concatenate([source[...] for source in sources], 0)
-    for n in range(first + second):
-        inward(n).wait()
-        if n + ahead < first + second:
-            inward(n + ahead).start()
-        if n < first:
-            cols = slice(n * tile, (n + 1) * tile)
+    tile = 2 * LANES
+    for (start, size), copy in zip(ups, copies):
+        copy.wait()
+        for at in range(start, start + size, tile):
+            cols = slice(at, min(at + tile, start + size))
             lifted = jnp.dot(rows, up_ref[:, cols], preferred_element_type=F32)
             hidden_ref[:, cols] = (lifted / (1.0 + jnp.exp(-lifted))).astype(BF16)
-        else:
-            cols = slice((n - first) * wide, (n - first + 1) * wide)
+    hidden = hidden_ref[...]
+    tile = 4 * LANES
+    flying = []
+    for n, ((start, size), copy) in enumerate(zip(downs, copies[len(ups) :])):
+        copy.wait()
+        for at in range(start, start + size, tile):
+            cols = slice(at, at + tile)
             made_ref[:, cols] = jnp.dot(
-                hidden_ref[...], down_ref[:, cols], preferred_element_type=F32
+                hidden, down_ref[:, cols], preferred_element_type=F32
             ).astype(BF16)
-            for k in range(count):
-                outward(k, n - first).start()
-    for n in range(second):
         for k in range(count):
-            outward(k, n).wait()
+            cols = pl.ds(start, size)
+            flying.append(
+                pltpu.make_async_copy(
+                    made_ref.at[pl.ds(k * each, each), cols],
+                    outs[k].at[:, cols],
+                    out_sems.at[k, n],
+                )
+            )
+            flying[-1].start()
+    for copy in flying:
+        copy.wait()
+
+
+def blocks_of(total, shares):
+    unit = total // sum(shares)
+    if unit % LANES or unit * sum(shares) != total:
+        return [(0, total)]
+    ends = [unit * sum(shares[: n + 1]) for n in range(len(shares))]
+    return [(end - unit * share, unit * share) for end, share in zip(ends, shares)]
 
 
 def apply_expert(chunks, up_local, down_local):
@@ -517,10 +622,10 @@
     each, width = chunks[0].shape
     hidden = up_local.shape[1]
     anywhere = pl.BlockSpec(memory_space=pl.ANY)
-    tiles = hidden // (2 * LANES if hidden % (2 * LANES) == 0 else LANES)
-    outs = width // (4 * LANES)
+    ups = blocks_of(hidden, UP_SHARES)
+    downs = blocks_of(width, DOWN_SHARES)
     return pl.pallas_call(
-        functools.partial(expert_kernel, count, 6),
+        functools.partial(expert_kernel, count, ups, downs),
         out_shape=[pltpu.HBM((each, width), BF16)] * count,
         in_specs=[VMEM] * count + [anywhere] * 2,
         out_specs=[anywhere] * count,
@@ -529,15 +634,15 @@
             pltpu.VMEM(down_local.shape, BF16),
             pltpu.VMEM((count * each, hidden), BF16),
             pltpu.VMEM((count * each, width), BF16),
-            pltpu.SemaphoreType.DMA((tiles + outs,)),
-            pltpu.SemaphoreType.DMA((count, outs)),
+            pltpu.SemaphoreType.DMA((len(ups) + len(downs),)),
+            pltpu.SemaphoreType.DMA((count, len(downs))),
         ],
         cost_estimate=pl.CostEstimate(
             flops=4 * count * each * width * hidden,
             bytes_accessed=4 * width * hidden + 4 * count * each * width,
             transcendentals=count * each * hidden,
         ),
-        compiler_params=pltpu.CompilerParams(vmem_limit_bytes=48 << 20),
+        compiler_params=pltpu.CompilerParams(vmem_limit_bytes=50 << 20),
         name="expert",
     )(
         *[resident(chunk) for chunk in chunks],
@@ -578,11 +683,6 @@
             for i in range(near)
         ]
 
-    holders = block_holder[0]
-    indices = block_index[0]
-    entries = holders.shape[0]
-    slot = entries // peers
-
     def move(rows, turn, side):
         return lax.ppermute(rows, "dp", route(turn, side))
 
@@ -591,34 +691,17 @@
         moved = lax.all_to_all(blocks, "expert", split_axis=0, concat_axis=0, tiled=True)
         return moved.reshape(rows.shape)
 
-    places = jnp.arange(entries, dtype=jnp.int32)
-    same = holders[:, None] == holders[None, :]
-    rank = jnp.sum((same & (places[None, :] < places[:, None])).astype(jnp.int32), axis=1)
-    seat = holders * slot + rank
-    at_seat = seat[None, :] == places[:, None]
-    wanted = jnp.sum(jnp.where(at_seat, indices[None, :], 0), axis=1)
-    entry = jnp.sum(jnp.where(at_seat, places[None, :], 0), axis=1)
-    known = jnp.where(entry < cached_blocks[0], 0.0, -1e30).astype(F32)
-    known = jnp.repeat(known, BLOCK)[None, :]
-    state_wanted = jnp.broadcast_to(state_index[0], (peers, 1))
-    mine = expert_ids.reshape(1, -1)
-    count = mine.shape[1]
-    ask = jnp.concatenate(
-        [
-            jnp.broadcast_to(mine, (peers, count)),
-            wanted.reshape(peers, slot),
-            state_wanted,
-        ],
-        1,
-    )
-    asked = lax.all_to_all(ask, "dp", split_axis=0, concat_axis=0, tiled=True)
+    slot = block_holder.shape[1] // peers
+    count = 2 * expert_ids.shape[0]
+    ask, known = plan(peers, block_holder, block_index, cached_blocks, state_index, expert_ids.T)
+    asked = lax.all_to_all(ask, "dp", split_axis=0, concat_axis=0, tiled=True)[:, 0]
     place = lax.axis_index("dp")
 
     def source_of(turn):
         return (place // near + 1) % 2 * near + (place % near + near - turn) % near
 
     states = state_pool.reshape(state_pool.shape[0], -1, LANES).astype(BF16)
-    packed = pack(asked[:, count:], block_pool, states)
+    packed = pack(asked[:, count : count + slot + 1], block_pool, states)
     got = lax.all_to_all(packed, "dp", split_axis=0, concat_axis=0, tiled=True)
 
     router = router_weight.T
@@ -627,7 +710,7 @@
     )
     mixed, normed, send, final_state, weights = mix(
         state_holder, queries, keys_values, got, known, sums, from_inputs, fade, keep, state_maps,
-        norm_gain[None, :], mine, router,
+        norm_gain[None, :], ask[0], router,
     )
     up_local, down_local = up_weight[0], down_weight[0]
 
@@ -658,8 +741,7 @@
     moved_back = [move(rows, near - turn, 0) for turn, rows in enumerate(moved_out, 1)]
     joined = join(near_out, moved_back)
     near_back = swap_rows(joined)
-    base = settle(near_back, weights, mixed)
-    layer_out = finish(base, mixed, far_sums)
+    layer_out = finish(near_back, weights, far_sums, mixed)
     return (layer_out, final_state.reshape(1, -1))
 
 

time: 247 us -> 238 us (0.964)
  Pallas kernels: 58.5 us -> 53.5 us
  local copies, waits for them, and re-layouts: 7.78 us -> 3.76 us
    ppermute x6, waiting for transfers between devices: 89.4 us -> 99 us  [move(): return lax.ppermute(rows, 'dp', route(turn, side))]
    all_to_all x6, waiting for transfers between devices: 9.47 us -> 0.75 us  [swap_rows(): lax.all_to_all(blocks, 'expert', split_axis=0, concat_axis=0, tiled=True)]
    pallas_call x5 -> x2, Pallas kernels: 4.32 us -> 0.83 us  [stream(): pl.pallas_call(functools.partial(stream_kernel, body, len(arrays), chunks...]
    unnamed x14 -> x9, local copies, waits for them, and re-layouts: 5.53 us -> 2.49 us
    pallas_call x2 -> x5, Pallas kernels: 35 us -> 33.5 us  [the longest x2 27.6 us: apply_expert(): pl.pallas_call(functools.partial(expert_kernel, count, ups, downs), out_s...]
  transfers between devices with their start and end apart: 14 -> 14, of which waited for: 8 -> 8; matrix products, arithmetic and copies ran while one was open for 2% -> 2% of each run, Pallas kernels for 19% -> 16%
where the time goes in v4:
time: 238 us; the launch traced here: 237 us
  waiting for transfers between devices  126 us (53%)
  Pallas kernels  53.5 us (22%)
  starting transfers between devices  49.8 us (21%)
  local copies, waits for them, and re-layouts  3.76 us (2%)
  between operations  2.88 us (1%)
    ppermute x6, waiting for transfers between devices, move(): return lax.ppermute(rows, 'dp', route(turn, side))  99 us
    all_to_all x6, starting transfers between devices, swap_rows(): lax.all_to_all(blocks, 'expert', split_axis=0, concat_axis=0, tiled=True)  30.7 us
    pallas_call x2, Pallas kernels, apply_expert(): pl.pallas_call(functools.partial(expert_kernel, count, ups, downs), out_s...  27.6 us
    all_to_all x1, waiting for transfers between devices, local(): got = lax.all_to_all(packed, 'dp', split_axis=0, concat_axis=0, tiled=True)  23.9 us
    ppermute x6, starting transfers between devices, move(): return lax.ppermute(rows, 'dp', route(turn, side))  9.7 us
    pallas_call x1, Pallas kernels, mix(): pl.pallas_call(mix_kernel, out_shape=(pltpu.HBM((length, width), BF16), j...  8.56 us
  transfers between devices with their start and end apart: 14, of which 8 were waited for; matrix products, arithmetic and copies ran while one was open for 2% of the time, Pallas kernels for 16%

profile of v4, /device:TPU:11, one launch (start us, length us, event | category | flops | bytes accessed | tf_op | source)
XLA Modules:
  0.0 236.9 jit_solution(17334298552363996739)
XLA Ops:
  0.6 0.0 copy-start.1
  2.0 1.5 plan.1
  3.5 4.8 %all-to-all-start = ((s32[4,1,256]{2,1,0:T(1,128)}), s32[4,1,256]{2,1,0:T(1,128)S(1)}, u32[]{:S(2)}, u32[]{:S(2)}) async-start(s32[4,1,256]{2,1,0:T(1,128)} %get-tuple-element.21), calls=%async_computation | async-start | bytes 8192 | tf_op jit(solution)/shard_map/all_to_all | solution.py:697
  8.2 1.2 convert_bitcast_fusion
  9.5 2.0 all-to-all-done
  11.5 0.0 copy-start
  11.5 1.0 copy-done
  12.5 2.4 pack.1
  14.9 4.7 %all-to-all-start.1 = ((bf16[4,96,2048]{2,1,0:T(8,128)(2,1)}), bf16[4,96,2048]{2,1,0:T(8,128)(2,1)S(1)}, u32[]{:S(2)}, u32[]{:S(2)}) async-start(bf16[4,96,2048]{2,1,0:T(8,128)(2,1)} %pack.1), calls=%async_computation.1 | async-start | bytes 3145728 | tf_op jit(solution)/shard_map/all_to_all | solution.py:705
  20.2 1.4 copy.24.maps_ref
  21.6 4.7 %scan_local.1 = (f32[64,4096]{1,0:T(8,128)}, f32[512,128]{1,0:T(8,128)}, f32[64,64]{1,0:T(8,128)}, f32[1,64]{1,0:T(1,128)}) custom-call(bf16[64,4096]{1,0:T(8,128)(2,1)} %x_ref.1, f32[64,32]{1,0:T(8,128)} %copy.24.maps_ref, f32[64,64]{1,0:T(8,128)} %steps_ref.1, f32[64,64]{1,0:T(8,128)} %decays_ref.1, bf16[64,4096]{1,0:T(8,128)(2,1)} %tokens_ref.1), custom_call_target="tpu_custom_call" | custom-call | tf_op jit(solution)/shard_map/scan_local/pallas_call | solution.py:242
  26.4 1.3 slice_bitcast_fusion.names_ref
  27.7 23.9 %all-to-all-done.1.got_ref = bf16[4,96,2048]{2,1,0:T(8,128)(2,1)S(1)} async-done(((bf16[4,96,2048]{2,1,0:T(8,128)(2,1)}), bf16[4,96,2048]{2,1,0:T(8,128)(2,1)S(1)}, u32[]{:S(2)}, u32[]{:S(2)}) %all-to-all-start.1) | async-done | bytes 1572896 | tf_op jit(solution)/shard_map/all_to_all | solution.py:705
  51.6 8.6 %mix.1 = (bf16[64,4096]{1,0:T(8,128)(2,1)}, bf16[64,4096]{1,0:T(8,128)(2,1)}, bf16[128,4096]{1,0:T(8,128)(2,1)}, f32[512,128]{1,0:T(8,128)}, bf16[128,128]{1,0:T(8,128)(2,1)}) custom-call(s32[1]{0:T(128)S(6)} %copy.33.owner_ref, bf16[64,4096]{1,0:T(8,128)(2,1)} %q_ref.1, bf16[64,2048]{1,0:T(8,128)(2,1)} %kv_ref.1, ...), custom_call_target="tpu_custom_call" | custom-call | tf_op jit(solution)/shard_map/mix/pallas_call | solution.py:400
  60.1 6.8 %all-to-all-start.2 = ((bf16[8,16,4096]{2,1,0:T(8,128)(2,1)}), bf16[8,16,4096]{2,1,0:T(8,128)(2,1)S(1)}, u32[]{:S(2)}, u32[]{:S(2)}) async-start(bf16[8,16,4096]{2,1,0:T(8,128)(2,1)} %bitcast.49), calls=%async_computation.2 | async-start | bytes 2097152 | tf_op jit(solution)/shard_map/all_to_all | solution.py:691
  67.0 3.0 %collective-permute-start.1 = (bf16[64,4096]{1,0:T(8,128)(2,1)}, bf16[64,4096]{1,0:T(8,128)(2,1)S(1)}, u32[]{:S(2)}, u32[]{:S(2)}) collective-permute-start(bf16[64,4096]{1,0:T(8,128)(2,1)} %get-tuple-element.28), channel_id=1, source_target_pairs={{0,16},{8,24},{16,0},{24,8},{1,17},{9,25},{17,1},{25,9},{2,18},{10... | collective-permute-start | bytes 1572872 | tf_op jit(solution)/shard_map/ppermute | solution.py:687
  70.0 22.9 %collective-permute-done.1.rows_ref = bf16[64,4096]{1,0:T(8,128)(2,1)S(1)} collective-permute-done((bf16[64,4096]{1,0:T(8,128)(2,1)}, bf16[64,4096]{1,0:T(8,128)(2,1)S(1)}, u32[]{:S(2)}, u32[]{:S(2)}) %collective-permute-start.1) | collective-permute-done | bytes 524320 | tf_op jit(solution)/shard_map/ppermute | solution.py:687
  92.9 0.0 copy-done.1
  92.9 1.7 choose.3
  94.6 0.0 all-to-all-done.2
  94.6 4.3 %all-to-all-start.4 = ((bf16[8,16,4096]{2,1,0:T(8,128)(2,1)}), bf16[8,16,4096]{2,1,0:T(8,128)(2,1)S(1)}, u32[]{:S(2)}, u32[]{:S(2)}) async-start(bf16[8,16,4096]{2,1,0:T(8,128)(2,1)} %bitcast.50), calls=%async_computation.4 | async-start | bytes 2097152 | tf_op jit(solution)/shard_map/all_to_all | solution.py:691
  98.9 2.1 collective-permute-start.2
  101.0 0.0 collective-permute-start
  101.0 11.9 %collective-permute-done.2.rows_ref = bf16[64,4096]{1,0:T(8,128)(2,1)S(1)} collective-permute-done((bf16[64,4096]{1,0:T(8,128)(2,1)S(1)}, bf16[64,4096]{1,0:T(8,128)(2,1)S(1)}, u32[]{:S(2)}, u32[]{:S(2)}) %collective-permute-start.2) | collective-permute-done | bytes 524320 | tf_op jit(solution)/shard_map/ppermute | solution.py:687
  112.9 1.8 choose.2
  114.7 0.0 all-to-all-done.4
  114.7 5.3 %all-to-all-start.3 = ((bf16[8,16,4096]{2,1,0:T(8,128)(2,1)}), bf16[8,16,4096]{2,1,0:T(8,128)(2,1)S(1)}, u32[]{:S(2)}, u32[]{:S(2)}) async-start(bf16[8,16,4096]{2,1,0:T(8,128)(2,1)} %bitcast.53), calls=%async_computation.3 | async-start | bytes 2097152 | tf_op jit(solution)/shard_map/all_to_all | solution.py:691
  120.0 13.2 %expert.3 = (bf16[128,4096]{1,0:T(8,128)(2,1)}, bf16[128,4096]{1,0:T(8,128)(2,1)}) custom-call(bf16[128,4096]{1,0:T(8,128)(2,1)S(1)} %bitcast.31, bf16[128,4096]{1,0:T(8,128)(2,1)S(1)} %bitcast.32, bf16[4096,1792]{1,0:T(8,128)(2,1)} %bitcast.44, bf16[1792,4096]{1,0:T(8,128)(2,1)} %bitcast.46), custom_call_target="tpu_custom_call" | custom-call | flops 7516192768 | bytes 33554432 | tf_op jit(solution)/shard_map/expert/pallas_call | solution.py:627
  133.2 0.7 all-to-all-done.3
  134.0 4.9 %all-to-all-start.6 = ((bf16[8,16,4096]{2,1,0:T(8,128)(2,1)}), bf16[8,16,4096]{2,1,0:T(8,128)(2,1)S(1)}, u32[]{:S(2)}, u32[]{:S(2)}) async-start(bf16[8,16,4096]{2,1,0:T(8,128)(2,1)} %bitcast.51), calls=%async_computation.6 | async-start | bytes 2097152 | tf_op jit(solution)/shard_map/all_to_all | solution.py:691
  138.9 0.0 collective-permute-done.refs_0_
  138.9 0.0 copy-start.2
  138.9 14.4 %expert.2 = (bf16[128,4096]{1,0:T(8,128)(2,1)}, bf16[128,4096]{1,0:T(8,128)(2,1)}) custom-call(bf16[128,4096]{1,0:T(8,128)(2,1)} %collective-permute-done.refs_0_, bf16[128,4096]{1,0:T(8,128)(2,1)S(1)} %bitcast.34, bf16[4096,1792]{1,0:T(8,128)(2,1)} %bitcast.45, bf16[1792,4096]{1,0:T(8,128)(2,1)} %bitcast.47), custom_call_target="tpu_custom_call" | custom-call | flops 7516192768 | bytes 33554432 | tf_op jit(solution)/shard_map/expert/pallas_call | solution.py:627
  153.3 1.8 collective-permute-start.3
  155.1 0.0 all-to-all-done.6
  155.1 4.5 %all-to-all-start.7 = ((bf16[8,16,4096]{2,1,0:T(8,128)(2,1)}), bf16[8,16,4096]{2,1,0:T(8,128)(2,1)S(1)}, u32[]{:S(2)}, u32[]{:S(2)}) async-start(bf16[8,16,4096]{2,1,0:T(8,128)(2,1)} %bitcast.52), calls=%async_computation.7 | async-start | bytes 2097152 | tf_op jit(solution)/shard_map/all_to_all | solution.py:691
  159.6 18.9 %collective-permute-done.3.refs_0_ = bf16[128,4096]{1,0:T(8,128)(2,1)S(1)} collective-permute-done((bf16[128,4096]{1,0:T(8,128)(2,1)}, bf16[128,4096]{1,0:T(8,128)(2,1)S(1)}, u32[]{:S(2)}, u32[]{:S(2)}) %collective-permute-start.3) | collective-permute-done | bytes 1048608 | tf_op jit(solution)/shard_map/ppermute | solution.py:687
  178.5 2.3 shard_map.194
  180.8 0.0 all-to-all-done.7
  180.8 4.8 %all-to-all-start.5 = ((bf16[8,16,4096]{2,1,0:T(8,128)(2,1)}), bf16[8,16,4096]{2,1,0:T(8,128)(2,1)S(1)}, u32[]{:S(2)}, u32[]{:S(2)}) async-start(bf16[8,16,4096]{2,1,0:T(8,128)(2,1)} %bitcast.48), calls=%async_computation.5 | async-start | bytes 2097152 | tf_op jit(solution)/shard_map/all_to_all | solution.py:691
  185.6 0.4 shard_map.195
  186.1 2.4 %collective-permute-start.4 = (bf16[64,4096]{1,0:T(8,128)(2,1)S(1)}, bf16[64,4096]{1,0:T(8,128)(2,1)S(1)}, u32[]{:S(2)}, u32[]{:S(2)}) collective-permute-start(bf16[64,4096]{1,0:T(8,128)(2,1)S(1)} %shard_map.195), channel_id=1, source_target_pairs={{0,16},{8,24},{16,0},{24,8},{1,17},{9,25},{17,1},{25,9},{2,18},{10... | collective-permute-start | bytes 1572872 | tf_op jit(solution)/shard_map/ppermute | solution.py:687
  188.5 0.4 shard_map.196
  188.9 0.3 collective-permute-start.5
  189.3 33.1 %collective-permute-done.4.refs_2_ = bf16[64,4096]{1,0:T(8,128)(2,1)S(1)} collective-permute-done((bf16[64,4096]{1,0:T(8,128)(2,1)S(1)}, bf16[64,4096]{1,0:T(8,128)(2,1)S(1)}, u32[]{:S(2)}, u32[]{:S(2)}) %collective-permute-start.4) | collective-permute-done | bytes 524320 | tf_op jit(solution)/shard_map/ppermute | solution.py:687
  222.3 12.3 %collective-permute-done.5.refs_3_ = bf16[64,4096]{1,0:T(8,128)(2,1)S(1)} collective-permute-done((bf16[64,4096]{1,0:T(8,128)(2,1)S(1)}, bf16[64,4096]{1,0:T(8,128)(2,1)S(1)}, u32[]{:S(2)}, u32[]{:S(2)}) %collective-permute-start.5) | collective-permute-done | bytes 524320 | tf_op jit(solution)/shard_map/ppermute | solution.py:687
  234.6 0.0 all-to-all-done.5
  234.6 0.0 copy-done.2
  234.6 2.1 shard_map.197
  (3 shorter events, 0.0 us)
Async XLA Ops:
  0.6 92.3 %copy-start.1 = (bf16[4096,8]{0,1:T(8,128)(2,1)S(1)}, bf16[4096,8]{0,1:T(8,128)(2,1)}, u32[]{:S(2)}) copy-start(bf16[4096,8]{0,1:T(8,128)(2,1)} %param.34) | copy-start | bytes 196612
  3.5 8.0 %all-to-all-start = ((s32[4,1,256]{2,1,0:T(1,128)}), s32[4,1,256]{2,1,0:T(1,128)S(1)}, u32[]{:S(2)}, u32[]{:S(2)}) async-start(s32[4,1,256]{2,1,0:T(1,128)} %get-tuple-element.21), calls=%async_computation | async-start | bytes 8192 | tf_op jit(solution)/shard_map/all_to_all | solution.py:697
  11.5 1.0 copy-start
  14.9 36.7 %all-to-all-start.1 = ((bf16[4,96,2048]{2,1,0:T(8,128)(2,1)}), bf16[4,96,2048]{2,1,0:T(8,128)(2,1)S(1)}, u32[]{:S(2)}, u32[]{:S(2)}) async-start(bf16[4,96,2048]{2,1,0:T(8,128)(2,1)} %pack.1), calls=%async_computation.1 | async-start | bytes 3145728 | tf_op jit(solution)/shard_map/all_to_all | solution.py:705
  60.1 34.5 %all-to-all-start.2 = ((bf16[8,16,4096]{2,1,0:T(8,128)(2,1)}), bf16[8,16,4096]{2,1,0:T(8,128)(2,1)S(1)}, u32[]{:S(2)}, u32[]{:S(2)}) async-start(bf16[8,16,4096]{2,1,0:T(8,128)(2,1)} %bitcast.49), calls=%async_computation.2 | async-start | bytes 2097152 | tf_op jit(solution)/shard_map/all_to_all | solution.py:691
  67.0 25.9 %collective-permute-start.1 = (bf16[64,4096]{1,0:T(8,128)(2,1)}, bf16[64,4096]{1,0:T(8,128)(2,1)S(1)}, u32[]{:S(2)}, u32[]{:S(2)}) collective-permute-start(bf16[64,4096]{1,0:T(8,128)(2,1)} %get-tuple-element.28), channel_id=1, source_target_pairs={{0,16},{8,24},{16,0},{24,8},{1,17},{9,25},{17,1},{25,9},{2,18},{10... | collective-permute-start | bytes 1572872 | tf_op jit(solution)/shard_map/ppermute | solution.py:687
  94.6 20.1 %all-to-all-start.4 = ((bf16[8,16,4096]{2,1,0:T(8,128)(2,1)}), bf16[8,16,4096]{2,1,0:T(8,128)(2,1)S(1)}, u32[]{:S(2)}, u32[]{:S(2)}) async-start(bf16[8,16,4096]{2,1,0:T(8,128)(2,1)} %bitcast.50), calls=%async_computation.4 | async-start | bytes 2097152 | tf_op jit(solution)/shard_map/all_to_all | solution.py:691
  98.9 14.0 %collective-permute-start.2 = (bf16[64,4096]{1,0:T(8,128)(2,1)S(1)}, bf16[64,4096]{1,0:T(8,128)(2,1)S(1)}, u32[]{:S(2)}, u32[]{:S(2)}) collective-permute-start(bf16[64,4096]{1,0:T(8,128)(2,1)S(1)} %collective-permute-done.1.rows_ref), channel_id=1, source_target_pairs={{0,8},{8,0},{16,24},{24,16},{1,9},{9,1},{17,25},{25,17},{2,10},{10... | collective-permute-start | bytes 1572872 | tf_op jit(solution)/shard_map/ppermute | solution.py:687
  101.0 37.9 %collective-permute-start = (bf16[128,4096]{1,0:T(8,128)(2,1)S(1)}, bf16[128,4096]{1,0:T(8,128)(2,1)}, u32[]{:S(2)}, u32[]{:S(2)}) collective-permute-start(bf16[128,4096]{1,0:T(8,128)(2,1)S(1)} %bitcast.30), channel_id=1, source_target_pairs={{0,8},{8,0},{16,24},{24,16},{1,9},{9,1},{17,25},{25,17},{2,10},{10... | collective-permute-start | bytes 3145736 | tf_op jit(solution)/shard_map/ppermute | solution.py:687
  114.7 19.3 %all-to-all-start.3 = ((bf16[8,16,4096]{2,1,0:T(8,128)(2,1)}), bf16[8,16,4096]{2,1,0:T(8,128)(2,1)S(1)}, u32[]{:S(2)}, u32[]{:S(2)}) async-start(bf16[8,16,4096]{2,1,0:T(8,128)(2,1)} %bitcast.53), calls=%async_computation.3 | async-start | bytes 2097152 | tf_op jit(solution)/shard_map/all_to_all | solution.py:691
  134.0 21.2 %all-to-all-start.6 = ((bf16[8,16,4096]{2,1,0:T(8,128)(2,1)}), bf16[8,16,4096]{2,1,0:T(8,128)(2,1)S(1)}, u32[]{:S(2)}, u32[]{:S(2)}) async-start(bf16[8,16,4096]{2,1,0:T(8,128)(2,1)} %bitcast.51), calls=%async_computation.6 | async-start | bytes 2097152 | tf_op jit(solution)/shard_map/all_to_all | solution.py:691
  138.9 95.7 %copy-start.2 = (bf16[128,128]{1,0:T(8,128)(2,1)S(1)}, bf16[128,128]{1,0:T(8,128)(2,1)}, u32[]{:S(2)}) copy-start(bf16[128,128]{1,0:T(8,128)(2,1)} %get-tuple-element.33.refs_1_) | copy-start | bytes 98308
  153.3 25.2 %collective-permute-start.3 = (bf16[128,4096]{1,0:T(8,128)(2,1)}, bf16[128,4096]{1,0:T(8,128)(2,1)S(1)}, u32[]{:S(2)}, u32[]{:S(2)}) collective-permute-start(bf16[128,4096]{1,0:T(8,128)(2,1)} %get-tuple-element.30), channel_id=1, source_target_pairs={{0,8},{8,0},{16,24},{24,16},{1,9},{9,1},{17,25},{25,17},{2,10},{10... | collective-permute-start | bytes 3145736 | tf_op jit(solution)/shard_map/ppermute | solution.py:687
  155.1 25.7 %all-to-all-start.7 = ((bf16[8,16,4096]{2,1,0:T(8,128)(2,1)}), bf16[8,16,4096]{2,1,0:T(8,128)(2,1)S(1)}, u32[]{:S(2)}, u32[]{:S(2)}) async-start(bf16[8,16,4096]{2,1,0:T(8,128)(2,1)} %bitcast.52), calls=%async_computation.7 | async-start | bytes 2097152 | tf_op jit(solution)/shard_map/all_to_all | solution.py:691
  180.8 53.8 %all-to-all-start.5 = ((bf16[8,16,4096]{2,1,0:T(8,128)(2,1)}), bf16[8,16,4096]{2,1,0:T(8,128)(2,1)S(1)}, u32[]{:S(2)}, u32[]{:S(2)}) async-start(bf16[8,16,4096]{2,1,0:T(8,128)(2,1)} %bitcast.48), calls=%async_computation.5 | async-start | bytes 2097152 | tf_op jit(solution)/shard_map/all_to_all | solution.py:691
  186.1 36.3 %collective-permute-start.4 = (bf16[64,4096]{1,0:T(8,128)(2,1)S(1)}, bf16[64,4096]{1,0:T(8,128)(2,1)S(1)}, u32[]{:S(2)}, u32[]{:S(2)}) collective-permute-start(bf16[64,4096]{1,0:T(8,128)(2,1)S(1)} %shard_map.195), channel_id=1, source_target_pairs={{0,16},{8,24},{16,0},{24,8},{1,17},{9,25},{17,1},{25,9},{2,18},{10... | collective-permute-start | bytes 1572872 | tf_op jit(solution)/shard_map/ppermute | solution.py:687
  188.9 45.7 %collective-permute-start.5 = (bf16[64,4096]{1,0:T(8,128)(2,1)S(1)}, bf16[64,4096]{1,0:T(8,128)(2,1)S(1)}, u32[]{:S(2)}, u32[]{:S(2)}) collective-permute-start(bf16[64,4096]{1,0:T(8,128)(2,1)S(1)} %shard_map.196), channel_id=1, source_target_pairs={{0,24},{8,16},{16,8},{24,0},{1,25},{9,17},{17,9},{25,1},{2,26},{10... | collective-permute-start | bytes 1572872 | tf_op jit(solution)/shard_map/ppermute | solution.py:687

commit v5 on v4

--- a/solution.py
+++ b/solution.py
@@ -1,4 +1,5 @@
 import functools
+import math
 
 import jax
 import jax.numpy as jnp
@@ -326,13 +327,12 @@
         )
         scores = (
             lax.dot_general(asks, keys, (((1,), (1,)), ((), ())), preferred_element_type=F32)
-            * HEAD ** (-0.5)
             + seen
         )
         top = jnp.max(scores, axis=1, keepdims=True)
-        weights = jnp.exp(scores - top)
-        weights = (weights * (1.0 / jnp.sum(weights, axis=1, keepdims=True))).astype(BF16)
-        attended = jnp.dot(weights, values, preferred_element_type=F32)
+        weights = jnp.exp2((scores - top) * (HEAD ** (-0.5) * math.log2(math.e)))
+        attended = jnp.dot(weights.astype(BF16), values, preferred_element_type=F32)
+        attended = attended * (1.0 / jnp.sum(weights, axis=1, keepdims=True))
         for i in range(groups):
             q = g * groups + i
             cols = slice(q * LANES, (q + 1) * LANES)
@@ -546,14 +546,39 @@
     return held_call(body, [parts, weights] + sums, mixed)
 
 
+def combine_keep_kernel(parts_ref, weights_ref, far_ref, out_ref, near_ref, sem):
+    copy = pltpu.make_async_copy(far_ref, near_ref, sem)
+    copy.start()
+    step = 8 * LANES
+    for at in range(0, out_ref.shape[1], step):
+        cols = slice(at, at + step)
+        out_ref[:, cols] = weighed(parts_ref[:, cols], weights_ref[...]).astype(BF16)
+    copy.wait()
+
+
+def combine_keep(parts, weights, far):
+    return pl.pallas_call(
+        combine_keep_kernel,
+        out_shape=(
+            pltpu.VMEM((weights.shape[0] // 2, parts.shape[1]), BF16),
+            pltpu.VMEM(far.shape, BF16),
+        ),
+        in_specs=[VMEM, VMEM, pl.BlockSpec(memory_space=pl.ANY)],
+        out_specs=(VMEM, VMEM),
+        scratch_shapes=[pltpu.SemaphoreType.DMA],
+        compiler_params=pltpu.CompilerParams(vmem_limit_bytes=8 << 20),
+        name="combine_keep",
+    )(resident(parts), weights, pltpu.with_memory_space_constraint(far, pltpu.HBM))
+
+
 def join(first, others):
     if not others:
         return first
 
-    def body(cols, *refs):
-        return sum(ref[:, cols].astype(F32) for ref in refs)
-
-    return held_call(body, others, first)
+    def body(held):
+        return sum(part.astype(F32) for part in held).astype(BF16)
+
+    return stream(body, [first] + others, [], first.shape[0], keep=False)
 
 
 def expert_kernel(count, ups, downs, *refs):
@@ -736,7 +761,10 @@
     far_sums = []
     for turn in range(near):
         back = swap_rows(far_out[turn])
-        part = combine(back, far_weights[turn])
+        if turn > 0 and turn == near - 1:
+            part, near_out = combine_keep(back, far_weights[turn], near_out)
+        else:
+            part = combine(back, far_weights[turn])
         far_sums.append(move(part, near - turn, 1))
     moved_back = [move(rows, near - turn, 0) for turn, rows in enumerate(moved_out, 1)]
     joined = join(near_out, moved_back)

time: 238 us -> 242 us (1.017)
  the two profiles are of different devices: /device:TPU:11 before, /device:TPU:13 now
where the time goes in v5:
time: 242 us; the launch traced here: 241 us
  waiting for transfers between devices  119 us (49%)
  starting transfers between devices  57.1 us (24%)
  Pallas kernels  54.3 us (22%)
  local copies, waits for them, and re-layouts  5.89 us (2%)
  between operations  2.89 us (1%)
    ppermute x6, waiting for transfers between devices, move(): return lax.ppermute(rows, 'dp', route(turn, side))  80.3 us
    all_to_all x6, starting transfers between devices, swap_rows(): lax.all_to_all(blocks, 'expert', split_axis=0, concat_axis=0, tiled=True)  36.1 us
    pallas_call x2, Pallas kernels, apply_expert(): pl.pallas_call(functools.partial(expert_kernel, count, ups, downs), out_s...  27.6 us
    all_to_all x1, waiting for transfers between devices, local(): got = lax.all_to_all(packed, 'dp', split_axis=0, concat_axis=0, tiled=True)  24 us
    all_to_all x6, waiting for transfers between devices, swap_rows(): lax.all_to_all(blocks, 'expert', split_axis=0, concat_axis=0, tiled=True)  12.9 us
    ppermute x6, starting transfers between devices, move(): return lax.ppermute(rows, 'dp', route(turn, side))  11.5 us
    pallas_call x1, Pallas kernels, mix(): pl.pallas_call(mix_kernel, out_shape=(pltpu.HBM((length, width), BF16), j...  8.33 us
  transfers between devices with their start and end apart: 14, of which 10 were waited for; matrix products, arithmetic and copies ran while one was open for 2% of the time, Pallas kernels for 17%

profile of v5, /device:TPU:13, one launch (start us, length us, event | category | flops | bytes accessed | tf_op | source)
XLA Modules:
  0.0 240.6 jit_solution(8565652476285137023)
XLA Ops:
  0.6 0.0 copy-start.3
  2.0 1.5 plan.1
  3.5 4.8 %all-to-all-start = ((s32[4,1,256]{2,1,0:T(1,128)}), s32[4,1,256]{2,1,0:T(1,128)S(1)}, u32[]{:S(2)}, u32[]{:S(2)}) async-start(s32[4,1,256]{2,1,0:T(1,128)} %get-tuple-element.23), calls=%async_computation | async-start | bytes 8192 | tf_op jit(solution)/shard_map/all_to_all | solution.py:722
  8.2 1.2 convert_bitcast_fusion
  9.5 2.0 all-to-all-done
  11.5 0.0 copy-start
  11.5 1.0 copy-done
  12.5 2.3 pack.1
  14.9 4.7 %all-to-all-start.1 = ((bf16[4,96,2048]{2,1,0:T(8,128)(2,1)}), bf16[4,96,2048]{2,1,0:T(8,128)(2,1)S(1)}, u32[]{:S(2)}, u32[]{:S(2)}) async-start(bf16[4,96,2048]{2,1,0:T(8,128)(2,1)} %pack.1), calls=%async_computation.1 | async-start | bytes 3145728 | tf_op jit(solution)/shard_map/all_to_all | solution.py:730
  20.2 1.4 copy.24.maps_ref
  21.6 4.7 %scan_local.1 = (f32[64,4096]{1,0:T(8,128)}, f32[512,128]{1,0:T(8,128)}, f32[64,64]{1,0:T(8,128)}, f32[1,64]{1,0:T(1,128)}) custom-call(bf16[64,4096]{1,0:T(8,128)(2,1)} %x_ref.1, f32[64,32]{1,0:T(8,128)} %copy.24.maps_ref, f32[64,64]{1,0:T(8,128)} %steps_ref.1, f32[64,64]{1,0:T(8,128)} %decays_ref.1, bf16[64,4096]{1,0:T(8,128)(2,1)} %tokens_ref.1), custom_call_target="tpu_custom_call" | custom-call | tf_op jit(solution)/shard_map/scan_local/pallas_call | solution.py:243
  26.4 1.2 slice_bitcast_fusion.names_ref
  27.6 24.0 %all-to-all-done.1.got_ref = bf16[4,96,2048]{2,1,0:T(8,128)(2,1)S(1)} async-done(((bf16[4,96,2048]{2,1,0:T(8,128)(2,1)}), bf16[4,96,2048]{2,1,0:T(8,128)(2,1)S(1)}, u32[]{:S(2)}, u32[]{:S(2)}) %all-to-all-start.1) | async-done | bytes 1572896 | tf_op jit(solution)/shard_map/all_to_all | solution.py:730
  51.5 8.3 %mix.1 = (bf16[64,4096]{1,0:T(8,128)(2,1)}, bf16[64,4096]{1,0:T(8,128)(2,1)}, bf16[128,4096]{1,0:T(8,128)(2,1)}, f32[512,128]{1,0:T(8,128)}, bf16[128,128]{1,0:T(8,128)(2,1)}) custom-call(s32[1]{0:T(128)S(6)} %copy.33.owner_ref, bf16[64,4096]{1,0:T(8,128)(2,1)} %q_ref.1, bf16[64,2048]{1,0:T(8,128)(2,1)} %kv_ref.1, ...), custom_call_target="tpu_custom_call" | custom-call | tf_op jit(solution)/shard_map/mix/pallas_call | solution.py:400
  59.9 3.1 %collective-permute-start.1 = (bf16[64,4096]{1,0:T(8,128)(2,1)}, bf16[64,4096]{1,0:T(8,128)(2,1)S(1)}, u32[]{:S(2)}, u32[]{:S(2)}) collective-permute-start(bf16[64,4096]{1,0:T(8,128)(2,1)} %get-tuple-element.30), channel_id=1, source_target_pairs={{0,16},{8,24},{16,0},{24,8},{1,17},{9,25},{17,1},{25,9},{2,18},{10... | collective-permute-start | bytes 1572872 | tf_op jit(solution)/shard_map/ppermute | solution.py:712
  62.9 7.1 %all-to-all-start.2 = ((bf16[8,16,4096]{2,1,0:T(8,128)(2,1)}), bf16[8,16,4096]{2,1,0:T(8,128)(2,1)S(1)}, u32[]{:S(2)}, u32[]{:S(2)}) async-start(bf16[8,16,4096]{2,1,0:T(8,128)(2,1)} %bitcast.48), calls=%async_computation.2 | async-start | bytes 2097152 | tf_op jit(solution)/shard_map/all_to_all | solution.py:716
  70.0 14.8 %collective-permute-done.1.rows_ref = bf16[64,4096]{1,0:T(8,128)(2,1)S(1)} collective-permute-done((bf16[64,4096]{1,0:T(8,128)(2,1)}, bf16[64,4096]{1,0:T(8,128)(2,1)S(1)}, u32[]{:S(2)}, u32[]{:S(2)}) %collective-permute-start.1) | collective-permute-done | bytes 524320 | tf_op jit(solution)/shard_map/ppermute | solution.py:712
  84.8 3.1 %collective-permute-start.2 = (bf16[64,4096]{1,0:T(8,128)(2,1)S(1)}, bf16[64,4096]{1,0:T(8,128)(2,1)S(1)}, u32[]{:S(2)}, u32[]{:S(2)}) collective-permute-start(bf16[64,4096]{1,0:T(8,128)(2,1)S(1)} %collective-permute-done.1.rows_ref), channel_id=1, source_target_pairs={{0,8},{8,0},{16,24},{24,16},{1,9},{9,1},{17,25},{25,17},{2,10},{10... | collective-permute-start | bytes 1572872 | tf_op jit(solution)/shard_map/ppermute | solution.py:712
  87.9 11.8 %collective-permute-done.2.rows_ref = bf16[64,4096]{1,0:T(8,128)(2,1)S(1)} collective-permute-done((bf16[64,4096]{1,0:T(8,128)(2,1)S(1)}, bf16[64,4096]{1,0:T(8,128)(2,1)S(1)}, u32[]{:S(2)}, u32[]{:S(2)}) %collective-permute-start.2) | collective-permute-done | bytes 524320 | tf_op jit(solution)/shard_map/ppermute | solution.py:712
  99.8 0.0 copy-done.3
  99.8 1.8 choose.2
  101.5 0.0 all-to-all-done.2
  101.5 4.9 %all-to-all-start.3 = ((bf16[8,16,4096]{2,1,0:T(8,128)(2,1)}), bf16[8,16,4096]{2,1,0:T(8,128)(2,1)S(1)}, u32[]{:S(2)}, u32[]{:S(2)}) async-start(bf16[8,16,4096]{2,1,0:T(8,128)(2,1)} %bitcast.49), calls=%async_computation.3 | async-start | bytes 2097152 | tf_op jit(solution)/shard_map/all_to_all | solution.py:716
  106.4 1.5 collective-permute-start
  107.9 1.8 choose.3
  109.7 8.3 %all-to-all-done.3 = bf16[8,16,4096]{2,1,0:T(8,128)(2,1)S(1)} async-done(((bf16[8,16,4096]{2,1,0:T(8,128)(2,1)}), bf16[8,16,4096]{2,1,0:T(8,128)(2,1)S(1)}, u32[]{:S(2)}, u32[]{:S(2)}) %all-to-all-start.3) | async-done | bytes 1048608 | tf_op jit(solution)/shard_map/all_to_all | solution.py:716
  118.0 7.3 %all-to-all-start.5 = ((bf16[8,16,4096]{2,1,0:T(8,128)(2,1)}), bf16[8,16,4096]{2,1,0:T(8,128)(2,1)S(1)}, u32[]{:S(2)}, u32[]{:S(2)}) async-start(bf16[8,16,4096]{2,1,0:T(8,128)(2,1)} %bitcast.51), calls=%async_computation.5 | async-start | bytes 2097152 | tf_op jit(solution)/shard_map/all_to_all | solution.py:716
  125.3 5.6 %collective-permute-done.refs_0_ = bf16[128,4096]{1,0:T(8,128)(2,1)} collective-permute-done((bf16[128,4096]{1,0:T(8,128)(2,1)S(1)}, bf16[128,4096]{1,0:T(8,128)(2,1)}, u32[]{:S(2)}, u32[]{:S(2)}) %collective-permute-start) | collective-permute-done | bytes 1048608 | tf_op jit(solution)/shard_map/ppermute | solution.py:712
  130.9 14.4 %expert.2 = (bf16[128,4096]{1,0:T(8,128)(2,1)}, bf16[128,4096]{1,0:T(8,128)(2,1)}) custom-call(bf16[128,4096]{1,0:T(8,128)(2,1)} %collective-permute-done.refs_0_, bf16[128,4096]{1,0:T(8,128)(2,1)S(1)} %bitcast.32, bf16[4096,1792]{1,0:T(8,128)(2,1)} %bitcast.44, bf16[1792,4096]{1,0:T(8,128)(2,1)} %bitcast.46), custom_call_target="tpu_custom_call" | custom-call | flops 7516192768 | bytes 33554432 | tf_op jit(solution)/shard_map/expert/pallas_call | solution.py:652
  145.3 0.0 all-to-all-done.5
  145.3 5.1 %all-to-all-start.4 = ((bf16[8,16,4096]{2,1,0:T(8,128)(2,1)}), bf16[8,16,4096]{2,1,0:T(8,128)(2,1)S(1)}, u32[]{:S(2)}, u32[]{:S(2)}) async-start(bf16[8,16,4096]{2,1,0:T(8,128)(2,1)} %bitcast.52), calls=%async_computation.4 | async-start | bytes 2097152 | tf_op jit(solution)/shard_map/all_to_all | solution.py:716
  150.4 1.5 collective-permute-start.3
  151.8 0.0 copy-start.4
  151.8 13.2 %expert.3 = (bf16[128,4096]{1,0:T(8,128)(2,1)}, bf16[128,4096]{1,0:T(8,128)(2,1)}) custom-call(bf16[128,4096]{1,0:T(8,128)(2,1)S(1)} %bitcast.31, bf16[128,4096]{1,0:T(8,128)(2,1)S(1)} %bitcast.34, bf16[4096,1792]{1,0:T(8,128)(2,1)} %bitcast.45, bf16[1792,4096]{1,0:T(8,128)(2,1)} %bitcast.47), custom_call_target="tpu_custom_call" | custom-call | flops 7516192768 | bytes 33554432 | tf_op jit(solution)/shard_map/expert/pallas_call | solution.py:652
  165.0 0.0 all-to-all-done.4
  165.0 0.0 copy-start.1
  165.0 1.0 copy-done.1
  166.0 4.5 %all-to-all-start.7 = ((bf16[8,16,4096]{2,1,0:T(8,128)(2,1)}), bf16[8,16,4096]{2,1,0:T(8,128)(2,1)S(1)}, u32[]{:S(2)}, u32[]{:S(2)}) async-start(bf16[8,16,4096]{2,1,0:T(8,128)(2,1)} %bitcast.50), calls=%async_computation.7 | async-start | bytes 2097152 | tf_op jit(solution)/shard_map/all_to_all | solution.py:716
  170.5 0.0 copy-start.2
  170.5 1.2 copy-done.2
  171.7 1.2 combine_keep.1
  173.0 2.0 collective-permute-done.3.refs_1_
  175.0 2.4 %shard_map.194 = bf16[128,4096]{1,0:T(8,128)(2,1)} custom-call(bf16[128,4096]{1,0:T(8,128)(2,1)S(1)} %get-tuple-element.36.refs_0_, bf16[128,4096]{1,0:T(8,128)(2,1)} %collective-permute-done.3.refs_1_), custom_call_target="tpu_custom_call" | custom-call | flops 3145728 | bytes 3145728 | tf_op jit(solution)/shard_map/pallas_call | solution.py:440
  177.4 4.6 %all-to-all-done.7 = bf16[8,16,4096]{2,1,0:T(8,128)(2,1)S(1)} async-done(((bf16[8,16,4096]{2,1,0:T(8,128)(2,1)}), bf16[8,16,4096]{2,1,0:T(8,128)(2,1)S(1)}, u32[]{:S(2)}, u32[]{:S(2)}) %all-to-all-start.7) | async-done | bytes 1048608 | tf_op jit(solution)/shard_map/all_to_all | solution.py:716
  182.1 7.3 %all-to-all-start.6 = ((bf16[8,16,4096]{2,1,0:T(8,128)(2,1)}), bf16[8,16,4096]{2,1,0:T(8,128)(2,1)S(1)}, u32[]{:S(2)}, u32[]{:S(2)}) async-start(bf16[8,16,4096]{2,1,0:T(8,128)(2,1)} %bitcast.16), calls=%async_computation.6 | async-start | bytes 2097152 | tf_op jit(solution)/shard_map/all_to_all | solution.py:716
  189.4 0.4 shard_map.195
  189.8 1.1 collective-permute-start.4
  190.9 1.3 collective-permute-start.5
  192.2 32.8 %collective-permute-done.4.refs_2_ = bf16[64,4096]{1,0:T(8,128)(2,1)S(1)} collective-permute-done((bf16[64,4096]{1,0:T(8,128)(2,1)S(1)}, bf16[64,4096]{1,0:T(8,128)(2,1)S(1)}, u32[]{:S(2)}, u32[]{:S(2)}) %collective-permute-start.4) | collective-permute-done | bytes 524320 | tf_op jit(solution)/shard_map/ppermute | solution.py:712
  225.0 13.3 %collective-permute-done.5.refs_3_ = bf16[64,4096]{1,0:T(8,128)(2,1)S(1)} collective-permute-done((bf16[64,4096]{1,0:T(8,128)(2,1)S(1)}, bf16[64,4096]{1,0:T(8,128)(2,1)S(1)}, u32[]{:S(2)}, u32[]{:S(2)}) %collective-permute-start.5) | collective-permute-done | bytes 524320 | tf_op jit(solution)/shard_map/ppermute | solution.py:712
  238.3 0.0 all-to-all-done.6
  238.3 0.0 copy-done.4
  238.3 2.1 shard_map.196
  (3 shorter events, 0.0 us)
Async XLA Ops:
  0.6 99.1 %copy-start.3 = (bf16[4096,8]{0,1:T(8,128)(2,1)S(1)}, bf16[4096,8]{0,1:T(8,128)(2,1)}, u32[]{:S(2)}) copy-start(bf16[4096,8]{0,1:T(8,128)(2,1)} %param.34) | copy-start | bytes 196612
  3.5 8.0 %all-to-all-start = ((s32[4,1,256]{2,1,0:T(1,128)}), s32[4,1,256]{2,1,0:T(1,128)S(1)}, u32[]{:S(2)}, u32[]{:S(2)}) async-start(s32[4,1,256]{2,1,0:T(1,128)} %get-tuple-element.23), calls=%async_computation | async-start | bytes 8192 | tf_op jit(solution)/shard_map/all_to_all | solution.py:722
  11.5 1.0 copy-start
  14.9 36.7 %all-to-all-start.1 = ((bf16[4,96,2048]{2,1,0:T(8,128)(2,1)}), bf16[4,96,2048]{2,1,0:T(8,128)(2,1)S(1)}, u32[]{:S(2)}, u32[]{:S(2)}) async-start(bf16[4,96,2048]{2,1,0:T(8,128)(2,1)} %pack.1), calls=%async_computation.1 | async-start | bytes 3145728 | tf_op jit(solution)/shard_map/all_to_all | solution.py:730
  59.9 25.0 %collective-permute-start.1 = (bf16[64,4096]{1,0:T(8,128)(2,1)}, bf16[64,4096]{1,0:T(8,128)(2,1)S(1)}, u32[]{:S(2)}, u32[]{:S(2)}) collective-permute-start(bf16[64,4096]{1,0:T(8,128)(2,1)} %get-tuple-element.30), channel_id=1, source_target_pairs={{0,16},{8,24},{16,0},{24,8},{1,17},{9,25},{17,1},{25,9},{2,18},{10... | collective-permute-start | bytes 1572872 | tf_op jit(solution)/shard_map/ppermute | solution.py:712
  62.9 38.6 %all-to-all-start.2 = ((bf16[8,16,4096]{2,1,0:T(8,128)(2,1)}), bf16[8,16,4096]{2,1,0:T(8,128)(2,1)S(1)}, u32[]{:S(2)}, u32[]{:S(2)}) async-start(bf16[8,16,4096]{2,1,0:T(8,128)(2,1)} %bitcast.48), calls=%async_computation.2 | async-start | bytes 2097152 | tf_op jit(solution)/shard_map/all_to_all | solution.py:716
  84.8 14.9 %collective-permute-start.2 = (bf16[64,4096]{1,0:T(8,128)(2,1)S(1)}, bf16[64,4096]{1,0:T(8,128)(2,1)S(1)}, u32[]{:S(2)}, u32[]{:S(2)}) collective-permute-start(bf16[64,4096]{1,0:T(8,128)(2,1)S(1)} %collective-permute-done.1.rows_ref), channel_id=1, source_target_pairs={{0,8},{8,0},{16,24},{24,16},{1,9},{9,1},{17,25},{25,17},{2,10},{10... | collective-permute-start | bytes 1572872 | tf_op jit(solution)/shard_map/ppermute | solution.py:712
  101.5 16.5 %all-to-all-start.3 = ((bf16[8,16,4096]{2,1,0:T(8,128)(2,1)}), bf16[8,16,4096]{2,1,0:T(8,128)(2,1)S(1)}, u32[]{:S(2)}, u32[]{:S(2)}) async-start(bf16[8,16,4096]{2,1,0:T(8,128)(2,1)} %bitcast.49), calls=%async_computation.3 | async-start | bytes 2097152 | tf_op jit(solution)/shard_map/all_to_all | solution.py:716
  106.4 24.4 %collective-permute-start = (bf16[128,4096]{1,0:T(8,128)(2,1)S(1)}, bf16[128,4096]{1,0:T(8,128)(2,1)}, u32[]{:S(2)}, u32[]{:S(2)}) collective-permute-start(bf16[128,4096]{1,0:T(8,128)(2,1)S(1)} %bitcast.30), channel_id=1, source_target_pairs={{0,8},{8,0},{16,24},{24,16},{1,9},{9,1},{17,25},{25,17},{2,10},{10... | collective-permute-start | bytes 3145736 | tf_op jit(solution)/shard_map/ppermute | solution.py:712
  118.0 27.3 %all-to-all-start.5 = ((bf16[8,16,4096]{2,1,0:T(8,128)(2,1)}), bf16[8,16,4096]{2,1,0:T(8,128)(2,1)S(1)}, u32[]{:S(2)}, u32[]{:S(2)}) async-start(bf16[8,16,4096]{2,1,0:T(8,128)(2,1)} %bitcast.51), calls=%async_computation.5 | async-start | bytes 2097152 | tf_op jit(solution)/shard_map/all_to_all | solution.py:716
  145.3 19.7 %all-to-all-start.4 = ((bf16[8,16,4096]{2,1,0:T(8,128)(2,1)}), bf16[8,16,4096]{2,1,0:T(8,128)(2,1)S(1)}, u32[]{:S(2)}, u32[]{:S(2)}) async-start(bf16[8,16,4096]{2,1,0:T(8,128)(2,1)} %bitcast.52), calls=%async_computation.4 | async-start | bytes 2097152 | tf_op jit(solution)/shard_map/all_to_all | solution.py:716
  150.4 24.6 %collective-permute-start.3 = (bf16[128,4096]{1,0:T(8,128)(2,1)}, bf16[128,4096]{1,0:T(8,128)(2,1)}, u32[]{:S(2)}, u32[]{:S(2)}) collective-permute-start(bf16[128,4096]{1,0:T(8,128)(2,1)} %get-tuple-element.37), channel_id=1, source_target_pairs={{0,8},{8,0},{16,24},{24,16},{1,9},{9,1},{17,25},{25,17},{2,10},{10... | collective-permute-start | bytes 3145736 | tf_op jit(solution)/shard_map/ppermute | solution.py:712
  151.8 86.5 %copy-start.4 = (bf16[128,128]{1,0:T(8,128)(2,1)S(1)}, bf16[128,128]{1,0:T(8,128)(2,1)}, u32[]{:S(2)}) copy-start(bf16[128,128]{1,0:T(8,128)(2,1)} %get-tuple-element.38.refs_1_) | copy-start | bytes 98308
  165.0 1.0 copy-start.1
  166.0 16.0 %all-to-all-start.7 = ((bf16[8,16,4096]{2,1,0:T(8,128)(2,1)}), bf16[8,16,4096]{2,1,0:T(8,128)(2,1)S(1)}, u32[]{:S(2)}, u32[]{:S(2)}) async-start(bf16[8,16,4096]{2,1,0:T(8,128)(2,1)} %bitcast.50), calls=%async_computation.7 | async-start | bytes 2097152 | tf_op jit(solution)/shard_map/all_to_all | solution.py:716
  170.5 1.2 copy-start.2
  182.1 56.3 %all-to-all-start.6 = ((bf16[8,16,4096]{2,1,0:T(8,128)(2,1)}), bf16[8,16,4096]{2,1,0:T(8,128)(2,1)S(1)}, u32[]{:S(2)}, u32[]{:S(2)}) async-start(bf16[8,16,4096]{2,1,0:T(8,128)(2,1)} %bitcast.16), calls=%async_computation.6 | async-start | bytes 2097152 | tf_op jit(solution)/shard_map/all_to_all | solution.py:716
  189.8 35.3 %collective-permute-start.4 = (bf16[64,4096]{1,0:T(8,128)(2,1)S(1)}, bf16[64,4096]{1,0:T(8,128)(2,1)S(1)}, u32[]{:S(2)}, u32[]{:S(2)}) collective-permute-start(bf16[64,4096]{1,0:T(8,128)(2,1)S(1)} %shard_map.195), channel_id=1, source_target_pairs={{0,16},{8,24},{16,0},{24,8},{1,17},{9,25},{17,1},{25,9},{2,18},{10... | collective-permute-start | bytes 1572872 | tf_op jit(solution)/shard_map/ppermute | solution.py:712
  190.9 47.4 %collective-permute-start.5 = (bf16[64,4096]{1,0:T(8,128)(2,1)S(1)}, bf16[64,4096]{1,0:T(8,128)(2,1)S(1)}, u32[]{:S(2)}, u32[]{:S(2)}) collective-permute-start(bf16[64,4096]{1,0:T(8,128)(2,1)S(1)} %get-tuple-element.41), channel_id=1, source_target_pairs={{0,24},{8,16},{16,8},{24,0},{1,25},{9,17},{17,9},{25,1},{2,26},{10... | collective-permute-start | bytes 1572872 | tf_op jit(solution)/shard_map/ppermute | solution.py:712

commit v6 on v5

--- a/solution.py
+++ b/solution.py
@@ -267,13 +267,11 @@
     keep_ref,
     maps_ref,
     gain_ref,
-    names_ref,
-    router_ref,
+    pick_ref,
     mixed_out,
     normed_ref,
     send_out,
     final_ref,
-    weights_ref,
     total_ref,
     mixed_ref,
     send_ref,
@@ -367,10 +365,7 @@
     send_copies = []
     mean = jnp.sum(squares, axis=1, keepdims=True) * (1.0 / width)
     scale = lax.rsqrt(mean + 1e-05)
-    experts = router_ref.shape[0]
-    hots = hots_of(names_ref[:, : 2 * length], 2 * length // experts)
-    pick = (hots[0] + hots[1]).astype(BF16)
-    logits = jnp.zeros((length, experts), F32)
+    pick = pick_ref[...]
     step = 4 * LANES
     for q in range(width // step):
         cols = slice(q * step, (q + 1) * step)
@@ -383,10 +378,6 @@
             pltpu.make_async_copy(send_ref.at[:, cols], send_out.at[:, cols], send_sems.at[q])
         )
         send_copies[-1].start()
-        logits = logits + lax.dot_general(
-            normed, router_ref[:, cols], (((1,), (1,)), ((), ())), preferred_element_type=F32
-        )
-    weights_ref[...] = weights_of(logits, hots)
     mixed_copy.wait()
     for copy in send_copies:
         copy.wait()
@@ -404,10 +395,9 @@
             jax.ShapeDtypeStruct((length, width), BF16),
             pltpu.HBM((count, width), BF16),
             jax.ShapeDtypeStruct(local.shape, F32),
-            jax.ShapeDtypeStruct((2 * length, count), BF16),
         ),
         in_specs=[SMEM] + [VMEM] * len(arrays),
-        out_specs=(anywhere, VMEM, anywhere, VMEM, VMEM),
+        out_specs=(anywhere, VMEM, anywhere, VMEM),
         scratch_shapes=[
             pltpu.VMEM((length, width), F32),
             pltpu.VMEM((length, width), BF16),
@@ -482,6 +472,47 @@
         compiler_params=pltpu.CompilerParams(vmem_limit_bytes=8 << 20),
         name="choose",
     )(source, resident(rows), names, router)
+
+
+def picks(sources, names, length, experts):
+    number = sources.shape[0]
+
+    def kernel(sources_ref, names_ref, *outs):
+        for k, out_ref in enumerate(outs):
+            names = names_ref[pl.ds(sources_ref[k], 1), :][:, : 2 * length]
+            hots = hots_of(names, 2 * length // experts)
+            out_ref[...] = (hots[0] + hots[1]).astype(BF16)
+
+    return pl.pallas_call(
+        kernel,
+        out_shape=[jax.ShapeDtypeStruct((length, 2 * length), BF16)] * number,
+        in_specs=[SMEM, VMEM],
+        out_specs=[VMEM] * number,
+        compiler_params=pltpu.CompilerParams(vmem_limit_bytes=56 << 20),
+        name="picks",
+    )(sources, names)
+
+
+def gates_kernel(source_ref, rows_ref, names_ref, router_ref, weights_ref):
+    length = rows_ref.shape[0]
+    names = names_ref[pl.ds(source_ref[0], 1), :][:, : 2 * length]
+    hots = hots_of(names, 2 * length // router_ref.shape[0])
+    logits = lax.dot_general(
+        rows_ref[...], router_ref[...], (((1,), (1,)), ((), ())), preferred_element_type=F32
+    )
+    weights_ref[...] = weights_of(logits, hots)
+
+
+def gates(source, rows, names, router):
+    length = rows.shape[0]
+    return pl.pallas_call(
+        gates_kernel,
+        out_shape=jax.ShapeDtypeStruct((2 * length, 2 * length), BF16),
+        in_specs=[SMEM] + [VMEM] * 3,
+        out_specs=VMEM,
+        compiler_params=pltpu.CompilerParams(vmem_limit_bytes=56 << 20),
+        name="gates",
+    )(source, rows, names, router)
 
 
 def weighed(parts, weights):
@@ -733,9 +764,11 @@
     sums, from_inputs, fade, keep = scan_local(
         scan_input, state_maps, step_size, step_decay, tokens
     )
-    mixed, normed, send, final_state, weights = mix(
+    own = jnp.asarray(place)[None]
+    (own_pick,) = picks(own, asked, tokens.shape[0], router_weight.shape[1])
+    mixed, normed, send, final_state = mix(
         state_holder, queries, keys_values, got, known, sums, from_inputs, fade, keep, state_maps,
-        norm_gain[None, :], ask[0], router,
+        norm_gain[None, :], own_pick,
     )
     up_local, down_local = up_weight[0], down_weight[0]
 
@@ -745,9 +778,11 @@
     far_rows += [move(far_rows[0], turn, 0) for turn in range(1, near)]
     far_in, far_weights = [], []
     for turn in range(near):
-        chosen, gates = choose(source_of(turn)[None], far_rows[turn], asked, router)
+        chosen, far_gates = choose(source_of(turn)[None], far_rows[turn], asked, router)
         far_in.append(swap_rows(chosen))
-        far_weights.append(gates)
+        far_weights.append(far_gates)
+
+    weights = gates(own, normed, asked, router)
 
     def experts_on(rows):
         return list(apply_expert(rows, up_local, down_local))

time: 242 us -> 243 us (level)
  the two profiles are of different devices: /device:TPU:13 before, /device:TPU:11 now
where the time goes in v6:
time: 243 us; the launch traced here: 241 us
  waiting for transfers between devices  121 us (50%)
  Pallas kernels  57.5 us (24%)
  starting transfers between devices  52.5 us (22%)
  local copies, waits for them, and re-layouts  6.82 us (3%)
  between operations  2.9 us (1%)
    ppermute x6, waiting for transfers between devices, move(): return lax.ppermute(rows, 'dp', route(turn, side))  78 us
    all_to_all x6, starting transfers between devices, swap_rows(): lax.all_to_all(blocks, 'expert', split_axis=0, concat_axis=0, tiled=True)  31.6 us
    pallas_call x2, Pallas kernels, apply_expert(): pl.pallas_call(functools.partial(expert_kernel, count, ups, downs), out_s...  27.6 us
    all_to_all x1, waiting for transfers between devices, local(): got = lax.all_to_all(packed, 'dp', split_axis=0, concat_axis=0, tiled=True)  23.7 us
    all_to_all x6, waiting for transfers between devices, swap_rows(): lax.all_to_all(blocks, 'expert', split_axis=0, concat_axis=0, tiled=True)  16.9 us
    ppermute x6, starting transfers between devices, move(): return lax.ppermute(rows, 'dp', route(turn, side))  11.5 us
    pallas_call x1, Pallas kernels, mix(): pl.pallas_call(mix_kernel, out_shape=(pltpu.HBM((length, width), BF16), j...  7.73 us
    unnamed x19, local copies, waits for them, and re-layouts  6.82 us
  transfers between devices with their start and end apart: 14, of which 10 were waited for; matrix products, arithmetic and copies ran while one was open for 1% of the time, Pallas kernels for 18%

profile of v6, /device:TPU:11, one launch (start us, length us, event | category | flops | bytes accessed | tf_op | source)
XLA Modules:
  0.0 241.4 jit_solution(335673649677113296)
XLA Ops:
  0.6 0.0 copy-start.3
  2.0 1.5 plan.1
  3.5 4.8 %all-to-all-start = ((s32[4,1,256]{2,1,0:T(1,128)}), s32[4,1,256]{2,1,0:T(1,128)S(1)}, u32[]{:S(2)}, u32[]{:S(2)}) async-start(s32[4,1,256]{2,1,0:T(1,128)} %get-tuple-element.22), calls=%async_computation | async-start | bytes 8192 | tf_op jit(solution)/shard_map/all_to_all | solution.py:753
  8.2 1.2 convert_bitcast_fusion
  9.5 2.0 all-to-all-done
  11.5 0.0 copy-start.5
  11.5 0.0 copy-start
  11.5 1.0 copy-done
  12.5 2.3 pack.1
  14.9 4.7 %all-to-all-start.1 = ((bf16[4,96,2048]{2,1,0:T(8,128)(2,1)}), bf16[4,96,2048]{2,1,0:T(8,128)(2,1)S(1)}, u32[]{:S(2)}, u32[]{:S(2)}) async-start(bf16[4,96,2048]{2,1,0:T(8,128)(2,1)} %pack.1), calls=%async_computation.1 | async-start | bytes 3145728 | tf_op jit(solution)/shard_map/all_to_all | solution.py:761
  20.2 1.4 copy.24.maps_ref
  21.6 4.7 %scan_local.1 = (f32[64,4096]{1,0:T(8,128)}, f32[512,128]{1,0:T(8,128)}, f32[64,64]{1,0:T(8,128)}, f32[1,64]{1,0:T(1,128)}) custom-call(bf16[64,4096]{1,0:T(8,128)(2,1)} %x_ref.1, f32[64,32]{1,0:T(8,128)} %copy.24.maps_ref, f32[64,64]{1,0:T(8,128)} %steps_ref.1, f32[64,64]{1,0:T(8,128)} %decays_ref.1, bf16[64,4096]{1,0:T(8,128)(2,1)} %tokens_ref.1), custom_call_target="tpu_custom_call" | custom-call | tf_op jit(solution)/shard_map/scan_local/pallas_call | solution.py:243
  26.4 0.0 copy-done.5
  26.4 1.5 picks.1.pick_ref
  27.9 23.7 %all-to-all-done.1.got_ref = bf16[4,96,2048]{2,1,0:T(8,128)(2,1)S(1)} async-done(((bf16[4,96,2048]{2,1,0:T(8,128)(2,1)}), bf16[4,96,2048]{2,1,0:T(8,128)(2,1)S(1)}, u32[]{:S(2)}, u32[]{:S(2)}) %all-to-all-start.1) | async-done | bytes 1572896 | tf_op jit(solution)/shard_map/all_to_all | solution.py:761
  51.5 7.7 %mix.1 = (bf16[64,4096]{1,0:T(8,128)(2,1)}, bf16[64,4096]{1,0:T(8,128)(2,1)}, bf16[128,4096]{1,0:T(8,128)(2,1)}, f32[512,128]{1,0:T(8,128)}) custom-call(s32[1]{0:T(128)S(6)} %copy.33.owner_ref, bf16[64,4096]{1,0:T(8,128)(2,1)} %q_ref.1, bf16[64,2048]{1,0:T(8,128)(2,1)} %kv_ref.1, bf16[4,96,2048]{2,1,0:T(8,128)(2,1)S(1)} %all-to-all-done.1.got_ref, ...), custom_call_target="tpu_custom_call" | custom-call | tf_op jit(solution)/shard_map/mix/pallas_call | solution.py:391
  59.3 3.1 %collective-permute-start.1 = (bf16[64,4096]{1,0:T(8,128)(2,1)}, bf16[64,4096]{1,0:T(8,128)(2,1)S(1)}, u32[]{:S(2)}, u32[]{:S(2)}) collective-permute-start(bf16[64,4096]{1,0:T(8,128)(2,1)} %get-tuple-element.29.rows_ref), channel_id=1, source_target_pairs={{0,16},{8,24},{16,0},{24,8},{1,17},{9,25},{17,1},{25,9},{2,18},{10... | collective-permute-start | bytes 1572872 | tf_op jit(solution)/shard_map/ppermute | solution.py:743
  62.3 7.1 %all-to-all-start.2 = ((bf16[8,16,4096]{2,1,0:T(8,128)(2,1)}), bf16[8,16,4096]{2,1,0:T(8,128)(2,1)S(1)}, u32[]{:S(2)}, u32[]{:S(2)}) async-start(bf16[8,16,4096]{2,1,0:T(8,128)(2,1)} %bitcast.49), calls=%async_computation.2 | async-start | bytes 2097152 | tf_op jit(solution)/shard_map/all_to_all | solution.py:747
  69.4 14.8 %collective-permute-done.1.rows_ref = bf16[64,4096]{1,0:T(8,128)(2,1)S(1)} collective-permute-done((bf16[64,4096]{1,0:T(8,128)(2,1)}, bf16[64,4096]{1,0:T(8,128)(2,1)S(1)}, u32[]{:S(2)}, u32[]{:S(2)}) %collective-permute-start.1) | collective-permute-done | bytes 524320 | tf_op jit(solution)/shard_map/ppermute | solution.py:743
  84.2 3.1 %collective-permute-start.2 = (bf16[64,4096]{1,0:T(8,128)(2,1)S(1)}, bf16[64,4096]{1,0:T(8,128)(2,1)S(1)}, u32[]{:S(2)}, u32[]{:S(2)}) collective-permute-start(bf16[64,4096]{1,0:T(8,128)(2,1)S(1)} %collective-permute-done.1.rows_ref), channel_id=1, source_target_pairs={{0,8},{8,0},{16,24},{24,16},{1,9},{9,1},{17,25},{25,17},{2,10},{10... | collective-permute-start | bytes 1572872 | tf_op jit(solution)/shard_map/ppermute | solution.py:743
  87.3 11.8 %collective-permute-done.2.rows_ref = bf16[64,4096]{1,0:T(8,128)(2,1)S(1)} collective-permute-done((bf16[64,4096]{1,0:T(8,128)(2,1)S(1)}, bf16[64,4096]{1,0:T(8,128)(2,1)S(1)}, u32[]{:S(2)}, u32[]{:S(2)}) %collective-permute-start.2) | collective-permute-done | bytes 524320 | tf_op jit(solution)/shard_map/ppermute | solution.py:743
  99.1 0.0 copy-done.3
  99.1 0.0 copy-start.6
  99.1 0.7 copy-done.6
  99.8 1.8 choose.2
  101.6 0.0 all-to-all-done.2
  101.6 4.9 %all-to-all-start.3 = ((bf16[8,16,4096]{2,1,0:T(8,128)(2,1)}), bf16[8,16,4096]{2,1,0:T(8,128)(2,1)S(1)}, u32[]{:S(2)}, u32[]{:S(2)}) async-start(bf16[8,16,4096]{2,1,0:T(8,128)(2,1)} %bitcast.50), calls=%async_computation.3 | async-start | bytes 2097152 | tf_op jit(solution)/shard_map/all_to_all | solution.py:747
  106.5 1.5 collective-permute-start
  108.0 0.0 copy-start.7
  108.0 0.7 copy-done.7
  108.7 1.8 choose.3
  110.5 10.0 %all-to-all-done.3 = bf16[8,16,4096]{2,1,0:T(8,128)(2,1)S(1)} async-done(((bf16[8,16,4096]{2,1,0:T(8,128)(2,1)}), bf16[8,16,4096]{2,1,0:T(8,128)(2,1)S(1)}, u32[]{:S(2)}, u32[]{:S(2)}) %all-to-all-start.3) | async-done | bytes 1048608 | tf_op jit(solution)/shard_map/all_to_all | solution.py:747
  120.5 4.9 %all-to-all-start.5 = ((bf16[8,16,4096]{2,1,0:T(8,128)(2,1)}), bf16[8,16,4096]{2,1,0:T(8,128)(2,1)S(1)}, u32[]{:S(2)}, u32[]{:S(2)}) async-start(bf16[8,16,4096]{2,1,0:T(8,128)(2,1)} %bitcast.53), calls=%async_computation.5 | async-start | bytes 2097152 | tf_op jit(solution)/shard_map/all_to_all | solution.py:747
  125.4 5.6 %collective-permute-done.refs_0_ = bf16[128,4096]{1,0:T(8,128)(2,1)} collective-permute-done((bf16[128,4096]{1,0:T(8,128)(2,1)S(1)}, bf16[128,4096]{1,0:T(8,128)(2,1)}, u32[]{:S(2)}, u32[]{:S(2)}) %collective-permute-start) | collective-permute-done | bytes 1048608 | tf_op jit(solution)/shard_map/ppermute | solution.py:743
  131.0 14.4 %expert.2 = (bf16[128,4096]{1,0:T(8,128)(2,1)}, bf16[128,4096]{1,0:T(8,128)(2,1)}) custom-call(bf16[128,4096]{1,0:T(8,128)(2,1)} %collective-permute-done.refs_0_, bf16[128,4096]{1,0:T(8,128)(2,1)S(1)} %bitcast.31, bf16[4096,1792]{1,0:T(8,128)(2,1)} %bitcast.45, bf16[1792,4096]{1,0:T(8,128)(2,1)} %bitcast.47), custom_call_target="tpu_custom_call" | custom-call | flops 7516192768 | bytes 33554432 | tf_op jit(solution)/shard_map/expert/pallas_call | solution.py:683
  145.4 0.0 all-to-all-done.5
  145.4 5.1 %all-to-all-start.4 = ((bf16[8,16,4096]{2,1,0:T(8,128)(2,1)}), bf16[8,16,4096]{2,1,0:T(8,128)(2,1)S(1)}, u32[]{:S(2)}, u32[]{:S(2)}) async-start(bf16[8,16,4096]{2,1,0:T(8,128)(2,1)} %bitcast.52), calls=%async_computation.4 | async-start | bytes 2097152 | tf_op jit(solution)/shard_map/all_to_all | solution.py:747
  150.5 1.5 collective-permute-start.3
  151.9 13.2 %expert.3 = (bf16[128,4096]{1,0:T(8,128)(2,1)}, bf16[128,4096]{1,0:T(8,128)(2,1)}) custom-call(bf16[128,4096]{1,0:T(8,128)(2,1)S(1)} %bitcast.30, bf16[128,4096]{1,0:T(8,128)(2,1)S(1)} %bitcast.33, bf16[4096,1792]{1,0:T(8,128)(2,1)} %bitcast.46, bf16[1792,4096]{1,0:T(8,128)(2,1)} %bitcast.48), custom_call_target="tpu_custom_call" | custom-call | flops 7516192768 | bytes 33554432 | tf_op jit(solution)/shard_map/expert/pallas_call | solution.py:683
  165.2 0.0 all-to-all-done.4
  165.2 0.0 copy-start.1
  165.2 1.0 copy-done.1
  166.2 4.5 %all-to-all-start.7 = ((bf16[8,16,4096]{2,1,0:T(8,128)(2,1)}), bf16[8,16,4096]{2,1,0:T(8,128)(2,1)S(1)}, u32[]{:S(2)}, u32[]{:S(2)}) async-start(bf16[8,16,4096]{2,1,0:T(8,128)(2,1)} %bitcast.51), calls=%async_computation.7 | async-start | bytes 2097152 | tf_op jit(solution)/shard_map/all_to_all | solution.py:747
  170.6 0.0 copy-start.2
  170.6 1.2 copy-done.2
  171.9 1.2 combine_keep.1
  173.1 2.0 collective-permute-done.3.refs_1_
  175.1 2.4 %shard_map.194 = bf16[128,4096]{1,0:T(8,128)(2,1)} custom-call(bf16[128,4096]{1,0:T(8,128)(2,1)S(1)} %get-tuple-element.35.refs_0_, bf16[128,4096]{1,0:T(8,128)(2,1)} %collective-permute-done.3.refs_1_), custom_call_target="tpu_custom_call" | custom-call | flops 3145728 | bytes 3145728 | tf_op jit(solution)/shard_map/pallas_call | solution.py:430
  177.5 6.9 %all-to-all-done.7 = bf16[8,16,4096]{2,1,0:T(8,128)(2,1)S(1)} async-done(((bf16[8,16,4096]{2,1,0:T(8,128)(2,1)}), bf16[8,16,4096]{2,1,0:T(8,128)(2,1)S(1)}, u32[]{:S(2)}, u32[]{:S(2)}) %all-to-all-start.7) | async-done | bytes 1048608 | tf_op jit(solution)/shard_map/all_to_all | solution.py:747
  184.4 5.0 %all-to-all-start.6 = ((bf16[8,16,4096]{2,1,0:T(8,128)(2,1)}), bf16[8,16,4096]{2,1,0:T(8,128)(2,1)S(1)}, u32[]{:S(2)}, u32[]{:S(2)}) async-start(bf16[8,16,4096]{2,1,0:T(8,128)(2,1)} %bitcast.16), calls=%async_computation.6 | async-start | bytes 2097152 | tf_op jit(solution)/shard_map/all_to_all | solution.py:747
  189.5 0.4 shard_map.195
  189.9 1.1 collective-permute-start.4
  191.0 1.3 collective-permute-start.5
  192.3 2.2 gates.1.refs_1_
  194.6 30.5 %collective-permute-done.4.refs_2_ = bf16[64,4096]{1,0:T(8,128)(2,1)S(1)} collective-permute-done((bf16[64,4096]{1,0:T(8,128)(2,1)S(1)}, bf16[64,4096]{1,0:T(8,128)(2,1)S(1)}, u32[]{:S(2)}, u32[]{:S(2)}) %collective-permute-start.4) | collective-permute-done | bytes 524320 | tf_op jit(solution)/shard_map/ppermute | solution.py:743
  225.1 13.3 %collective-permute-done.5.refs_3_ = bf16[64,4096]{1,0:T(8,128)(2,1)S(1)} collective-permute-done((bf16[64,4096]{1,0:T(8,128)(2,1)S(1)}, bf16[64,4096]{1,0:T(8,128)(2,1)S(1)}, u32[]{:S(2)}, u32[]{:S(2)}) %collective-permute-start.5) | collective-permute-done | bytes 524320 | tf_op jit(solution)/shard_map/ppermute | solution.py:743
  238.4 0.0 all-to-all-done.6
  238.4 0.0 copy-start.4
  238.4 0.8 copy-done.4
  239.1 2.1 shard_map.196
  (3 shorter events, 0.0 us)
Async XLA Ops:
  0.6 98.5 %copy-start.3 = (bf16[4096,8]{0,1:T(8,128)(2,1)S(1)}, bf16[4096,8]{0,1:T(8,128)(2,1)}, u32[]{:S(2)}) copy-start(bf16[4096,8]{0,1:T(8,128)(2,1)} %param.34) | copy-start | bytes 196612
  3.5 8.0 %all-to-all-start = ((s32[4,1,256]{2,1,0:T(1,128)}), s32[4,1,256]{2,1,0:T(1,128)S(1)}, u32[]{:S(2)}, u32[]{:S(2)}) async-start(s32[4,1,256]{2,1,0:T(1,128)} %get-tuple-element.22), calls=%async_computation | async-start | bytes 8192 | tf_op jit(solution)/shard_map/all_to_all | solution.py:753
  11.5 14.9 %copy-start.5 = (s32[4,1,256]{2,0,1:T(4,128)}, s32[4,1,256]{2,0,1:T(4,128)S(1)}, u32[]{:S(2)}) copy-start(s32[4,1,256]{2,0,1:T(4,128)S(1)} %copy.31) | copy-start | bytes 12292
  11.5 1.0 copy-start
  14.9 36.7 %all-to-all-start.1 = ((bf16[4,96,2048]{2,1,0:T(8,128)(2,1)}), bf16[4,96,2048]{2,1,0:T(8,128)(2,1)S(1)}, u32[]{:S(2)}, u32[]{:S(2)}) async-start(bf16[4,96,2048]{2,1,0:T(8,128)(2,1)} %pack.1), calls=%async_computation.1 | async-start | bytes 3145728 | tf_op jit(solution)/shard_map/all_to_all | solution.py:761
  59.3 25.0 %collective-permute-start.1 = (bf16[64,4096]{1,0:T(8,128)(2,1)}, bf16[64,4096]{1,0:T(8,128)(2,1)S(1)}, u32[]{:S(2)}, u32[]{:S(2)}) collective-permute-start(bf16[64,4096]{1,0:T(8,128)(2,1)} %get-tuple-element.29.rows_ref), channel_id=1, source_target_pairs={{0,16},{8,24},{16,0},{24,8},{1,17},{9,25},{17,1},{25,9},{2,18},{10... | collective-permute-start | bytes 1572872 | tf_op jit(solution)/shard_map/ppermute | solution.py:743
  62.3 39.3 %all-to-all-start.2 = ((bf16[8,16,4096]{2,1,0:T(8,128)(2,1)}), bf16[8,16,4096]{2,1,0:T(8,128)(2,1)S(1)}, u32[]{:S(2)}, u32[]{:S(2)}) async-start(bf16[8,16,4096]{2,1,0:T(8,128)(2,1)} %bitcast.49), calls=%async_computation.2 | async-start | bytes 2097152 | tf_op jit(solution)/shard_map/all_to_all | solution.py:747
  84.2 14.9 %collective-permute-start.2 = (bf16[64,4096]{1,0:T(8,128)(2,1)S(1)}, bf16[64,4096]{1,0:T(8,128)(2,1)S(1)}, u32[]{:S(2)}, u32[]{:S(2)}) collective-permute-start(bf16[64,4096]{1,0:T(8,128)(2,1)S(1)} %collective-permute-done.1.rows_ref), channel_id=1, source_target_pairs={{0,8},{8,0},{16,24},{24,16},{1,9},{9,1},{17,25},{25,17},{2,10},{10... | collective-permute-start | bytes 1572872 | tf_op jit(solution)/shard_map/ppermute | solution.py:743
  99.1 0.7 copy-start.6
  101.6 18.8 %all-to-all-start.3 = ((bf16[8,16,4096]{2,1,0:T(8,128)(2,1)}), bf16[8,16,4096]{2,1,0:T(8,128)(2,1)S(1)}, u32[]{:S(2)}, u32[]{:S(2)}) async-start(bf16[8,16,4096]{2,1,0:T(8,128)(2,1)} %bitcast.50), calls=%async_computation.3 | async-start | bytes 2097152 | tf_op jit(solution)/shard_map/all_to_all | solution.py:747
  106.5 24.4 %collective-permute-start = (bf16[128,4096]{1,0:T(8,128)(2,1)S(1)}, bf16[128,4096]{1,0:T(8,128)(2,1)}, u32[]{:S(2)}, u32[]{:S(2)}) collective-permute-start(bf16[128,4096]{1,0:T(8,128)(2,1)S(1)} %bitcast.29), channel_id=1, source_target_pairs={{0,8},{8,0},{16,24},{24,16},{1,9},{9,1},{17,25},{25,17},{2,10},{10... | collective-permute-start | bytes 3145736 | tf_op jit(solution)/shard_map/ppermute | solution.py:743
  108.0 0.7 copy-start.7
  120.5 24.9 %all-to-all-start.5 = ((bf16[8,16,4096]{2,1,0:T(8,128)(2,1)}), bf16[8,16,4096]{2,1,0:T(8,128)(2,1)S(1)}, u32[]{:S(2)}, u32[]{:S(2)}) async-start(bf16[8,16,4096]{2,1,0:T(8,128)(2,1)} %bitcast.53), calls=%async_computation.5 | async-start | bytes 2097152 | tf_op jit(solution)/shard_map/all_to_all | solution.py:747
  145.4 19.8 %all-to-all-start.4 = ((bf16[8,16,4096]{2,1,0:T(8,128)(2,1)}), bf16[8,16,4096]{2,1,0:T(8,128)(2,1)S(1)}, u32[]{:S(2)}, u32[]{:S(2)}) async-start(bf16[8,16,4096]{2,1,0:T(8,128)(2,1)} %bitcast.52), calls=%async_computation.4 | async-start | bytes 2097152 | tf_op jit(solution)/shard_map/all_to_all | solution.py:747
  150.5 24.6 %collective-permute-start.3 = (bf16[128,4096]{1,0:T(8,128)(2,1)}, bf16[128,4096]{1,0:T(8,128)(2,1)}, u32[]{:S(2)}, u32[]{:S(2)}) collective-permute-start(bf16[128,4096]{1,0:T(8,128)(2,1)} %get-tuple-element.36), channel_id=1, source_target_pairs={{0,8},{8,0},{16,24},{24,16},{1,9},{9,1},{17,25},{25,17},{2,10},{10... | collective-permute-start | bytes 3145736 | tf_op jit(solution)/shard_map/ppermute | solution.py:743
  165.2 1.0 copy-start.1
  166.2 18.3 %all-to-all-start.7 = ((bf16[8,16,4096]{2,1,0:T(8,128)(2,1)}), bf16[8,16,4096]{2,1,0:T(8,128)(2,1)S(1)}, u32[]{:S(2)}, u32[]{:S(2)}) async-start(bf16[8,16,4096]{2,1,0:T(8,128)(2,1)} %bitcast.51), calls=%async_computation.7 | async-start | bytes 2097152 | tf_op jit(solution)/shard_map/all_to_all | solution.py:747
  170.6 1.2 copy-start.2
  184.4 53.9 %all-to-all-start.6 = ((bf16[8,16,4096]{2,1,0:T(8,128)(2,1)}), bf16[8,16,4096]{2,1,0:T(8,128)(2,1)S(1)}, u32[]{:S(2)}, u32[]{:S(2)}) async-start(bf16[8,16,4096]{2,1,0:T(8,128)(2,1)} %bitcast.16), calls=%async_computation.6 | async-start | bytes 2097152 | tf_op jit(solution)/shard_map/all_to_all | solution.py:747
  189.9 35.2 %collective-permute-start.4 = (bf16[64,4096]{1,0:T(8,128)(2,1)S(1)}, bf16[64,4096]{1,0:T(8,128)(2,1)S(1)}, u32[]{:S(2)}, u32[]{:S(2)}) collective-permute-start(bf16[64,4096]{1,0:T(8,128)(2,1)S(1)} %shard_map.195), channel_id=1, source_target_pairs={{0,16},{8,24},{16,0},{24,8},{1,17},{9,25},{17,1},{25,9},{2,18},{10... | collective-permute-start | bytes 1572872 | tf_op jit(solution)/shard_map/ppermute | solution.py:743
  191.0 47.4 %collective-permute-start.5 = (bf16[64,4096]{1,0:T(8,128)(2,1)S(1)}, bf16[64,4096]{1,0:T(8,128)(2,1)S(1)}, u32[]{:S(2)}, u32[]{:S(2)}) collective-permute-start(bf16[64,4096]{1,0:T(8,128)(2,1)S(1)} %get-tuple-element.39), channel_id=1, source_target_pairs={{0,24},{8,16},{16,8},{24,0},{1,25},{9,17},{17,9},{25,1},{2,26},{10... | collective-permute-start | bytes 1572872 | tf_op jit(solution)/shard_map/ppermute | solution.py:743
  238.4 0.8 copy-start.4
